TPU v7x, 256 devices: a whole 4x4x8 slice. The times are simulated.
256 devices in a mesh: dp: 32 (over y, x, core), tsp: 8 (over z).
Axes of the slice: x: 4, y: 4, z: 8, core: 2. Of those that a mesh axis runs over, the one named last changes fastest.
Arguments:
- tokens: bfloat16 [65536, 8192], P('dp', 'tsp'), may hold values from -6 to 6
- cotangent: bfloat16 [65536, 1024], P('dp', 'tsp'), may hold values from -6 to 6
- frozen_key_weight: bfloat16 [8192, 1024], P('tsp'), may hold values from -0.1875 to 0.1875
- adapter_down_weight: bfloat16 [64, 64, 8192], P('dp', None, 'tsp'), may hold values from -0.0625 to 0.0625
- adapter_up_weight: bfloat16 [64, 64, 1024], P('dp', None, 'tsp'), may hold values from -0.1875 to 0.1875
- adapter_place_table: int32 [64], replicated, may hold values from 0 to 63, as said below
- segment_adapter: int32 [512], P('dp'), may hold values from 0 to 63, as said below
- segment_live_count: int32 [512], P('dp'), may hold values from 1 to 128, as said below
Outputs:
- token_gradient: bfloat16 [65536, 8192], P('dp', 'tsp')
- down_grad: float32 [64, 64, 8192], P('dp', None, 'tsp')
- up_grad: float32 [64, 64, 1024], P('dp', None, 'tsp')
Inputs may be any that keep to these rules, and one draw needn't show every extreme that they name: A permutation: adapter a is held at place adapter_place_table[a], that is by the dp index adapter_place_table[a] // 2 as its entry adapter_place_table[a] % 2; the adapters' arrays and gradients are indexed by place. `segment_adapter`: the 16 segments of one dp index name at most one adapter held by any one dp index; an adapter may be named by several of them. `segment_live_count`: the live rows stand at the start of each segment; on every dp index some segment is full.
All inputs are finite; a program needn't handle non-finite values.
Results may differ from a plain program's by a relative error of at most 0.0034.
Values may be sent and summed in bfloat16 or wider, within the bound.
A program may use at most 128 MiB of HBM per device.

v0:
```python
import jax
import jax.numpy as jnp
from jax import lax
from jax.sharding import PartitionSpec as P

ADAPTER_SCALE = 2.0


def lookup(idents, mapping):
    matches = idents[:, None] == jnp.arange(mapping.shape[0], dtype=jnp.int32)[None, :]
    return jnp.sum(jnp.where(matches, mapping[None, :], 0), axis=1)


def on_device(
    tokens,
    cotangent,
    frozen_key_weight,
    adapter_down_weight,
    adapter_up_weight,
    adapter_place_table,
    segment_adapter,
    segment_live_count,
):
    dp_count = lax.axis_size("dp")
    places_per_device = adapter_down_weight.shape[0]
    rank_of_adapter = adapter_down_weight.shape[1]
    width_per_device = tokens.shape[1]
    key_dev = cotangent.shape[1]
    segments_per_device = segment_adapter.shape[0]
    segment_token_rows = tokens.shape[0] // segments_per_device
    adapter_places = lookup(segment_adapter, adapter_place_table)
    seg_owner = adapter_places // places_per_device
    seg_entry = adapter_places % places_per_device
    owner_hit = seg_owner[:, None] == jnp.arange(dp_count, dtype=jnp.int32)[None, :]
    wanted = jnp.max(jnp.where(owner_hit, seg_entry[:, None], -1), axis=0)
    incoming = lax.all_to_all(wanted[:, None], "dp", split_axis=0, concat_axis=0, tiled=True)[:, 0]
    serving_mesh = (
        incoming[:, None] == jnp.arange(places_per_device, dtype=jnp.int32)[None, :]
    ).astype(jnp.bfloat16)
    reply_down = jnp.einsum(
        "ap,phc->ahc", serving_mesh, adapter_down_weight, preferred_element_type=jnp.float32
    ).astype(jnp.bfloat16)
    reply_up = jnp.einsum(
        "hv,vun->hun", serving_mesh, adapter_up_weight, preferred_element_type=jnp.float32
    ).astype(jnp.bfloat16)
    fetched_down, fetched_up = (
        lax.all_to_all(reply_down, "dp", split_axis=0, concat_axis=0, tiled=True),
        lax.all_to_all(reply_up, "dp", split_axis=0, concat_axis=0, tiled=True),
    )
    picker = owner_hit.astype(jnp.bfloat16)
    segment_down_weight = jnp.einsum(
        "go,ord->grd", picker, fetched_down, preferred_element_type=jnp.float32
    ).astype(jnp.bfloat16)
    segment_up_weight = jnp.einsum(
        "go,ork->grk", picker, fetched_up, preferred_element_type=jnp.float32
    ).astype(jnp.bfloat16)
    seg_tokens = tokens.reshape(segments_per_device, segment_token_rows, width_per_device)
    seg_cotangent = cotangent.reshape(segments_per_device, segment_token_rows, key_dev)
    live_rows = (
        jnp.arange(segment_token_rows, dtype=jnp.int32)[None, :] < segment_live_count[:, None]
    ).astype(jnp.float32)
    partial_terms = jnp.concatenate(
        [
            jnp.einsum(
                "gtd,grd->gtr", seg_tokens, segment_down_weight, preferred_element_type=jnp.float32
            ),
            jnp.einsum(
                "gtk,grk->gtr", seg_cotangent, segment_up_weight, preferred_element_type=jnp.float32
            ),
        ],
        axis=2,
    )
    summed = lax.psum(partial_terms, "tsp")
    reduced_rows = (summed[:, :, :rank_of_adapter] * live_rows[:, :, None]).astype(jnp.bfloat16)
    gathered_weights = (summed[:, :, rank_of_adapter:] * live_rows[:, :, None]).astype(jnp.bfloat16)
    frozen_output = lax.dot_general(
        lax.all_gather(cotangent, "tsp", axis=1, tiled=True),
        frozen_key_weight,
        (((1,), (1,)), ((), ())),
        preferred_element_type=jnp.float32,
    )
    adapter_output = jnp.einsum(
        "wks,wsx->wkx", gathered_weights, segment_down_weight, preferred_element_type=jnp.float32
    )
    token_gradient = (
        frozen_output.reshape(segments_per_device, segment_token_rows, width_per_device)
        + ADAPTER_SCALE * adapter_output
    ) * live_rows[:, :, None]
    token_gradient = token_gradient.reshape(
        segments_per_device * segment_token_rows, width_per_device
    ).astype(jnp.bfloat16)
    gradient_scale = ADAPTER_SCALE / segment_token_rows
    segment_down_gradient = jnp.einsum(
        "upf,upb->ufb", gathered_weights, seg_tokens, preferred_element_type=jnp.float32
    )
    segment_up_gradient = jnp.einsum(
        "ija,ijn->ian", reduced_rows, seg_cotangent, preferred_element_type=jnp.float32
    )
    picker_f = owner_hit.astype(jnp.float32)
    slot_dgrad = (
        jnp.einsum("go,grd->ord", picker_f, segment_down_gradient, precision=lax.Precision.HIGHEST)
        * gradient_scale
    )
    slot_ugrad = (
        jnp.einsum("go,grk->ork", picker_f, segment_up_gradient, precision=lax.Precision.HIGHEST)
        * gradient_scale
    )
    slot_match = (wanted[:, None] == jnp.arange(places_per_device, dtype=jnp.int32)[None, :])[
        :, :, None, None
    ]
    dense_down = jnp.where(slot_match, slot_dgrad[:, None], 0.0).reshape(
        dp_count * places_per_device, rank_of_adapter, width_per_device
    )
    dense_up = jnp.where(slot_match, slot_ugrad[:, None], 0.0).reshape(
        dp_count * places_per_device, rank_of_adapter, key_dev
    )
    down_grad, up_grad = (
        lax.psum_scatter(dense_down, "dp", scatter_dimension=0, tiled=True),
        lax.psum_scatter(dense_up, "dp", scatter_dimension=0, tiled=True),
    )
    return (token_gradient, down_grad, up_grad)


def solution(mesh):
    placed = (
        P("dp", "tsp"),
        P("dp", "tsp"),
        P("tsp", None),
        P("dp", None, "tsp"),
        P("dp", None, "tsp"),
        P(),
        P("dp"),
        P("dp"),
    )
    return jax.shard_map(
        on_device,
        mesh=mesh,
        in_specs=placed,
        out_specs=(P("dp", "tsp"), P("dp", None, "tsp"), P("dp", None, "tsp")),
        check_vma=False,
    )
```

profile of v0, /device:TPU:1, one launch (start us, length us, event | category | flops | bytes accessed | tf_op | source)
XLA Modules:
  0.0 470.9 jit_solution(15498572598505192805)
XLA Ops:
  7.2 1.0 select_reduce_fusion.1
  8.4 15.3 %all_to_all.19 = s32[32,1,1]{2,1,0:T(1,128)S(1)} all-to-all(s32[32,1,1]{2,1,0:T(1,128)S(1)} %copy.57), channel_id=1, replica_groups=mesh['dp'=32,'tsp'=8] {'dp'}, dimensions={0} | all-to-all | bytes 256 | tf_op jit(solution)/shard_map/all_to_all | solution.py:36
  23.7 0.7 reduce
  24.4 1.1 convolution_convert_fusion.1
  25.5 1.0 copy.63
  26.5 4.2 all-to-all-start.2
  30.7 2.3 convolution_convert_fusion
  33.0 4.3 copy.59
  37.3 4.9 %all-to-all-done.2 = bf16[32,64,128]{2,1,0:T(8,128)(2,1)S(1)} async-done(((bf16[32,64,128]{2,1,0:T(8,128)(2,1)}), bf16[32,64,128]{2,1,0:T(8,128)(2,1)S(1)}, u32[]{:S(2)}, u32[]{:S(2)}) %all-to-all-start.2) | async-done | bytes 524320 | tf_op jit(solution)/shard_map/all_to_all | solution.py:48
  42.3 4.8 %all-to-all-start.1 = ((bf16[32,64,1024]{2,1,0:T(8,128)(2,1)}), bf16[32,64,1024]{2,1,0:T(8,128)(2,1)}, u32[]{:S(2)}, u32[]{:S(2)}) async-start(bf16[32,64,1024]{2,1,0:T(8,128)(2,1)} %copy.59), calls=%async_computation.1 | async-start | bytes 8388608 | tf_op jit(solution)/shard_map/all_to_all | solution.py:47
  47.3 0.4 convolution_convert_fusion.2
  47.8 0.5 convolution_bitcast_fusion
  48.2 49.6 %all-to-all-done.1 = bf16[32,64,1024]{2,1,0:T(8,128)(2,1)} async-done(((bf16[32,64,1024]{2,1,0:T(8,128)(2,1)}), bf16[32,64,1024]{2,1,0:T(8,128)(2,1)}, u32[]{:S(2)}, u32[]{:S(2)}) %all-to-all-start.1) | async-done | bytes 4194336 | tf_op jit(solution)/shard_map/all_to_all | solution.py:47
  97.8 6.9 %fusion.6 = bf16[16,64,1024]{2,0,1:T(8,128)(2,1)S(1)} fusion(bf16[32,64,1024]{2,1,0:T(8,128)(2,1)} %all-to-all-done.1, s32[16]{0:T(128)S(1)} %get-tuple-element.3), kind=kOutput, calls=%fused_computation.9 | convolution fusion | flops 68157952 | bytes 6291520 | tf_op jit(solution)/shard_map/go,ord->grd/dot_general | solution.py:51
  104.7 1.3 copy-done.1
  106.0 1.7 fusion.12
  107.8 1.1 pad_maximum_fusion
  108.9 0.7 all-gather.2.cloned.1.call-update
  110.0 71.8 %all-reduce.2.cloned.1.call-done = f32[16,128,128]{1,2,0:T(8,128)} async-done(((f32[16,128,128]{1,2,0:T(8,128)}), f32[16,128,128]{1,2,0:T(8,128)}) %all-reduce.2.cloned.1.call-update) | async-done | bytes 1048592 | tf_op jit(solution)/shard_map/psum | solution.py:73
  181.7 1.3 fusion.19
  183.0 0.9 convolution_multiply_fusion
  183.9 0.6 copy.70
  184.6 1.5 bitcast_select_fusion.1
  186.4 2.9 fusion.24
  189.3 6.1 %broadcast_multiply_fusion = f32[32,64,1024]{2,0,1:T(8,128)S(1)} fusion(f32[16,64,1024]{2,1,0:T(8,128)S(1)} %fusion.24, s32[16]{0:T(128)S(1)} %get-tuple-element.3), kind=kOutput, calls=%fused_computation.6 | convolution fusion | flops 404750848 | bytes 12582976 | tf_op jit(solution)/shard_map/go,grd->ord/dot_general | solution.py:101
  195.4 8.1 %copy.68 = f32[32,64,1024]{2,1,0:T(8,128)} copy(f32[32,64,1024]{2,0,1:T(8,128)S(1)} %broadcast_multiply_fusion) | data formatting | bytes 16777216 | tf_op jit(solution)/shard_map/mul | solution.py:101
  203.5 12.6 %bitcast_select_fusion = f32[64,64,1024]{2,1,0:T(8,128)} fusion(f32[32,64,1024]{2,1,0:T(8,128)} %copy.68, pred[64]{0:T(512)(128)(4,1)S(1)} %eq.76), kind=kLoop, calls=%fused_computation | loop fusion | flops 4194304 | bytes 25165888 | tf_op jit(solution)/shard_map/jit(_where)/select_n | solution.py:111
  216.1 29.0 %all-gather.2.cloned.1.call-done = bf16[2048,1024]{1,0:T(8,128)(2,1)} async-done(((bf16[2048,128]{1,0:T(8,128)(2,1)}), bf16[2048,1024]{1,0:T(8,128)(2,1)}) %all-gather.2.cloned.1.call-update) | async-done | bytes 4194320 | tf_op jit(solution)/shard_map/all_gather | solution.py:77
  245.0 6.5 %fusion.42 = f32[2048,1024]{1,0:T(8,128)S(1)} fusion(bf16[2048,1024]{1,0:T(8,128)(2,1)} %all-gather.2.cloned.1.call-done, bf16[1024,1024]{1,0:T(8,128)(2,1)S(1)} %copy-done), kind=kOutput, calls=%fused_computation.53 | convolution fusion | flops 4294967296 | bytes 14680064 | tf_op jit(solution)/shard_map/dot_general | solution.py:76
  251.6 5.2 %multiply_convert_fusion = bf16[16,128,1024]{2,1,0:T(8,128)(2,1)} fusion(f32[16,128,1024]{2,1,0:T(8,128)S(1)} %bitcast.32, f32[16,128]{1,0:T(8,128)S(1)} %fusion.33, bf16[16,64,1024]{2,0,1:T(8,128)(2,1)S(1)} %copy-done.2, f32[16,128,128]{1,2,0:T(8,128)S(1)} %copy-done.6), kind=kOutput, calls=%fused_computation.1 | convolution fusion | flops 277086208 | bytes 15220736 | tf_op jit(solution)/shard_map/wks,wsx->wkx/dot_general | solution.py:82
  256.8 80.1 %reduce-scatter.5.cloned.1.call-done = f32[2,64,128]{2,1,0:T(8,128)} async-done(((f32[64,64,128]{2,1,0:T(8,128)}), f32[2,64,128]{2,1,0:T(8,128)}) %reduce-scatter.5.cloned.1.call-update) | async-done | bytes 65552 | tf_op jit(solution)/shard_map/reduce_scatter | solution.py:119
  336.9 127.4 %reduce-scatter.3.cloned.1.call-done = f32[2,64,1024]{2,1,0:T(8,128)} async-done(((f32[64,64,1024]{2,1,0:T(8,128)}), f32[2,64,1024]{2,1,0:T(8,128)}) %reduce-scatter.3.cloned.1.call-update) | async-done | bytes 524304 | tf_op jit(solution)/shard_map/reduce_scatter | solution.py:118
  (28 shorter events, 1.1 us)
Async XLA Ops:
  7.2 237.9 %copy-start = (bf16[1024,1024]{1,0:T(8,128)(2,1)S(1)}, bf16[1024,1024]{1,0:T(8,128)(2,1)}, u32[]{:S(2)}) copy-start(bf16[1024,1024]{1,0:T(8,128)(2,1)} %param.10) | copy-start | bytes 6291460
  26.5 15.7 %all-to-all-start.2 = ((bf16[32,64,128]{2,1,0:T(8,128)(2,1)}), bf16[32,64,128]{2,1,0:T(8,128)(2,1)S(1)}, u32[]{:S(2)}, u32[]{:S(2)}) async-start(bf16[32,64,128]{2,1,0:T(8,128)(2,1)} %copy.63), calls=%async_computation.2 | async-start | bytes 1048576 | tf_op jit(solution)/shard_map/all_to_all | solution.py:48
  37.3 10.4 %copy-start.4 = (bf16[2048,128]{1,0:T(8,128)(2,1)S(1)}, bf16[2048,128]{1,0:T(8,128)(2,1)}, u32[]{:S(2)}) copy-start(bf16[2048,128]{1,0:T(8,128)(2,1)} %param.9) | copy-start | bytes 1572868
  42.3 55.5 %all-to-all-start.1 = ((bf16[32,64,1024]{2,1,0:T(8,128)(2,1)}), bf16[32,64,1024]{2,1,0:T(8,128)(2,1)}, u32[]{:S(2)}, u32[]{:S(2)}) async-start(bf16[32,64,1024]{2,1,0:T(8,128)(2,1)} %copy.59), calls=%async_computation.1 | async-start | bytes 8388608 | tf_op jit(solution)/shard_map/all_to_all | solution.py:47
  47.1 134.6 %all-reduce.2.cloned.1.call-start = ((), (), s32[]{:S(2)}) async-start(), calls=%async_computation.6 | async-start | bytes 2097152 | tf_op jit(solution)/shard_map/psum | solution.py:73
  97.8 8.2 %copy-start.3 = (bf16[2048,1024]{1,0:T(8,128)(2,1)S(1)}, bf16[2048,1024]{1,0:T(8,128)(2,1)}, u32[]{:S(2)}) copy-start(bf16[2048,1024]{1,0:T(8,128)(2,1)} %param.8) | copy-start | bytes 12582916
  104.7 1.3 copy-start.1
  106.0 3.9 copy-start.7
  106.0 75.7 %copy-start.5 = (bf16[2048,128]{1,0:T(8,128)(2,1)S(1)}, bf16[2048,128]{1,0:T(8,128)(2,1)}, u32[]{:S(2)}) copy-start(bf16[2048,128]{1,0:T(8,128)(2,1)} %param.9) | copy-start | bytes 1572868
  108.9 136.1 %all-gather.2.cloned.1.call-start = ((), (), s32[]{:S(2)}) async-start(), calls=%async_computation.5 | async-start | bytes 4718592 | tf_op jit(solution)/shard_map/all_gather | solution.py:77
  109.6 227.3 %reduce-scatter.5.cloned.1.call-start = ((), (), s32[]{:S(2)}) async-start(), calls=%async_computation.8 | async-start | bytes 2162688 | tf_op jit(solution)/shard_map/reduce_scatter | solution.py:119
  183.0 3.4 copy-start.6
  186.1 278.3 %reduce-scatter.3.cloned.1.call-start = ((), (), s32[]{:S(2)}) async-start(), calls=%async_computation.7 | async-start | bytes 17301504 | tf_op jit(solution)/shard_map/reduce_scatter | solution.py:118
  245.0 6.5 %copy-start.2 = (bf16[16,64,1024]{2,0,1:T(8,128)(2,1)S(1)}, bf16[16,64,1024]{2,0,1:T(8,128)(2,1)}, u32[]{:S(2)}) copy-start(bf16[16,64,1024]{2,0,1:T(8,128)(2,1)} %copy-done.1) | copy-start | bytes 6291460
Sparse Core Ops, SparseCore 0:
  109.0 72.6 all-reduce.1
  183.4 61.5 all-gather.1
  249.5 87.4 reduce-scatter.4
  341.6 122.7 reduce-scatter.2
where the time goes:
time: 472 us; the launch traced here: 471 us
  waiting for transfers between devices  364 us (77%)
  matrix products  35.8 us (8%)
  other arithmetic  17.2 us (4%)
  local copies, waits for them, and re-layouts  15.6 us (3%)
  blocking collectives  15.3 us (3%)
  between operations  13.9 us (3%)
  starting transfers between devices  9.6 us (2%)
    reduce_scatter x1, waiting for transfers between devices, on_device(): lax.psum_scatter(dense_down, 'dp', scatter_dimension=0, tiled=True)  127 us
    reduce_scatter x1, waiting for transfers between devices, on_device(): lax.psum_scatter(dense_up, 'dp', scatter_dimension=0, tiled=True)  80.1 us
    psum x1, waiting for transfers between devices, on_device(): summed = lax.psum(partial_terms, 'tsp')  71.8 us
    all_to_all x1, waiting for transfers between devices, on_device(): lax.all_to_all(reply_down, 'dp', split_axis=0, concat_axis=0, tiled=True)  49.6 us
    all_gather x1, waiting for transfers between devices, on_device(): lax.all_gather(cotangent, 'tsp', axis=1, tiled=True)  29 us
    all_to_all x1, blocking collectives, on_device(): lax.all_to_all(wanted[:, None], 'dp', split_axis=0, concat_axis=0, tiled=...  15.3 us
    select_n x1, other arithmetic, on_device(): jnp.where(slot_match, slot_dgrad[:, None], 0.0)  12.6 us
  transfers between devices with their start and end apart: 6, of which 6 were waited for; matrix products, arithmetic and copies ran while one was open for 11% of the time, Pallas kernels for 0%

commit v1 on v0

v1 whole, which is shorter than its diff:
```python
import jax
import jax.numpy as jnp
from jax import lax
from jax.experimental import pallas as pl
from jax.experimental.pallas import tpu as pltpu
from jax.sharding import PartitionSpec as P

ADAPTER_SCALE = 2.0
MESH = pl.DeviceIdType.MESH
SIDE = 4
RING = 8
HALF = 32
VMEM_LIMIT = 60 * 1024 * 1024


def lookup(idents, mapping):
    matches = idents[:, None] == jnp.arange(mapping.shape[0], dtype=jnp.int32)[None, :]
    return jnp.sum(jnp.where(matches, mapping[None, :], 0), axis=1)


def place_in_plane():
    me = lax.axis_index("dp")
    core = lax.rem(me, 2)
    chip = lax.div(me, 2)
    return me, core, lax.div(chip, SIDE), lax.rem(chip, SIDE)


def side(v):
    return lax.rem(v + 2 * SIDE, SIDE)


def device_of(y, x, core):
    return (side(y) * SIDE + side(x)) * 2 + core


def greet(devices):
    barrier = pltpu.get_barrier_semaphore()
    for device in devices:
        pl.semaphore_signal(barrier, inc=1, device_id=device, device_id_type=MESH)
    pl.semaphore_wait(barrier, len(devices))


def plane_neighbours():
    me, core, y, x = place_in_plane()
    z = lax.axis_index("tsp")
    return [
        (me + 1 - 2 * core, z),
        (device_of(y, x + 1, core), z),
        (device_of(y, x - 1, core), z),
        (device_of(y + 1, x, core), z),
        (device_of(y - 1, x, core), z),
    ]


def gather_kernel(mine, out, local_sem, send_sem, recv_sem):
    me, core, y, x = place_in_plane()
    z = lax.axis_index("tsp")
    peer = me + 1 - 2 * core
    greet(plane_neighbours())
    ids = {}
    sends = []

    def index_of(key):
        return ids.setdefault(key, len(ids))

    def send(ref, device, key):
        k = index_of(key)
        copy = pltpu.make_async_remote_copy(
            ref, ref, send_sem.at[k], recv_sem.at[k], (device, z), MESH
        )
        copy.start()
        sends.append(copy)

    def arrived(ref, key):
        k = index_of(key)
        pltpu.make_async_remote_copy(
            ref, ref, send_sem.at[k], recv_sem.at[k], (peer, z), MESH
        ).wait_recv()

    def owner(tau, di, dj):
        return device_of(y + dj, x + di, tau) if tau == 0 else device_of(y + di, x + dj, tau)

    def near(tau, di, dj):
        return device_of(y + dj, x + di, core) if tau == 0 else device_of(y + di, x + dj, core)

    def block(tau, di, dj, half):
        return out.at[pl.ds(2 * owner(tau, di, dj), 2), half]

    def unit(tau, di, dj, e):
        return out.at[2 * owner(tau, di, dj) + e, core]

    def swap(tau, di, dj):
        send(block(tau, di, dj, core), peer, ("swap", tau, di, dj))

    local = pltpu.make_async_copy(mine, out.at[pl.ds(2 * me, 2)], local_sem)
    local.start()
    k = index_of("own")
    own = pltpu.make_async_remote_copy(
        mine, out.at[pl.ds(2 * me, 2)], send_sem.at[k], recv_sem.at[k], (peer, z), MESH
    )
    own.start()
    sends.append(own)
    local.wait()
    pltpu.make_async_remote_copy(
        mine, out.at[pl.ds(2 * peer, 2)], send_sem.at[k], recv_sem.at[k], (peer, z), MESH
    ).wait_recv()
    for tau in (0, 1):
        for s in (1, -1):
            send(block(tau, 0, 0, core), near(tau, s, 0), ("one", tau, s))
    for tau in (0, 1):
        for s in (1, -1):
            send(block(tau, 0, 0, core), near(tau, 0, s), ("two", tau, 0, s))
    for tau in (0, 1):
        for s in (1, -1):
            arrived(block(tau, -s, 0, core), ("one", tau, s))
            send(unit(tau, -s, 0, 0 if s == 1 else 1), near(tau, s, 0), ("onward", tau, s))
    for tau in (0, 1):
        for s in (1, -1):
            for t in (1, -1):
                send(block(tau, -s, 0, core), near(tau, 0, t), ("two", tau, -s, t))
            swap(tau, -s, 0)
    for tau in (0, 1):
        arrived(unit(tau, 2, 0, 0), ("onward", tau, 1))
        arrived(unit(tau, 2, 0, 1), ("onward", tau, -1))
        for t in (1, -1):
            send(block(tau, 2, 0, core), near(tau, 0, t), ("two", tau, 2, t))
        swap(tau, 2, 0)
    for di in (0, -1, 1, 2):
        for tau in (0, 1):
            for t in (1, -1):
                arrived(block(tau, di, -t, core), ("two", tau, di, t))
                send(
                    unit(tau, di, -t, 0 if t == 1 else 1),
                    near(tau, 0, t),
                    ("last", tau, di, t),
                )
                swap(tau, di, -t)
    for di in (0, -1, 1, 2):
        for tau in (0, 1):
            arrived(unit(tau, di, 2, 0), ("last", tau, di, 1))
            arrived(unit(tau, di, 2, 1), ("last", tau, di, -1))
            swap(tau, di, 2)
    for copy in sends:
        copy.wait_send()
    for tau in (0, 1):
        for di in (0, -1, 1, 2):
            for dj in (0, -1, 1, 2):
                if di or dj:
                    arrived(block(tau, di, dj, 1 - core), ("swap", tau, di, dj))


def gather_maps(mine):
    places, width = 2 * lax.axis_size("dp"), mine.shape[-1]
    return pl.pallas_call(
        gather_kernel,
        out_shape=jax.ShapeDtypeStruct((places, 2, HALF, width), mine.dtype),
        in_specs=[pl.BlockSpec(memory_space=pltpu.VMEM)],
        out_specs=pl.BlockSpec(memory_space=pl.ANY),
        scratch_shapes=[
            pltpu.SemaphoreType.DMA,
            pltpu.SemaphoreType.DMA((71,)),
            pltpu.SemaphoreType.DMA((71,)),
        ],
        compiler_params=pltpu.CompilerParams(
            collective_id=0, has_side_effects=True, vmem_limit_bytes=8 * 1024 * 1024
        ),
        name="gather_maps",
    )(mine)


def project_kernel(places, live, tokens, cotangent, maps, out):
    g = pl.program_id(0)
    width = tokens.shape[1]
    both = maps[0]
    contract = (((1,), (1,)), ((), ()))
    lowered = lax.dot_general(
        tokens[...], both[:, :width], contract, preferred_element_type=jnp.float32
    )
    pulled = lax.dot_general(
        cotangent[...], both[:, width:], contract, preferred_element_type=jnp.float32
    )
    terms = jnp.concatenate([lowered, pulled], axis=1)
    row = lax.broadcasted_iota(jnp.int32, terms.shape, 0)
    out[0] = jnp.where(row < live[g], terms, 0.0)


def project(places, live, tokens, cotangent, maps):
    segments = places.shape[0]
    rows = tokens.shape[0] // segments
    width, key = tokens.shape[1], cotangent.shape[1]
    ranks = maps.shape[1]
    return pl.pallas_call(
        project_kernel,
        out_shape=jax.ShapeDtypeStruct((segments, rows, 2 * ranks), jnp.float32),
        grid_spec=pltpu.PrefetchScalarGridSpec(
            num_scalar_prefetch=2,
            grid=(segments,),
            in_specs=[
                pl.BlockSpec((rows, width), lambda g, p, n: (g, 0)),
                pl.BlockSpec((rows, key), lambda g, p, n: (g, 0)),
                pl.BlockSpec((1, ranks, width + key), lambda g, p, n: (p[g], 0, 0)),
            ],
            out_specs=pl.BlockSpec((1, rows, 2 * ranks), lambda g, p, n: (g, 0, 0)),
        ),
        name="project",
    )(places, live, tokens, cotangent, maps)


def sum_kernel(part, out, held, sent, send_sem, recv_sem, out_send_sem, out_recv_sem):
    i = lax.axis_index("tsp")
    dp = lax.axis_index("dp")

    def at(v):
        return lax.rem(v + 2 * RING, RING)

    greet([(dp, at(i + 1)), (dp, at(i - 1))])
    copies = []

    def send(src, d, step, u):
        copy = pltpu.make_async_remote_copy(
            src,
            held.at[d, step, u],
            send_sem.at[d, step, u],
            recv_sem.at[d, step, u],
            (dp, at(i + 1 - 2 * d)),
            MESH,
        )
        copy.start()
        copies.append(copy)

    def arrived(d, step, u):
        pltpu.make_async_remote_copy(
            held.at[d, step, u],
            held.at[d, step, u],
            send_sem.at[d, step, u],
            recv_sem.at[d, step, u],
            (dp, at(i + 1 - 2 * d)),
            MESH,
        ).wait_recv()

    for d in (0, 1):
        send(part.at[2 * at(i + 4) + d], d, 0, d)
    for d in (0, 1):
        s = 1 - 2 * d
        send(part.at[2 * at(i + 3 * s) + 1 - d], d, 1, 1 - d)
    for step in (1, 2, 3):
        for v in (0, 1):
            for d in (0, 1):
                u = v if d == 0 else 1 - v
                if step == 1 and v == 1:
                    continue
                s = 1 - 2 * d
                arrived(d, step - 1, u)
                sent[d, step, u] = held[d, step - 1, u] + part[2 * at(i + s * (4 - step)) + u]
                send(sent.at[d, step, u], d, step, u)
    for u in (0, 1):
        arrived(0, 3, u)
        arrived(1, 3, u)
        out[2 * i + u] = (part[2 * i + u] + held[0, 3, u] + held[1, 3, u]).astype(out.dtype)

    def pass_on(chunk, u, d, step):
        ref = out.at[pl.ds(2 * at(chunk), 2)] if u is None else out.at[2 * at(chunk) + u]
        copy = pltpu.make_async_remote_copy(
            ref,
            ref,
            out_send_sem.at[d, step],
            out_recv_sem.at[d, step],
            (dp, at(i + 1 - 2 * d)),
            MESH,
        )
        return copy

    for d in (0, 1):
        copy = pass_on(i, None, d, 0)
        copy.start()
        copies.append(copy)
    for step in (1, 2, 3):
        for d in (0, 1):
            s = 1 - 2 * d
            pass_on(i - step * s, None, d, step - 1).wait_recv()
            copy = pass_on(i - step * s, d if step == 3 else None, d, step)
            copy.start()
            copies.append(copy)
    for d in (0, 1):
        pass_on(i + 4, d, d, 3).wait_recv()
    for copy in copies:
        copy.wait_send()


def sum_over_features(part):
    segments, rows, terms = part.shape
    return pl.pallas_call(
        sum_kernel,
        out_shape=jax.ShapeDtypeStruct(part.shape, jnp.bfloat16),
        in_specs=[pl.BlockSpec(memory_space=pltpu.VMEM)],
        out_specs=pl.BlockSpec(memory_space=pltpu.VMEM),
        scratch_shapes=[
            pltpu.VMEM((2, 4, 2, rows, terms), jnp.float32),
            pltpu.VMEM((2, 4, 2, rows, terms), jnp.float32),
            pltpu.SemaphoreType.DMA((2, 4, 2)),
            pltpu.SemaphoreType.DMA((2, 4, 2)),
            pltpu.SemaphoreType.DMA((2, 4)),
            pltpu.SemaphoreType.DMA((2, 4)),
        ],
        compiler_params=pltpu.CompilerParams(collective_id=1, has_side_effects=True),
        name="sum_over_features",
    )(part)


def slots_kernel(owners, summed, tokens, cotangent, out, total):
    g = pl.program_id(0)
    width = tokens.shape[1]
    rows = tokens.shape[0]
    ranks = summed.shape[2] // 2

    @pl.when(g == 0)
    def _():
        total[...] = jnp.zeros_like(total)

    contract = (((0,), (0,)), ((), ()))
    both = summed[0]
    down = lax.dot_general(
        both[:, ranks:], tokens[...], contract, preferred_element_type=jnp.float32
    )
    up = lax.dot_general(
        both[:, :ranks], cotangent[...], contract, preferred_element_type=jnp.float32
    )
    slot = owners[g]
    total[slot, :, :width] += down
    total[slot, :, width:] += up

    @pl.when(g == pl.num_programs(0) - 1)
    def _():
        @pl.loop(0, total.shape[0])
        def _(o):
            out[o] = (total[o] * (ADAPTER_SCALE / rows)).astype(out.dtype)


def slot_gradients(owners, summed, tokens, cotangent):
    segments, rows, terms = summed.shape
    width, key = tokens.shape[1], cotangent.shape[1]
    shape = (lax.axis_size("dp"), terms // 2, width + key)
    return pl.pallas_call(
        slots_kernel,
        out_shape=jax.ShapeDtypeStruct(shape, jnp.bfloat16),
        grid_spec=pltpu.PrefetchScalarGridSpec(
            num_scalar_prefetch=1,
            grid=(segments,),
            in_specs=[
                pl.BlockSpec((1, rows, terms), lambda g, o: (g, 0, 0)),
                pl.BlockSpec((rows, width), lambda g, o: (g, 0)),
                pl.BlockSpec((rows, key), lambda g, o: (g, 0)),
            ],
            out_specs=pl.BlockSpec(shape, lambda g, o: (0, 0, 0)),
            scratch_shapes=[pltpu.VMEM(shape, jnp.float32)],
        ),
        name="slot_gradients",
    )(owners, summed, tokens, cotangent)


def scatter_kernel(
    slots, entry, out,
    peer_slots, peer_entry, s1, r1, s2, r2, acc, s3, r3, s4, r4, res,
    peer_send, peer_recv, send1, recv1, send2, recv2, send3, recv3, send4, recv4, end_send, end_recv,
):
    me, core, y, x = place_in_plane()
    z = lax.axis_index("tsp")
    peer = me + 1 - 2 * core
    width = slots.shape[-1]
    greet(plane_neighbours())
    waits = []

    def copy_of(src, dst, ss, rs, device):
        return pltpu.make_async_remote_copy(src, dst, ss, rs, (device, z), MESH)

    def go(copy):
        copy.start()
        waits.append(copy)

    def piece(tau, di):
        if tau == 0:
            return slots.at[side(y + di), :, 0, 1 - core], peer_slots.at[side(y + di), :, 0]
        return slots.at[:, side(x + di), 1, 1 - core], peer_slots.at[:, side(x + di), 1]

    def from_peer(tau, di):
        src, dst = piece(tau, di)
        k = di + 1
        return copy_of(src, dst, peer_send.at[tau, k], peer_recv.at[tau, k], peer)

    go(copy_of(entry, peer_entry, end_send.at[1], end_recv.at[1], peer))
    for di in (2, 1, -1, 0):
        for tau in (0, 1):
            go(from_peer(tau, di))
    copy_of(entry, peer_entry, end_send.at[1], end_recv.at[1], peer).wait_recv()

    def term(tau, di, j, e):
        yy, xx = (side(y + di), j) if tau == 0 else (j, side(x + di))
        o = (yy * SIDE + xx) * 2 + tau
        tile = [width // entry.shape[1]]
        mine = jnp.concatenate([entry[pl.ds(o, 1), :]] * tile[0], axis=1)
        theirs = jnp.concatenate([peer_entry[pl.ds(o, 1), :]] * tile[0], axis=1)
        a = slots[yy, xx, tau, core].astype(jnp.float32)
        b = peer_slots[yy, xx, tau].astype(jnp.float32)
        return jnp.where(mine == e, a, 0.0) + jnp.where(theirs == e, b, 0.0)

    def near(tau, axis, s):
        vertical = (tau == 0) == (axis == 0)
        return device_of(y + s, x, core) if vertical else device_of(y, x + s, core)

    def first(tau, d, j):
        return copy_of(
            s1.at[tau, d, j], r1.at[tau, d, j], send1.at[tau, d, j], recv1.at[tau, d, j],
            near(tau, 0, 1 - 2 * d),
        )

    def second(tau, d, j, e):
        return copy_of(
            s2.at[tau, d, j, e], r2.at[tau, d, j, e],
            send2.at[tau, d, j, e], recv2.at[tau, d, j, e], near(tau, 0, 1 - 2 * d),
        )

    for tau in (0, 1):
        from_peer(tau, 2).wait_recv()

        @pl.loop(0, SIDE)
        def _(j):
            for d in (0, 1):
                s1[tau, d, j] = term(tau, 2, j, d).astype(s1.dtype)
                first(tau, d, j).start()

    for tau in (0, 1):
        for d in (0, 1):
            from_peer(tau, 1 - 2 * d).wait_recv()

        @pl.loop(0, SIDE)
        def _(j):
            for d in (0, 1):
                s2[tau, d, j, 1 - d] = term(tau, 1 - 2 * d, j, 1 - d).astype(s2.dtype)
                second(tau, d, j, 1 - d).start()

    for tau in (0, 1):

        @pl.loop(0, SIDE)
        def _(j):
            for d in (0, 1):
                first(tau, d, j).wait_recv()
                passed = r1[tau, d, j].astype(jnp.float32)
                s2[tau, d, j, d] = (term(tau, 1 - 2 * d, j, d) + passed).astype(s2.dtype)
                second(tau, d, j, d).start()

    for tau in (0, 1):
        from_peer(tau, 0).wait_recv()

        @pl.loop(0, SIDE)
        def _(j):
            for e in (0, 1):
                acc[tau, j, e] = term(tau, 0, j, e)

    def spot(tau, dj):
        return side((x if tau == 0 else y) + dj)

    def third(tau, d):
        return copy_of(
            s3.at[tau, d], r3.at[tau, d], send3.at[tau, d], recv3.at[tau, d], near(tau, 1, 1 - 2 * d)
        )

    def fourth(tau, d, e):
        return copy_of(
            s4.at[tau, d, e], r4.at[tau, d, e], send4.at[tau, d, e], recv4.at[tau, d, e],
            near(tau, 1, 1 - 2 * d),
        )

    def total(tau, dj, e):
        j = spot(tau, dj)
        for d in (0, 1):
            second(tau, d, j, e).wait_recv()
        return (
            acc[tau, j, e]
            + r2[tau, 0, j, e].astype(jnp.float32)
            + r2[tau, 1, j, e].astype(jnp.float32)
        )

    for tau in (0, 1):
        for d in (0, 1):
            s3[tau, d] = total(tau, 2, d).astype(s3.dtype)
            go(third(tau, d))
    for tau in (0, 1):
        for d in (0, 1):
            s4[tau, d, 1 - d] = total(tau, 1 - 2 * d, 1 - d).astype(s4.dtype)
            go(fourth(tau, d, 1 - d))
    for tau in (0, 1):
        for d in (0, 1):
            value = total(tau, 1 - 2 * d, d)
            third(tau, d).wait_recv()
            s4[tau, d, d] = (value + r3[tau, d].astype(jnp.float32)).astype(s4.dtype)
            go(fourth(tau, d, d))
    for tau in (0, 1):
        for e in (0, 1):
            value = total(tau, 0, e)
            for d in (0, 1):
                fourth(tau, d, e).wait_recv()
                value += r4[tau, d, e].astype(jnp.float32)
            res[tau, e] = value
    last = copy_of(res.at[1 - core], out.at[:, core], end_send.at[0], end_recv.at[0], peer)
    last.start()
    out[:, core] = res[core]
    copy_of(res.at[1 - core], out.at[:, 1 - core], end_send.at[0], end_recv.at[0], peer).wait_recv()
    last.wait_send()
    for copy in waits:
        copy.wait_send()
    for tau in (0, 1):
        for d in (0, 1):

            @pl.loop(0, SIDE)
            def _(j):
                first(tau, d, j).wait_send()
                for e in (0, 1):
                    second(tau, d, j, e).wait_send()


def scatter_gradients(slots, entry):
    width = slots.shape[-1]
    unit = (HALF, width)
    bf16, f32 = jnp.bfloat16, jnp.float32
    dma = pltpu.SemaphoreType.DMA
    pair = lambda *dims: [dma(dims), dma(dims)]
    return pl.pallas_call(
        scatter_kernel,
        out_shape=jax.ShapeDtypeStruct((2, 2) + unit, f32),
        in_specs=[pl.BlockSpec(memory_space=pltpu.VMEM)] * 2,
        out_specs=pl.BlockSpec(memory_space=pltpu.VMEM),
        scratch_shapes=[
            pltpu.VMEM((SIDE, SIDE, 2) + unit, bf16),
            pltpu.VMEM(entry.shape, f32),
            pltpu.VMEM((2, 2, SIDE) + unit, bf16),
            pltpu.VMEM((2, 2, SIDE) + unit, bf16),
            pltpu.VMEM((2, 2, SIDE, 2) + unit, bf16),
            pltpu.VMEM((2, 2, SIDE, 2) + unit, bf16),
            pltpu.VMEM((2, SIDE, 2) + unit, f32),
            pltpu.VMEM((2, 2) + unit, bf16),
            pltpu.VMEM((2, 2) + unit, bf16),
            pltpu.VMEM((2, 2, 2) + unit, bf16),
            pltpu.VMEM((2, 2, 2) + unit, bf16),
            pltpu.VMEM((2, 2) + unit, f32),
        ]
        + pair(2, 4)
        + pair(2, 2, SIDE)
        + pair(2, 2, SIDE, 2)
        + pair(2, 2)
        + pair(2, 2, 2)
        + pair(2),
        compiler_params=pltpu.CompilerParams(
            collective_id=2, has_side_effects=True, vmem_limit_bytes=VMEM_LIMIT
        ),
        name="scatter_gradients",
    )(slots, entry)


def tokens_kernel(places, live, cotangent, frozen, summed, maps, out):
    g = pl.program_id(0)
    width = out.shape[1]
    ranks = summed.shape[2] // 2
    value = lax.dot_general(
        cotangent[...], frozen[...], (((1,), (1,)), ((), ())), preferred_element_type=jnp.float32
    )
    value += ADAPTER_SCALE * jnp.dot(
        summed[0][:, ranks:], maps[0][:, :width], preferred_element_type=jnp.float32
    )
    row = lax.broadcasted_iota(jnp.int32, value.shape, 0)
    out[...] = jnp.where(row < live[g], value, 0.0).astype(out.dtype)


def token_gradients(places, live, cotangent, frozen, summed, maps):
    segments, rows, terms = summed.shape
    width, keys = frozen.shape
    ranks = maps.shape[1]
    return pl.pallas_call(
        tokens_kernel,
        out_shape=jax.ShapeDtypeStruct((segments * rows, width), jnp.bfloat16),
        grid_spec=pltpu.PrefetchScalarGridSpec(
            num_scalar_prefetch=2,
            grid=(segments,),
            in_specs=[
                pl.BlockSpec((rows, keys), lambda g, p, n: (g, 0)),
                pl.BlockSpec((width, keys), lambda g, p, n: (0, 0)),
                pl.BlockSpec((1, rows, terms), lambda g, p, n: (g, 0, 0)),
                pl.BlockSpec((1, ranks, maps.shape[2]), lambda g, p, n: (p[g], 0, 0)),
            ],
            out_specs=pl.BlockSpec((rows, width), lambda g, p, n: (g, 0)),
        ),
        name="token_gradients",
    )(places, live, cotangent, frozen, summed, maps)


def on_device(
    tokens,
    cotangent,
    frozen_key_weight,
    adapter_down_weight,
    adapter_up_weight,
    adapter_place_table,
    segment_adapter,
    segment_live_count,
):
    dp_count = lax.axis_size("dp")
    held, ranks, width = adapter_down_weight.shape
    places = lookup(segment_adapter, adapter_place_table)
    owners = places // held
    owner_hit = owners[:, None] == jnp.arange(dp_count, dtype=jnp.int32)[None, :]
    wanted = jnp.max(jnp.where(owner_hit, (places % held)[:, None], -1), axis=0)
    entry = jnp.broadcast_to(wanted.astype(jnp.float32)[:, None], (dp_count, 128))
    all_cotangent = lax.all_gather(cotangent, "tsp", axis=1, tiled=True)
    mine = jnp.concatenate([adapter_down_weight, adapter_up_weight], axis=2)
    mine = mine.reshape(held, 2, HALF, mine.shape[2])
    maps = gather_maps(mine).reshape(dp_count * held, ranks, mine.shape[3])
    part = project(places, segment_live_count, tokens, cotangent, maps)
    summed = sum_over_features(part)
    slots = slot_gradients(owners, summed, tokens, cotangent)
    slots = slots.reshape(SIDE, SIDE, 2, 2, HALF, slots.shape[2])
    grads = scatter_gradients(slots, entry).reshape(held, ranks, slots.shape[-1])
    token_gradient = token_gradients(
        places, segment_live_count, all_cotangent, frozen_key_weight, summed, maps
    )
    return token_gradient, grads[:, :, :width], grads[:, :, width:]


def solution(mesh):
    placed = (
        P("dp", "tsp"),
        P("dp", "tsp"),
        P("tsp", None),
        P("dp", None, "tsp"),
        P("dp", None, "tsp"),
        P(),
        P("dp"),
        P("dp"),
    )
    return jax.shard_map(
        on_device,
        mesh=mesh,
        in_specs=placed,
        out_specs=(P("dp", "tsp"), P("dp", None, "tsp"), P("dp", None, "tsp")),
        check_vma=False,
    )
```

time: 472 us -> 188 us (0.40)
  waiting for transfers between devices: 364 us -> 0.68 us
  Pallas kernels: 0 us -> 162 us
  matrix products: 35.8 us -> 0 us
  blocking collectives: 15.3 us -> 0 us
  other arithmetic: 17.2 us -> 2.27 us
  starting transfers between devices: 9.6 us -> 0.04 us
  local copies, waits for them, and re-layouts: 15.6 us -> 7.67 us
    reduce_scatter x2 -> x0, waiting for transfers between devices: 208 us -> none  [the longest x1 127 us: on_device(): lax.psum_scatter(dense_down, 'dp', scatter_dimension=0, tiled=True)]
    pallas_call x0 -> x6, Pallas kernels: none -> 162 us  [the longest x1 43.8 us: scatter_gradients(): pl.pallas_call(scatter_kernel, out_shape=jax.ShapeDtypeStruct((2, 2) + un...]
    psum x1 -> x0, waiting for transfers between devices: 71.8 us -> none  [on_device(): summed = lax.psum(partial_terms, 'tsp')]
    all_to_all x2 -> x0, waiting for transfers between devices: 54.5 us -> none  [the longest x1 49.6 us: on_device(): lax.all_to_all(reply_down, 'dp', split_axis=0, concat_axis=0, tiled=True)]
    dot_general x12 -> x0, matrix products: 35.8 us -> none  [the longest x1 6.88 us: on_device(): jnp.einsum('go,ord->grd', picker, fetched_down, preferred_element_type=jn...]
    all_gather x1, waiting for transfers between devices: 29 us -> 0.01 us  [on_device(): all_cotangent = lax.all_gather(cotangent, 'tsp', axis=1, tiled=True)]
    all_to_all x1 -> x0, blocking collectives: 15.3 us -> none  [on_device(): lax.all_to_all(wanted[:, None], 'dp', split_axis=0, concat_axis=0, tiled=...]
    select_n x3 -> x1, other arithmetic: 14.1 us -> 0.52 us  [on_device(): wanted = jnp.max(jnp.where(owner_hit, (places % held)[:, None], -1), axis=0)]
  transfers between devices with their start and end apart: 6 -> 1, of which waited for: 6 -> 0; matrix products, arithmetic and copies ran while one was open for 11% -> 3% of each run, Pallas kernels for 0% -> 76%
where the time goes in v1:
time: 188 us; the launch traced here: 187 us
  Pallas kernels  162 us (86%)
  between operations  14.1 us (8%)
  local copies, waits for them, and re-layouts  7.67 us (4%)
  other arithmetic  2.27 us (1%)
    pallas_call x1, Pallas kernels, scatter_gradients(): pl.pallas_call(scatter_kernel, out_shape=jax.ShapeDtypeStruct((2, 2) + un...  43.8 us
    pallas_call x1, Pallas kernels, gather_maps(): pl.pallas_call(gather_kernel, out_shape=jax.ShapeDtypeStruct((places, 2,...  35.6 us
    pallas_call x1, Pallas kernels, sum_over_features(): pl.pallas_call(sum_kernel, out_shape=jax.ShapeDtypeStruct(part.shape, jnp...  35.6 us
    pallas_call x1, Pallas kernels, token_gradients(): pl.pallas_call(tokens_kernel, out_shape=jax.ShapeDtypeStruct((segments *...  19.6 us
    pallas_call x1, Pallas kernels, slot_gradients(): pl.pallas_call(slots_kernel, out_shape=jax.ShapeDtypeStruct(shape, jnp.bf...  14.8 us
    pallas_call x1, Pallas kernels, project(): pl.pallas_call(project_kernel, out_shape=jax.ShapeDtypeStruct((segments,...  13 us
  transfers between devices with their start and end apart: 1, of which 0 were waited for; matrix products, arithmetic and copies ran while one was open for 3% of the time, Pallas kernels for 76%

profile of v1, /device:TPU:1, one launch (start us, length us, event | category | flops | bytes accessed | tf_op | source)
XLA Modules:
  0.0 187.1 jit_solution(5777952871249544427)
XLA Ops:
  7.2 0.0 all-gather.2.cloned.1.call-start
  7.2 0.7 all-gather.2.cloned.1.call-update
  7.9 1.0 pad_maximum_fusion
  8.9 0.0 copy-start.3
  8.9 0.0 copy-start.4
  8.9 35.6 %gather_maps.1 = bf16[64,2,32,1152]{3,2,1,0:T(8,128)(2,1)S(1)} custom-call(bf16[2,2,32,1152]{3,2,1,0:T(8,128)(2,1)S(1)} %bitcast.6), custom_call_target="tpu_custom_call" | custom-call | tf_op jit(solution)/shard_map/gather_maps/pallas_call | solution.py:154
  44.5 0.0 copy-start
  44.6 3.6 %copy-done = bf16[64,2,32,1152]{3,2,1,0:T(8,128)(2,1)} copy-done((bf16[64,2,32,1152]{3,2,1,0:T(8,128)(2,1)}, bf16[64,2,32,1152]{3,2,1,0:T(8,128)(2,1)S(1)}, u32[]{:S(2)}) %copy-start) | copy-done | bytes 9437208
  48.2 0.0 copy-done.3
  48.2 0.0 copy-done.4
  48.2 0.7 select_reduce_fusion.1.places
  48.8 0.0 copy-start.1
  48.8 13.0 %project.1.part = f32[16,128,128]{2,1,0:T(8,128)} custom-call(s32[16]{0:T(128)} %select_reduce_fusion.1.places, s32[16]{0:T(128)} %live.3, bf16[2048,1024]{1,0:T(8,128)(2,1)} %tokens.3, bf16[2048,128]{1,0:T(8,128)(2,1)} %cotangent.3, bf16[64,64,1152]{2,1,0:T(8,128)(2,1)} %bitcast.4), custom_call_target="tpu_custom_call" | custom-call | tf_op jit(solution)/shard_map/project/pallas_call | solution.py:192
  61.8 35.6 %sum_over_features.1.summed = bf16[16,128,128]{2,1,0:T(8,128)(2,1)} custom-call(f32[16,128,128]{2,1,0:T(8,128)} %project.1.part), custom_call_target="tpu_custom_call" | custom-call | tf_op jit(solution)/shard_map/sum_over_features/pallas_call | solution.py:292
  97.4 0.0 copy-done.1
  97.4 0.5 and_select_fusion
  98.0 0.0 copy-start.2
  98.0 14.8 %slot_gradients.1 = bf16[32,64,1152]{2,1,0:T(8,128)(2,1)} custom-call(s32[16]{0:T(128)} %get-tuple-element.4.owners, bf16[16,128,128]{2,1,0:T(8,128)(2,1)} %sum_over_features.1.summed, bf16[2048,1024]{1,0:T(8,128)(2,1)} %tokens.3, bf16[2048,128]{1,0:T(8,128)(2,1)} %cotangent.3), custom_call_target="tpu_custom_call" | custom-call | tf_op jit(solution)/shard_map/slot_gradients/pallas_call | solution.py:343
  112.7 0.0 copy-done.2
  112.7 0.1 select_reduce_fusion
  112.8 0.7 broadcast_in_dim.40.entry
  113.5 43.8 %scatter_gradients.1 = f32[2,2,32,1152]{3,2,1,0:T(8,128)} custom-call(bf16[4,4,2,2,32,1152]{5,4,3,2,1,0:T(8,128)(2,1)} %bitcast.7, f32[32,128]{1,0:T(8,128)} %broadcast_in_dim.40.entry), custom_call_target="tpu_custom_call" | custom-call | tf_op jit(solution)/shard_map/scatter_gradients/pallas_call | solution.py:527
  157.3 1.9 %slice.8 = f32[2,64,1024]{2,1,0:T(8,128)} slice(f32[2,64,1152]{2,1,0:T(8,128)} %bitcast.8), slice={[0:2], [0:64], [0:1024]} | slice | bytes 1048576 | tf_op jit(solution)/shard_map/slice | solution.py:624
  159.2 1.5 slice.9
  160.6 0.0 all-gather.2.cloned.1.call-done.cotangent
  160.6 19.6 %token_gradients.1 = bf16[2048,1024]{1,0:T(8,128)(2,1)} custom-call(s32[16]{0:T(128)} %select_reduce_fusion.1.places, s32[16]{0:T(128)} %live.3, bf16[2048,1024]{1,0:T(8,128)(2,1)} %all-gather.2.cloned.1.call-done.cotangent, bf16[1024,1024]{1,0:T(8,128)(2,1)} %frozen.1, bf16[16,128,128]{2,1,0:T(8,128)(2,1)} %sum_over_features.1.summed, ...), custom_call_target="tpu_custom_call" | custom-call | tf_op jit(solution)/shard_map/token_gradients/pallas_call | solution.py:577
  (1 shorter events, 0.0 us)
Async XLA Ops:
  7.2 153.5 %all-gather.2.cloned.1.call-start = ((), (), s32[]{:S(2)}) async-start(), calls=%async_computation | async-start | bytes 4718592 | tf_op jit(solution)/shard_map/all_gather | solution.py:612
  8.9 39.3 %copy-start.3 = (s32[64]{0:T(128)S(1)}, s32[64]{0:T(128)}, u32[]{:S(2)}) copy-start(s32[64]{0:T(128)} %param.13) | copy-start | bytes 772
  8.9 39.3 %copy-start.4 = (s32[16]{0:T(128)S(1)}, s32[16]{0:T(128)}, u32[]{:S(2)}) copy-start(s32[16]{0:T(128)} %param.14) | copy-start | bytes 196
  44.5 3.6 %copy-start = (bf16[64,2,32,1152]{3,2,1,0:T(8,128)(2,1)}, bf16[64,2,32,1152]{3,2,1,0:T(8,128)(2,1)S(1)}, u32[]{:S(2)}) copy-start(bf16[64,2,32,1152]{3,2,1,0:T(8,128)(2,1)S(1)} %gather_maps.1) | copy-start | bytes 28311556
  48.8 48.6 %copy-start.1 = (s32[16]{0:T(128)S(1)}, s32[16]{0:T(128)}, u32[]{:S(2)}) copy-start(s32[16]{0:T(128)} %select_reduce_fusion.1.places) | copy-start | bytes 196
  98.0 14.8 %copy-start.2 = (s32[16]{0:T(128)S(1)}, s32[16]{0:T(128)}, u32[]{:S(2)}) copy-start(s32[16]{0:T(128)} %get-tuple-element.4.owners) | copy-start | bytes 196
Sparse Core Ops, SparseCore 0:
  9.7 67.1 all-gather.1

commit v2 on v1

--- a/solution.py
+++ b/solution.py
@@ -10,7 +10,7 @@
 SIDE = 4
 RING = 8
 HALF = 32
-VMEM_LIMIT = 60 * 1024 * 1024
+MIB = 1024 * 1024
 
 
 def lookup(idents, mapping):
@@ -52,11 +52,27 @@
     ]
 
 
-def gather_kernel(mine, out, local_sem, send_sem, recv_sem):
+def ring(v):
+    return lax.rem(v + 2 * RING, RING)
+
+
+def ring_neighbours():
+    me, z = lax.axis_index("dp"), lax.axis_index("tsp")
+    return [(me, ring(z + 1)), (me, ring(z - 1))]
+
+
+def gather_kernel(mine, cotangent, out, beside, local_sem, send_sem, recv_sem, ring_send, ring_recv):
     me, core, y, x = place_in_plane()
     z = lax.axis_index("tsp")
     peer = me + 1 - 2 * core
-    greet(plane_neighbours())
+    greet(plane_neighbours() + ring_neighbours())
+
+    def hop(src, step, d):
+        return pltpu.make_async_remote_copy(
+            src, beside.at[2 * step + d], ring_send.at[step, d], ring_recv.at[step, d],
+            (me, ring(z + 1 - 2 * d)), MESH,
+        )
+
     ids = {}
     sends = []
 
@@ -110,6 +126,10 @@
     for tau in (0, 1):
         for s in (1, -1):
             send(block(tau, 0, 0, core), near(tau, 0, s), ("two", tau, 0, s))
+    for d in (0, 1):
+        copy = hop(cotangent, 0, d)
+        copy.start()
+        sends.append(copy)
     for tau in (0, 1):
         for s in (1, -1):
             arrived(block(tau, -s, 0, core), ("one", tau, s))
@@ -126,6 +146,12 @@
             send(block(tau, 2, 0, core), near(tau, 0, t), ("two", tau, 2, t))
         swap(tau, 2, 0)
     for di in (0, -1, 1, 2):
+        if di == 1:
+            for d in (0, 1):
+                hop(cotangent, 0, d).wait_recv()
+                copy = hop(beside.at[d], 1, d)
+                copy.start()
+                sends.append(copy)
         for tau in (0, 1):
             for t in (1, -1):
                 arrived(block(tau, di, -t, core), ("two", tau, di, t))
@@ -142,6 +168,8 @@
             swap(tau, di, 2)
     for copy in sends:
         copy.wait_send()
+    for d in (0, 1):
+        hop(beside.at[d], 1, d).wait_recv()
     for tau in (0, 1):
         for di in (0, -1, 1, 2):
             for dj in (0, -1, 1, 2):
@@ -149,59 +177,61 @@
                     arrived(block(tau, di, dj, 1 - core), ("swap", tau, di, dj))
 
 
-def gather_maps(mine):
+def gather_maps(mine, cotangent):
     places, width = 2 * lax.axis_size("dp"), mine.shape[-1]
+    anywhere = pl.BlockSpec(memory_space=pl.ANY)
     return pl.pallas_call(
         gather_kernel,
-        out_shape=jax.ShapeDtypeStruct((places, 2, HALF, width), mine.dtype),
-        in_specs=[pl.BlockSpec(memory_space=pltpu.VMEM)],
-        out_specs=pl.BlockSpec(memory_space=pl.ANY),
+        out_shape=(
+            jax.ShapeDtypeStruct((places, 2, HALF, width), mine.dtype),
+            jax.ShapeDtypeStruct((4,) + cotangent.shape, cotangent.dtype),
+        ),
+        in_specs=[pl.BlockSpec(memory_space=pltpu.VMEM), anywhere],
+        out_specs=(anywhere, anywhere),
         scratch_shapes=[
             pltpu.SemaphoreType.DMA,
             pltpu.SemaphoreType.DMA((71,)),
             pltpu.SemaphoreType.DMA((71,)),
+            pltpu.SemaphoreType.DMA((2, 2)),
+            pltpu.SemaphoreType.DMA((2, 2)),
         ],
         compiler_params=pltpu.CompilerParams(
-            collective_id=0, has_side_effects=True, vmem_limit_bytes=8 * 1024 * 1024
+            collective_id=0, has_side_effects=True, vmem_limit_bytes=4 * MIB
         ),
+        cost_estimate=pl.CostEstimate(flops=0, transcendentals=0, bytes_accessed=60 * MIB),
         name="gather_maps",
-    )(mine)
+    )(mine, cotangent)
 
 
 def project_kernel(places, live, tokens, cotangent, maps, out):
-    g = pl.program_id(0)
+    segments, rows, _ = out.shape
     width = tokens.shape[1]
-    both = maps[0]
     contract = (((1,), (1,)), ((), ()))
-    lowered = lax.dot_general(
-        tokens[...], both[:, :width], contract, preferred_element_type=jnp.float32
-    )
-    pulled = lax.dot_general(
-        cotangent[...], both[:, width:], contract, preferred_element_type=jnp.float32
-    )
-    terms = jnp.concatenate([lowered, pulled], axis=1)
-    row = lax.broadcasted_iota(jnp.int32, terms.shape, 0)
-    out[0] = jnp.where(row < live[g], terms, 0.0)
+    row = lax.broadcasted_iota(jnp.int32, out.shape[1:], 0)
+    for g in range(segments):
+        p = places[g]
+        here = pl.ds(g * rows, rows)
+        lowered = lax.dot_general(
+            tokens[here, :], maps[p, :, :width], contract, preferred_element_type=jnp.float32
+        )
+        pulled = lax.dot_general(
+            cotangent[here, :], maps[p, :, width:], contract, preferred_element_type=jnp.float32
+        )
+        terms = jnp.concatenate([lowered, pulled], axis=1)
+        out[g] = jnp.where(row < live[g], terms, 0.0)
 
 
 def project(places, live, tokens, cotangent, maps):
     segments = places.shape[0]
     rows = tokens.shape[0] // segments
-    width, key = tokens.shape[1], cotangent.shape[1]
-    ranks = maps.shape[1]
+    scalars = pl.BlockSpec(memory_space=pltpu.SMEM)
+    whole = pl.BlockSpec(memory_space=pltpu.VMEM)
     return pl.pallas_call(
         project_kernel,
-        out_shape=jax.ShapeDtypeStruct((segments, rows, 2 * ranks), jnp.float32),
-        grid_spec=pltpu.PrefetchScalarGridSpec(
-            num_scalar_prefetch=2,
-            grid=(segments,),
-            in_specs=[
-                pl.BlockSpec((rows, width), lambda g, p, n: (g, 0)),
-                pl.BlockSpec((rows, key), lambda g, p, n: (g, 0)),
-                pl.BlockSpec((1, ranks, width + key), lambda g, p, n: (p[g], 0, 0)),
-            ],
-            out_specs=pl.BlockSpec((1, rows, 2 * ranks), lambda g, p, n: (g, 0, 0)),
-        ),
+        out_shape=jax.ShapeDtypeStruct((segments, rows, 2 * maps.shape[1]), jnp.float32),
+        in_specs=[scalars, scalars, whole, whole, whole],
+        out_specs=whole,
+        compiler_params=pltpu.CompilerParams(vmem_limit_bytes=20 * MIB),
         name="project",
     )(places, live, tokens, cotangent, maps)
 
@@ -302,73 +332,78 @@
             pltpu.SemaphoreType.DMA((2, 4)),
             pltpu.SemaphoreType.DMA((2, 4)),
         ],
-        compiler_params=pltpu.CompilerParams(collective_id=1, has_side_effects=True),
+        compiler_params=pltpu.CompilerParams(
+            collective_id=1, has_side_effects=True, vmem_limit_bytes=8 * MIB
+        ),
+        cost_estimate=pl.CostEstimate(flops=0, transcendentals=0, bytes_accessed=60 * MIB),
         name="sum_over_features",
     )(part)
 
 
-def slots_kernel(owners, summed, tokens, cotangent, out, total):
-    g = pl.program_id(0)
-    width = tokens.shape[1]
-    rows = tokens.shape[0]
-    ranks = summed.shape[2] // 2
-
-    @pl.when(g == 0)
-    def _():
-        total[...] = jnp.zeros_like(total)
-
+def packed_kernel(heads, summed, tokens, cotangent, out, total):
+    segments, rows, terms = summed.shape
+    ranks, width = terms // 2, tokens.shape[1]
     contract = (((0,), (0,)), ((), ()))
-    both = summed[0]
-    down = lax.dot_general(
-        both[:, ranks:], tokens[...], contract, preferred_element_type=jnp.float32
-    )
-    up = lax.dot_general(
-        both[:, :ranks], cotangent[...], contract, preferred_element_type=jnp.float32
-    )
-    slot = owners[g]
-    total[slot, :, :width] += down
-    total[slot, :, width:] += up
-
-    @pl.when(g == pl.num_programs(0) - 1)
-    def _():
-        @pl.loop(0, total.shape[0])
-        def _(o):
-            out[o] = (total[o] * (ADAPTER_SCALE / rows)).astype(out.dtype)
-
-
-def slot_gradients(owners, summed, tokens, cotangent):
+    for g in range(segments):
+        here = pl.ds(g * rows, rows)
+        down = lax.dot_general(
+            summed[g, :, ranks:], tokens[here, :], contract, preferred_element_type=jnp.float32
+        )
+        up = lax.dot_general(
+            summed[g, :, :ranks], cotangent[here, :], contract, preferred_element_type=jnp.float32
+        )
+        value = jnp.concatenate([down, up], axis=1)
+        h = heads[g]
+        total[h] = jnp.where(h == g, value, total[h] + value)
+
+    @pl.loop(0, segments)
+    def _(g):
+        out[g] = (total[g] * (ADAPTER_SCALE / rows)).astype(out.dtype)
+
+
+def packed_gradients(heads, summed, tokens, cotangent):
     segments, rows, terms = summed.shape
-    width, key = tokens.shape[1], cotangent.shape[1]
-    shape = (lax.axis_size("dp"), terms // 2, width + key)
+    shape = (segments, terms // 2, tokens.shape[1] + cotangent.shape[1])
+    whole = pl.BlockSpec(memory_space=pltpu.VMEM)
     return pl.pallas_call(
-        slots_kernel,
+        packed_kernel,
         out_shape=jax.ShapeDtypeStruct(shape, jnp.bfloat16),
-        grid_spec=pltpu.PrefetchScalarGridSpec(
-            num_scalar_prefetch=1,
-            grid=(segments,),
-            in_specs=[
-                pl.BlockSpec((1, rows, terms), lambda g, o: (g, 0, 0)),
-                pl.BlockSpec((rows, width), lambda g, o: (g, 0)),
-                pl.BlockSpec((rows, key), lambda g, o: (g, 0)),
-            ],
-            out_specs=pl.BlockSpec(shape, lambda g, o: (0, 0, 0)),
-            scratch_shapes=[pltpu.VMEM(shape, jnp.float32)],
-        ),
-        name="slot_gradients",
-    )(owners, summed, tokens, cotangent)
+        in_specs=[pl.BlockSpec(memory_space=pltpu.SMEM), whole, whole, whole],
+        out_specs=whole,
+        scratch_shapes=[pltpu.VMEM(shape, jnp.float32)],
+        compiler_params=pltpu.CompilerParams(vmem_limit_bytes=16 * MIB),
+        name="packed_gradients",
+    )(heads, summed, tokens, cotangent)
 
 
 def scatter_kernel(
-    slots, entry, out,
-    peer_slots, peer_entry, s1, r1, s2, r2, acc, s3, r3, s4, r4, res,
+    index, packed, entry, beside, out_down, out_up, beyond,
+    slots, peer_slots, peer_entry, s1, r1, s2, r2, acc, s3, r3, s4, r4, res_down, res_up,
     peer_send, peer_recv, send1, recv1, send2, recv2, send3, recv3, send4, recv4, end_send, end_recv,
+    ring_send, ring_recv,
 ):
     me, core, y, x = place_in_plane()
     z = lax.axis_index("tsp")
     peer = me + 1 - 2 * core
-    width = slots.shape[-1]
-    greet(plane_neighbours())
+    width = packed.shape[-1]
+    split = out_down.shape[-1]
+    greet(plane_neighbours() + ring_neighbours())
     waits = []
+    half_rows = beside.shape[1] // 2
+
+    def hop(step, d):
+        half = pl.ds(d * half_rows, half_rows)
+        src = beside.at[2 + d] if step == 0 else beyond.at[d, half]
+        dst = beyond.at[d] if step == 0 else beyond.at[2, half]
+        return pltpu.make_async_remote_copy(
+            src, dst, ring_send.at[step, d], ring_recv.at[step, d],
+            (me, ring(z + 1 - 2 * d)), MESH,
+        )
+
+    for d in (0, 1):
+        copy = hop(0, d)
+        copy.start()
+        waits.append(copy)
 
     def copy_of(src, dst, ss, rs, device):
         return pltpu.make_async_remote_copy(src, dst, ss, rs, (device, z), MESH)
@@ -379,8 +414,8 @@
 
     def piece(tau, di):
         if tau == 0:
-            return slots.at[side(y + di), :, 0, 1 - core], peer_slots.at[side(y + di), :, 0]
-        return slots.at[:, side(x + di), 1, 1 - core], peer_slots.at[:, side(x + di), 1]
+            return slots.at[side(y + di), :, 0], peer_slots.at[side(y + di), :, 0]
+        return slots.at[:, side(x + di), 1], peer_slots.at[:, side(x + di), 1]
 
     def from_peer(tau, di):
         src, dst = piece(tau, di)
@@ -390,6 +425,12 @@
     go(copy_of(entry, peer_entry, end_send.at[1], end_recv.at[1], peer))
     for di in (2, 1, -1, 0):
         for tau in (0, 1):
+
+            @pl.loop(0, SIDE)
+            def _(j):
+                yy, xx = (side(y + di), j) if tau == 0 else (j, side(x + di))
+                slots[yy, xx, tau] = packed[index[(yy * SIDE + xx) * 2 + tau], 1 - core]
+
             go(from_peer(tau, di))
     copy_of(entry, peer_entry, end_send.at[1], end_recv.at[1], peer).wait_recv()
 
@@ -399,7 +440,7 @@
         tile = [width // entry.shape[1]]
         mine = jnp.concatenate([entry[pl.ds(o, 1), :]] * tile[0], axis=1)
         theirs = jnp.concatenate([peer_entry[pl.ds(o, 1), :]] * tile[0], axis=1)
-        a = slots[yy, xx, tau, core].astype(jnp.float32)
+        a = packed[index[o], core].astype(jnp.float32)
         b = peer_slots[yy, xx, tau].astype(jnp.float32)
         return jnp.where(mine == e, a, 0.0) + jnp.where(theirs == e, b, 0.0)
 
@@ -455,6 +496,12 @@
         def _(j):
             for e in (0, 1):
                 acc[tau, j, e] = term(tau, 0, j, e)
+
+    for d in (0, 1):
+        hop(0, d).wait_recv()
+        copy = hop(1, d)
+        copy.start()
+        waits.append(copy)
 
     def spot(tau, dj):
         return side((x if tau == 0 else y) + dj)
@@ -500,12 +547,17 @@
             for d in (0, 1):
                 fourth(tau, d, e).wait_recv()
                 value += r4[tau, d, e].astype(jnp.float32)
-            res[tau, e] = value
-    last = copy_of(res.at[1 - core], out.at[:, core], end_send.at[0], end_recv.at[0], peer)
-    last.start()
-    out[:, core] = res[core]
-    copy_of(res.at[1 - core], out.at[:, 1 - core], end_send.at[0], end_recv.at[0], peer).wait_recv()
-    last.wait_send()
+            res_down[tau, e] = value[:, :split]
+            res_up[tau, e] = value[:, split:]
+    for k, (res, out) in enumerate(((res_down, out_down), (res_up, out_up))):
+        go(copy_of(res.at[1 - core], out.at[:, core], end_send.at[2 * k], end_recv.at[2 * k], peer))
+        out[:, core] = res[core]
+    for k, (res, out) in enumerate(((res_down, out_down), (res_up, out_up))):
+        copy_of(
+            res.at[1 - core], out.at[:, 1 - core], end_send.at[2 * k], end_recv.at[2 * k], peer
+        ).wait_recv()
+    for d in (0, 1):
+        hop(1, d).wait_recv()
     for copy in waits:
         copy.wait_send()
     for tau in (0, 1):
@@ -518,18 +570,25 @@
                     second(tau, d, j, e).wait_send()
 
 
-def scatter_gradients(slots, entry):
-    width = slots.shape[-1]
-    unit = (HALF, width)
+def scatter_gradients(index, packed, entry, beside, width):
+    unit = packed.shape[2:]
+    keys = unit[1] - width
     bf16, f32 = jnp.bfloat16, jnp.float32
     dma = pltpu.SemaphoreType.DMA
     pair = lambda *dims: [dma(dims), dma(dims)]
+    whole = pl.BlockSpec(memory_space=pltpu.VMEM)
+    anywhere = pl.BlockSpec(memory_space=pl.ANY)
     return pl.pallas_call(
         scatter_kernel,
-        out_shape=jax.ShapeDtypeStruct((2, 2) + unit, f32),
-        in_specs=[pl.BlockSpec(memory_space=pltpu.VMEM)] * 2,
-        out_specs=pl.BlockSpec(memory_space=pltpu.VMEM),
+        out_shape=(
+            jax.ShapeDtypeStruct((2, 2, HALF, width), f32),
+            jax.ShapeDtypeStruct((2, 2, HALF, keys), f32),
+            jax.ShapeDtypeStruct((3,) + beside.shape[1:], bf16),
+        ),
+        in_specs=[pl.BlockSpec(memory_space=pltpu.SMEM), whole, whole, anywhere],
+        out_specs=(whole, whole, anywhere),
         scratch_shapes=[
+            pltpu.VMEM((SIDE, SIDE, 2) + unit, bf16),
             pltpu.VMEM((SIDE, SIDE, 2) + unit, bf16),
             pltpu.VMEM(entry.shape, f32),
             pltpu.VMEM((2, 2, SIDE) + unit, bf16),
@@ -541,55 +600,93 @@
             pltpu.VMEM((2, 2) + unit, bf16),
             pltpu.VMEM((2, 2, 2) + unit, bf16),
             pltpu.VMEM((2, 2, 2) + unit, bf16),
-            pltpu.VMEM((2, 2) + unit, f32),
+            pltpu.VMEM((2, 2, HALF, width), f32),
+            pltpu.VMEM((2, 2, HALF, keys), f32),
         ]
         + pair(2, 4)
         + pair(2, 2, SIDE)
         + pair(2, 2, SIDE, 2)
         + pair(2, 2)
         + pair(2, 2, 2)
-        + pair(2),
+        + pair(3)
+        + pair(2, 2),
         compiler_params=pltpu.CompilerParams(
-            collective_id=2, has_side_effects=True, vmem_limit_bytes=VMEM_LIMIT
+            collective_id=2, has_side_effects=True, vmem_limit_bytes=24 * MIB
         ),
+        cost_estimate=pl.CostEstimate(flops=0, transcendentals=0, bytes_accessed=100 * MIB),
         name="scatter_gradients",
-    )(slots, entry)
-
-
-def tokens_kernel(places, live, cotangent, frozen, summed, maps, out):
-    g = pl.program_id(0)
-    width = out.shape[1]
-    ranks = summed.shape[2] // 2
-    value = lax.dot_general(
-        cotangent[...], frozen[...], (((1,), (1,)), ((), ())), preferred_element_type=jnp.float32
+    )(index, packed, entry, beside)
+
+
+def tokens_kernel(
+    places, live, cotangent, beside, beyond, frozen, summed, maps, out, tiles, sems
+):
+    segments, rows, terms = summed.shape
+    ranks, width = terms // 2, out.shape[1]
+    keys = cotangent.shape[1]
+    z = lax.axis_index("tsp")
+    block = tiles.shape[1]
+    steps = out.shape[0] // block
+    row = lax.broadcasted_iota(jnp.int32, (rows, width), 0)
+    parts = (
+        (cotangent, None, 0), (beside, 0, -1), (beside, 1, 1), (beside, 2, -2),
+        (beside, 3, 2), (beyond, 0, -3), (beyond, 1, 3), (beyond, 2, 4),
     )
-    value += ADAPTER_SCALE * jnp.dot(
-        summed[0][:, ranks:], maps[0][:, :width], preferred_element_type=jnp.float32
+    weights = jnp.concatenate(
+        [frozen[:, pl.ds(pl.multiple_of(ring(z + r) * keys, keys), keys)] for _, _, r in parts],
+        axis=1,
     )
-    row = lax.broadcasted_iota(jnp.int32, value.shape, 0)
-    out[...] = jnp.where(row < live[g], value, 0.0).astype(out.dtype)
-
-
-def token_gradients(places, live, cotangent, frozen, summed, maps):
+
+    def store(b):
+        return pltpu.make_async_copy(
+            tiles.at[lax.rem(b, 2)], out.at[pl.ds(b * block, block)], sems.at[lax.rem(b, 2)]
+        )
+
+    @pl.loop(0, steps)
+    def _(b):
+        @pl.when(b >= 2)
+        def _():
+            store(b - 2).wait()
+
+        here = pl.ds(pl.multiple_of(b * block, block), block)
+        left = jnp.concatenate(
+            [ref[here, :] if k is None else ref[k, here, :] for ref, k, _ in parts], axis=1
+        )
+        value = lax.dot_general(
+            left, weights, (((1,), (1,)), ((), ())), preferred_element_type=jnp.float32
+        )
+        for k in range(block // rows):
+            g = b * (block // rows) + k
+            extra = jnp.dot(
+                summed[g, :, ranks:], maps[places[g], :, :width], preferred_element_type=jnp.float32
+            )
+            total = value[k * rows : (k + 1) * rows] + ADAPTER_SCALE * extra
+            tiles[lax.rem(b, 2), k * rows : (k + 1) * rows] = jnp.where(
+                row < live[g], total, 0.0
+            ).astype(out.dtype)
+        store(b).start()
+
+    for b in (steps - 2, steps - 1):
+        store(b).wait()
+
+
+def token_gradients(places, live, cotangent, beside, beyond, frozen, summed, maps):
     segments, rows, terms = summed.shape
-    width, keys = frozen.shape
-    ranks = maps.shape[1]
+    width = frozen.shape[0]
+    scalars = pl.BlockSpec(memory_space=pltpu.SMEM)
+    whole = pl.BlockSpec(memory_space=pltpu.VMEM)
     return pl.pallas_call(
         tokens_kernel,
         out_shape=jax.ShapeDtypeStruct((segments * rows, width), jnp.bfloat16),
-        grid_spec=pltpu.PrefetchScalarGridSpec(
-            num_scalar_prefetch=2,
-            grid=(segments,),
-            in_specs=[
-                pl.BlockSpec((rows, keys), lambda g, p, n: (g, 0)),
-                pl.BlockSpec((width, keys), lambda g, p, n: (0, 0)),
-                pl.BlockSpec((1, rows, terms), lambda g, p, n: (g, 0, 0)),
-                pl.BlockSpec((1, ranks, maps.shape[2]), lambda g, p, n: (p[g], 0, 0)),
-            ],
-            out_specs=pl.BlockSpec((rows, width), lambda g, p, n: (g, 0)),
-        ),
+        in_specs=[scalars, scalars] + [whole] * 6,
+        out_specs=pl.BlockSpec(memory_space=pl.ANY),
+        scratch_shapes=[
+            pltpu.VMEM((2, 2 * rows, width), jnp.bfloat16),
+            pltpu.SemaphoreType.DMA((2,)),
+        ],
+        compiler_params=pltpu.CompilerParams(vmem_limit_bytes=28 * MIB),
         name="token_gradients",
-    )(places, live, cotangent, frozen, summed, maps)
+    )(places, live, cotangent, beside, beyond, frozen, summed, maps)
 
 
 def on_device(
@@ -606,22 +703,30 @@
     held, ranks, width = adapter_down_weight.shape
     places = lookup(segment_adapter, adapter_place_table)
     owners = places // held
+    segment = jnp.arange(places.shape[0], dtype=jnp.int32)
+    same = owners[:, None] == owners[None, :]
+    heads = jnp.min(jnp.where(same, segment[None, :], places.shape[0]), axis=1)
     owner_hit = owners[:, None] == jnp.arange(dp_count, dtype=jnp.int32)[None, :]
     wanted = jnp.max(jnp.where(owner_hit, (places % held)[:, None], -1), axis=0)
+    index = jnp.max(jnp.where(owner_hit, heads[:, None], 0), axis=0)
     entry = jnp.broadcast_to(wanted.astype(jnp.float32)[:, None], (dp_count, 128))
-    all_cotangent = lax.all_gather(cotangent, "tsp", axis=1, tiled=True)
     mine = jnp.concatenate([adapter_down_weight, adapter_up_weight], axis=2)
     mine = mine.reshape(held, 2, HALF, mine.shape[2])
-    maps = gather_maps(mine).reshape(dp_count * held, ranks, mine.shape[3])
+    maps, beside = gather_maps(mine, cotangent)
+    maps = maps.reshape(dp_count * held, ranks, mine.shape[3])
     part = project(places, segment_live_count, tokens, cotangent, maps)
     summed = sum_over_features(part)
-    slots = slot_gradients(owners, summed, tokens, cotangent)
-    slots = slots.reshape(SIDE, SIDE, 2, 2, HALF, slots.shape[2])
-    grads = scatter_gradients(slots, entry).reshape(held, ranks, slots.shape[-1])
+    packed = packed_gradients(heads, summed, tokens, cotangent)
+    packed = packed.reshape(packed.shape[0], 2, HALF, packed.shape[2])
+    down_grad, up_grad, beyond = scatter_gradients(index, packed, entry, beside, width)
     token_gradient = token_gradients(
-        places, segment_live_count, all_cotangent, frozen_key_weight, summed, maps
+        places, segment_live_count, cotangent, beside, beyond, frozen_key_weight, summed, maps
     )
-    return token_gradient, grads[:, :, :width], grads[:, :, width:]
+    return (
+        token_gradient,
+        down_grad.reshape(held, ranks, width),
+        up_grad.reshape(held, ranks, cotangent.shape[1]),
+    )
 
 
 def solution(mesh):

time: 188 us -> 131 us (0.70)
  Pallas kernels: 162 us -> 122 us
  between operations: 14.1 us -> 0.73 us
  local copies, waits for them, and re-layouts: 7.67 us -> 5.38 us
    pallas_call x1, Pallas kernels: 13 us -> 1.99 us  [project(): pl.pallas_call(project_kernel, out_shape=jax.ShapeDtypeStruct((segments,...]
    pallas_call x1, Pallas kernels: 19.6 us -> 9.05 us  [token_gradients(): pl.pallas_call(tokens_kernel, out_shape=jax.ShapeDtypeStruct((segments *...]
    pallas_call x1, Pallas kernels: 35.6 us -> 26.3 us  [sum_over_features(): pl.pallas_call(sum_kernel, out_shape=jax.ShapeDtypeStruct(part.shape, jnp...]
    pallas_call x3, Pallas kernels: 94.1 us -> 85 us  [the longest x1 42.5 us: scatter_gradients(): pl.pallas_call(scatter_kernel, out_shape=(jax.ShapeDtypeStruct((2, 2, HAL...]
    slice x2 -> x0, local copies, waits for them, and re-layouts: 3.36 us -> none  [on_device(): return (token_gradient, grads[:, :, :width], grads[:, :, width:])]
  transfers between devices with their start and end apart: 1 -> 0, of which waited for: 0 -> 0; matrix products, arithmetic and copies ran while one was open for 3% -> 0% of each run, Pallas kernels for 76% -> 0%
where the time goes in v2:
time: 131 us
  Pallas kernels  122 us (93%)
  local copies, waits for them, and re-layouts  5.38 us (4%)
  other arithmetic  2.14 us (2%)
    pallas_call x1, Pallas kernels, scatter_gradients(): pl.pallas_call(scatter_kernel, out_shape=(jax.ShapeDtypeStruct((2, 2, HAL...  42.5 us
    pallas_call x1, Pallas kernels, gather_maps(): pl.pallas_call(gather_kernel, out_shape=(jax.ShapeDtypeStruct((places, 2,...  39.8 us
    pallas_call x1, Pallas kernels, sum_over_features(): pl.pallas_call(sum_kernel, out_shape=jax.ShapeDtypeStruct(part.shape, jnp...  26.3 us
    pallas_call x1, Pallas kernels, token_gradients(): pl.pallas_call(tokens_kernel, out_shape=jax.ShapeDtypeStruct((segments *...  9.05 us
    unnamed x10, local copies, waits for them, and re-layouts  5.31 us
    pallas_call x1, Pallas kernels, packed_gradients(): pl.pallas_call(packed_kernel, out_shape=jax.ShapeDtypeStruct(shape, jnp.b...  2.68 us

profile of v2, /device:TPU:1, one launch (start us, length us, event | category | flops | bytes accessed | tf_op | source)
XLA Modules:
  0.0 130.6 jit_solution(7849695040739844427)
XLA Ops:
  0.6 0.9 select_reduce_fusion.3.places
  1.5 0.2 select_reduce_fusion.2.heads
  1.7 0.1 select_reduce_fusion
  1.8 0.1 broadcast_in_dim.68.entry
  1.9 1.0 pad_maximum_fusion
  2.9 0.0 copy-start.1
  2.9 1.0 copy-done.1
  3.9 39.8 %gather_maps.1 = (bf16[64,2,32,1152]{3,2,1,0:T(8,128)(2,1)S(1)}, bf16[4,2048,128]{2,1,0:T(8,128)(2,1)S(1)}) custom-call(bf16[2,2,32,1152]{3,2,1,0:T(8,128)(2,1)S(1)} %bitcast.8, bf16[2048,128]{1,0:T(8,128)(2,1)S(1)} %copy-done.1), custom_call_target="tpu_custom_call" | custom-call | bytes 62914560 | tf_op jit(solution)/shard_map/gather_maps/pallas_call | solution.py:183
  43.8 0.0 copy-start
  43.8 2.2 %copy-done = bf16[2048,1024]{1,0:T(8,128)(2,1)S(1)} copy-done((bf16[2048,1024]{1,0:T(8,128)(2,1)S(1)}, bf16[2048,1024]{1,0:T(8,128)(2,1)}, u32[]{:S(2)}) %copy-start) | copy-done | bytes 4194328
  45.9 0.0 copy-start.3
  45.9 0.7 copy-done.3
  46.6 2.0 %project.1.part = f32[16,128,128]{2,1,0:T(8,128)S(1)} custom-call(s32[16]{0:T(128)S(1)} %select_reduce_fusion.3.places, s32[16]{0:T(128)S(1)} %copy-done.3, bf16[2048,1024]{1,0:T(8,128)(2,1)S(1)} %copy-done, bf16[2048,128]{1,0:T(8,128)(2,1)S(1)} %copy-done.1, bf16[64,64,1152]{2,1,0:T(8,128)(2,1)S(1)} %bitcast.5), custom_call_target="tpu_custom_call" | custom-call | tf_op jit(solution)/shard_map/project/pallas_call | solution.py:229
  48.6 26.3 %sum_over_features.1.summed = bf16[16,128,128]{2,1,0:T(8,128)(2,1)S(1)} custom-call(f32[16,128,128]{2,1,0:T(8,128)S(1)} %project.1.part), custom_call_target="tpu_custom_call" | custom-call | bytes 62914560 | tf_op jit(solution)/shard_map/sum_over_features/pallas_call | solution.py:322
  74.9 2.7 %packed_gradients.1 = bf16[16,64,1152]{2,1,0:T(8,128)(2,1)S(1)} custom-call(s32[16]{0:T(128)S(1)} %select_reduce_fusion.2.heads, bf16[16,128,128]{2,1,0:T(8,128)(2,1)S(1)} %sum_over_features.1.summed, bf16[2048,1024]{1,0:T(8,128)(2,1)S(1)} %copy-done, bf16[2048,128]{1,0:T(8,128)(2,1)S(1)} %copy-done.1), custom_call_target="tpu_custom_call" | custom-call | tf_op jit(solution)/shard_map/packed_gradients/pallas_call | solution.py:368
  77.6 0.0 copy-start.2
  77.6 42.5 %scatter_gradients.1 = (f32[2,2,32,1024]{3,2,1,0:T(8,128)S(1)}, f32[2,2,32,128]{3,2,1,0:T(8,128)S(1)}, bf16[3,2048,128]{2,1,0:T(8,128)(2,1)S(1)}) custom-call(s32[32]{0:T(128)S(1)} %get-tuple-element.14.index, bf16[16,2,32,1152]{3,2,1,0:T(8,128)(2,1)S(1)} %bitcast.7, f32[32,128]{1,0:T(8,128)S(1)} %broadcast_in_dim.68.entry, ...), custom_call_target="tpu_custom_call" | custom-call | bytes 104857600 | tf_op jit(solution)/shard_map/scatter_gradients/pallas_call | solution.py:581
  120.1 0.0 copy-done.2
  120.1 9.0 %token_gradients.1 = bf16[2048,1024]{1,0:T(8,128)(2,1)} custom-call(s32[16]{0:T(128)S(1)} %select_reduce_fusion.3.places, s32[16]{0:T(128)S(1)} %copy-done.3, bf16[2048,128]{1,0:T(8,128)(2,1)S(1)} %copy-done.1, bf16[4,2048,128]{2,1,0:T(8,128)(2,1)S(1)} %get-tuple-element.8.beside, bf16[3,2048,128]{2,1,0:T(8,128)(2,1)S(1)} %get-tuple-element.10.beyond, ...), custom_call_target="tpu_custom_call" | custom-call | tf_op jit(solution)/shard_map/token_gradients/pallas_call | solution.py:678
  129.1 0.8 copy.13
  129.9 0.6 copy.14
  (2 shorter events, 0.0 us)
Async XLA Ops:
  2.9 1.0 copy-start.1
  43.8 2.2 %copy-start = (bf16[2048,1024]{1,0:T(8,128)(2,1)S(1)}, bf16[2048,1024]{1,0:T(8,128)(2,1)}, u32[]{:S(2)}) copy-start(bf16[2048,1024]{1,0:T(8,128)(2,1)} %tokens.3) | copy-start | bytes 12582916
  45.9 0.7 copy-start.3
  77.6 42.5 %copy-start.2 = (bf16[1024,1024]{1,0:T(8,128)(2,1)S(1)}, bf16[1024,1024]{1,0:T(8,128)(2,1)}, u32[]{:S(2)}) copy-start(bf16[1024,1024]{1,0:T(8,128)(2,1)} %frozen.1) | copy-start | bytes 6291460

commit v3 on v0

v3 whole, which is shorter than its diff:
```python
import jax
import jax.numpy as jnp
from jax import lax
from jax.experimental import pallas as pl
from jax.experimental.pallas import tpu as pltpu
from jax.sharding import PartitionSpec as P

ADAPTER_SCALE = 2.0
MESH = pl.DeviceIdType.MESH
SIDE = 4
RING = 8
HALF = 32
MIB = 1024 * 1024
NEAR = (0, -1, 1, 2)


def lookup(idents, mapping):
    matches = idents[:, None] == jnp.arange(mapping.shape[0], dtype=jnp.int32)[None, :]
    return jnp.sum(jnp.where(matches, mapping[None, :], 0), axis=1)


def place_in_plane():
    me = lax.axis_index("dp")
    core = lax.rem(me, 2)
    chip = lax.div(me, 2)
    return me, core, lax.div(chip, SIDE), lax.rem(chip, SIDE)


def side(v):
    return lax.rem(v + 2 * SIDE, SIDE)


def ring(v):
    return lax.rem(v + 2 * RING, RING)


def device_of(y, x, core):
    return (side(y) * SIDE + side(x)) * 2 + core


def greet_neighbours():
    me, core, y, x = place_in_plane()
    z = lax.axis_index("tsp")
    devices = [
        (me + 1 - 2 * core, z),
        (device_of(y, x + 1, core), z),
        (device_of(y, x - 1, core), z),
        (device_of(y + 1, x, core), z),
        (device_of(y - 1, x, core), z),
        (me, ring(z + 1)),
        (me, ring(z - 1)),
    ]
    barrier = pltpu.get_barrier_semaphore()
    for device in devices:
        pl.semaphore_signal(barrier, inc=1, device_id=device, device_id_type=MESH)
    pl.semaphore_wait(barrier, len(devices))


def remote(src, dst, send, recv, device):
    return pltpu.make_async_remote_copy(src, dst, send, recv, device, MESH)


class PlaneGather:
    copies = 71

    def __init__(self, mine, out, local_sem, send_sem, recv_sem):
        self.me, self.core, self.y, self.x = place_in_plane()
        self.z = lax.axis_index("tsp")
        self.peer = self.me + 1 - 2 * self.core
        self.mine, self.out = mine, out
        self.local_sem, self.send_sem, self.recv_sem = local_sem, send_sem, recv_sem
        self.ids, self.sends = {}, []

    def make(self, src, dst, device, key):
        k = self.ids.setdefault(key, len(self.ids))
        return remote(src, dst, self.send_sem.at[k], self.recv_sem.at[k], (device, self.z))

    def send(self, ref, device, key):
        copy = self.make(ref, ref, device, key)
        copy.start()
        self.sends.append(copy)

    def arrived(self, ref, key):
        self.make(ref, ref, self.peer, key).wait_recv()

    def spot(self, tau, di, dj, core):
        if tau == 0:
            return device_of(self.y + dj, self.x + di, core)
        return device_of(self.y + di, self.x + dj, core)

    def near(self, tau, di, dj):
        return self.spot(tau, di, dj, self.core)

    def block(self, tau, di, dj, half):
        return self.out.at[pl.ds(2 * self.spot(tau, di, dj, tau), 2), half]

    def unit(self, tau, di, dj, e):
        return self.out.at[2 * self.spot(tau, di, dj, tau) + e, self.core]

    def swap(self, tau, di, dj):
        self.send(self.block(tau, di, dj, self.core), self.peer, ("swap", tau, di, dj))

    def own(self):
        here = self.out.at[pl.ds(2 * self.me, 2)]
        self.local = pltpu.make_async_copy(self.mine, here, self.local_sem)
        self.local.start()
        copy = self.make(self.mine, here, self.peer, "own")
        copy.start()
        self.sends.append(copy)

    def own_arrived(self):
        self.local.wait()
        self.make(self.mine, self.out.at[pl.ds(2 * self.peer, 2)], self.peer, "own").wait_recv()

    def one(self):
        for tau in (0, 1):
            for s in (1, -1):
                self.send(self.block(tau, 0, 0, self.core), self.near(tau, s, 0), ("one", tau, s))

    def two(self, *offsets):
        for di in offsets:
            for tau in (0, 1):
                for t in (1, -1):
                    self.send(
                        self.block(tau, di, 0, self.core), self.near(tau, 0, t), ("two", tau, di, t)
                    )

    def one_arrived(self):
        for tau in (0, 1):
            for s in (1, -1):
                self.arrived(self.block(tau, -s, 0, self.core), ("one", tau, s))
                e = 0 if s == 1 else 1
                self.send(self.unit(tau, -s, 0, e), self.near(tau, s, 0), ("onward", tau, s))
        self.two(-1, 1)
        for tau in (0, 1):
            for s in (1, -1):
                self.swap(tau, -s, 0)

    def onward_arrived(self):
        for tau in (0, 1):
            self.arrived(self.unit(tau, 2, 0, 0), ("onward", tau, 1))
            self.arrived(self.unit(tau, 2, 0, 1), ("onward", tau, -1))
        self.two(2)
        for tau in (0, 1):
            self.swap(tau, 2, 0)

    def two_arrived(self, di):
        for tau in (0, 1):
            for t in (1, -1):
                self.arrived(self.block(tau, di, -t, self.core), ("two", tau, di, t))
                e = 0 if t == 1 else 1
                self.send(
                    self.unit(tau, di, -t, e), self.near(tau, 0, t), ("last", tau, di, t)
                )
                self.swap(tau, di, -t)

    def last_arrived(self, di):
        for tau in (0, 1):
            self.arrived(self.unit(tau, di, 2, 0), ("last", tau, di, 1))
            self.arrived(self.unit(tau, di, 2, 1), ("last", tau, di, -1))
            self.swap(tau, di, 2)

    def swaps_arrived(self):
        for tau in (0, 1):
            for di in NEAR:
                for dj in NEAR:
                    if di or dj:
                        self.arrived(self.block(tau, di, dj, 1 - self.core), ("swap", tau, di, dj))

    def sent(self):
        for copy in self.sends:
            copy.wait_send()


class RingSum:
    def __init__(self, part, out, held, passed, send_sem, recv_sem, out_send, out_recv):
        self.me, self.i = lax.axis_index("dp"), lax.axis_index("tsp")
        self.part, self.out, self.held, self.passed = part, out, held, passed
        self.send_sem, self.recv_sem = send_sem, recv_sem
        self.out_send, self.out_recv = out_send, out_recv
        self.copies = []

    def copy(self, src, d, step, u):
        return remote(
            src, self.held.at[d, step, u], self.send_sem.at[d, step, u],
            self.recv_sem.at[d, step, u], (self.me, ring(self.i + 1 - 2 * d)),
        )

    def send(self, src, d, step, u):
        copy = self.copy(src, d, step, u)
        copy.start()
        self.copies.append(copy)

    def begin(self):
        for d in (0, 1):
            self.send(self.part.at[ring(self.i + 4), d], d, 0, d)
        for d in (0, 1):
            s = 1 - 2 * d
            self.send(self.part.at[ring(self.i + 3 * s), 1 - d], d, 1, 1 - d)

    def step(self, step):
        for v in (0, 1):
            for d in (0, 1):
                u = v if d == 0 else 1 - v
                if step == 1 and v == 1:
                    continue
                s = 1 - 2 * d
                self.copy(self.held.at[d, step - 1, u], d, step - 1, u).wait_recv()
                self.passed[d, step, u] = (
                    self.held[d, step - 1, u] + self.part[ring(self.i + s * (4 - step)), u]
                )
                self.send(self.passed.at[d, step, u], d, step, u)

    def pass_on(self, chunk, u, d, step):
        ref = self.out.at[ring(chunk)] if u is None else self.out.at[ring(chunk), u]
        return remote(
            ref, ref, self.out_send.at[d, step], self.out_recv.at[d, step],
            (self.me, ring(self.i + 1 - 2 * d)),
        )

    def total(self):
        for u in (0, 1):
            for d in (0, 1):
                self.copy(self.held.at[d, 3, u], d, 3, u).wait_recv()
            self.out[self.i, u] = (
                self.part[self.i, u] + self.held[0, 3, u] + self.held[1, 3, u]
            ).astype(self.out.dtype)
        for d in (0, 1):
            copy = self.pass_on(self.i, None, d, 0)
            copy.start()
            self.copies.append(copy)

    def onward(self, step):
        for d in (0, 1):
            s = 1 - 2 * d
            self.pass_on(self.i - step * s, None, d, step - 1).wait_recv()
            copy = self.pass_on(self.i - step * s, d if step == 3 else None, d, step)
            copy.start()
            self.copies.append(copy)

    def end(self):
        for d in (0, 1):
            self.pass_on(self.i + 4, d, d, 3).wait_recv()

    def sent(self):
        for copy in self.copies:
            copy.wait_send()


def ring_sum_scratch(part):
    dma = pltpu.SemaphoreType.DMA
    shape = (2, 4, 2) + part[2:]
    return [
        pltpu.VMEM(shape, jnp.float32), pltpu.VMEM(shape, jnp.float32),
        dma((2, 4, 2)), dma((2, 4, 2)), dma((2, 4)), dma((2, 4)),
    ]


class CotangentRing:
    def __init__(self, source, target, send_sem, recv_sem, rows):
        self.me, self.z = lax.axis_index("dp"), lax.axis_index("tsp")
        self.source, self.target = source, target
        self.send_sem, self.recv_sem = send_sem, recv_sem
        self.quarter = rows // 4
        self.copies = []

    def copy(self, step, d, q):
        here = pl.ds(q * self.quarter, self.quarter)
        src, dst = self.source(step, d), self.target(step, d)
        return remote(
            src.at[here], dst.at[here], self.send_sem.at[step, d, q],
            self.recv_sem.at[step, d, q], (self.me, ring(self.z + 1 - 2 * d)),
        )

    def launch(self, step, q, first=False):
        for d in (0, 1):
            if step == 3 and q // 2 != d:
                continue
            if not first:
                self.copy(step - 1, d, q).wait_recv()
            copy = self.copy(step, d, q)
            copy.start()
            self.copies.append(copy)

    def arrived(self, step, q):
        for d in (0, 1):
            if step == 3 and q // 2 != d:
                continue
            self.copy(step, d, q).wait_recv()

    def sent(self):
        for copy in self.copies:
            copy.wait_send()


def gather_kernel(
    places, live, down, up, tokens, cotangent,
    down_maps, pulled, tokens_here, cotangent_here, beside,
    up_maps, part, held, passed, send_sem, recv_sem, out_send, out_recv,
    local_sem, down_send, down_recv, up_send, up_recv, cot_send, cot_recv,
):
    greet_neighbours()
    downs = PlaneGather(down, down_maps, local_sem.at[0], down_send, down_recv)
    ups = PlaneGather(up, up_maps, local_sem.at[1], up_send, up_recv)
    sums = RingSum(part, pulled, held, passed, send_sem, recv_sem, out_send, out_recv)
    cots = CotangentRing(
        lambda step, d: cotangent if step == 0 else beside.at[2 * (step - 1) + d],
        lambda step, d: beside.at[2 * step + d],
        cot_send, cot_recv, cotangent.shape[0],
    )
    ups.own()
    downs.own()
    cotangent_copy = pltpu.make_async_copy(cotangent, cotangent_here, local_sem.at[2])
    cotangent_copy.start()
    tokens_copy = pltpu.make_async_copy(tokens, tokens_here, local_sem.at[3])
    tokens_copy.start()
    ups.own_arrived()
    ups.one()
    ups.two(0)
    downs.own_arrived()
    downs.one()
    for q in range(4):
        cots.launch(0, q, first=True)
    ups.one_arrived()
    downs.two(0)
    ups.onward_arrived()
    downs.one_arrived()
    for di in NEAR:
        ups.two_arrived(di)
    for di in NEAR:
        ups.last_arrived(di)
    downs.onward_arrived()
    ups.swaps_arrived()
    cotangent_copy.wait()

    segments = places.shape[0]
    rows = cotangent.shape[0] // segments
    ranks, keys = 2 * HALF, cotangent.shape[1]
    row = lax.broadcasted_iota(jnp.int32, (rows, ranks), 0)
    for j in range(segments // 2):
        pair = []
        for g in (2 * j, 2 * j + 1):
            term = lax.dot_general(
                cotangent_here[g * rows : (g + 1) * rows, :],
                up_maps[places[g]].reshape(ranks, keys),
                (((1,), (1,)), ((), ())),
                preferred_element_type=jnp.float32,
            )
            pair.append(jnp.where(row < live[g], term, 0.0))
        part[j] = jnp.concatenate(pair, axis=1).reshape(part.shape[1:])
    sums.begin()
    sums.step(1)
    downs.two_arrived(0)
    sums.step(2)
    downs.two_arrived(-1)
    sums.step(3)
    downs.two_arrived(1)
    sums.total()
    cots.launch(1, 0)
    downs.two_arrived(2)
    sums.onward(1)
    downs.last_arrived(0)
    cots.launch(1, 1)
    downs.last_arrived(-1)
    sums.onward(2)
    downs.last_arrived(1)
    downs.last_arrived(2)
    sums.onward(3)
    sums.end()
    downs.swaps_arrived()
    tokens_copy.wait()
    for q in (2, 3):
        cots.arrived(0, q)
    for q in (0, 1):
        cots.arrived(1, q)
    for each in (ups, downs, sums, cots):
        each.sent()


def gather_maps(places, live, down, up, tokens, cotangent):
    count = 2 * lax.axis_size("dp")
    rows = cotangent.shape[0] // places.shape[0]
    ranks = 2 * HALF
    part = (places.shape[0] // 2, 2, rows // 2, 2 * ranks)
    bf16 = jnp.bfloat16
    dma = pltpu.SemaphoreType.DMA
    scalars = pl.BlockSpec(memory_space=pltpu.SMEM)
    whole = pl.BlockSpec(memory_space=pltpu.VMEM)
    anywhere = pl.BlockSpec(memory_space=pl.ANY)
    far = pl.BlockSpec(memory_space=pltpu.HBM)
    return pl.pallas_call(
        gather_kernel,
        out_shape=(
            jax.ShapeDtypeStruct((count,) + down.shape[1:], bf16),
            jax.ShapeDtypeStruct(part, bf16),
            jax.ShapeDtypeStruct(tokens.shape, bf16),
            jax.ShapeDtypeStruct(cotangent.shape, bf16),
            jax.ShapeDtypeStruct((4,) + cotangent.shape, bf16),
        ),
        in_specs=[scalars, scalars, far, far, far, far],
        out_specs=(anywhere, whole, whole, whole, anywhere),
        scratch_shapes=[pltpu.VMEM((count,) + up.shape[1:], bf16), pltpu.VMEM(part, jnp.float32)]
        + ring_sum_scratch(part)
        + [dma((4,))]
        + [dma((PlaneGather.copies,)) for _ in range(4)]
        + [dma((2, 2, 4)), dma((2, 2, 4))],
        compiler_params=pltpu.CompilerParams(
            collective_id=0, has_side_effects=True, vmem_limit_bytes=12 * MIB
        ),
        name="gather_maps",
    )(places, live, down, up, tokens, cotangent)


def between_kernel(places, live, heads, tokens, maps, pulled, part, packed, total):
    segments = places.shape[0]
    rows, width = tokens.shape[0] // segments, tokens.shape[1]
    ranks = 2 * HALF
    row = lax.broadcasted_iota(jnp.int32, (rows, ranks), 0)
    for j in range(segments // 2):
        both = pulled[j].reshape(rows, 2 * ranks)
        pair = []
        for k in (0, 1):
            g = 2 * j + k
            here = slice(g * rows, (g + 1) * rows)
            term = lax.dot_general(
                tokens[here, :], maps[places[g]].reshape(ranks, width),
                (((1,), (1,)), ((), ())), preferred_element_type=jnp.float32,
            )
            pair.append(jnp.where(row < live[g], term, 0.0))
            value = lax.dot_general(
                both[:, k * ranks : (k + 1) * ranks], tokens[here, :],
                (((0,), (0,)), ((), ())), preferred_element_type=jnp.float32,
            )
            h = heads[g]
            total[h] = jnp.where(h == g, value, total[h] + value)
        part[j] = jnp.concatenate(pair, axis=1).reshape(part.shape[1:])

    @pl.loop(0, segments)
    def _(g):
        scaled = (total[g] * (ADAPTER_SCALE / rows)).astype(packed.dtype)
        packed[g] = scaled.reshape(packed.shape[1:])


def between(places, live, heads, tokens, maps, pulled):
    segments, width = places.shape[0], tokens.shape[1]
    scalars = pl.BlockSpec(memory_space=pltpu.SMEM)
    whole = pl.BlockSpec(memory_space=pltpu.VMEM)
    return pl.pallas_call(
        between_kernel,
        out_shape=(
            jax.ShapeDtypeStruct(pulled.shape, jnp.float32),
            jax.ShapeDtypeStruct((segments, 2, HALF, width), jnp.bfloat16),
        ),
        in_specs=[scalars] * 3 + [whole] * 3,
        out_specs=(whole, whole),
        scratch_shapes=[pltpu.VMEM((segments, 2 * HALF, width), jnp.float32)],
        compiler_params=pltpu.CompilerParams(vmem_limit_bytes=24 * MIB),
        name="between",
    )(places, live, heads, tokens, maps, pulled)


class PlaneReduce:
    def __init__(self, index, packed, entry, peer_entry, out, bufs, sems):
        self.me, self.core, self.y, self.x = place_in_plane()
        self.z = lax.axis_index("tsp")
        self.peer = self.me + 1 - 2 * self.core
        self.index, self.packed, self.entry, self.peer_entry = index, packed, entry, peer_entry
        self.out = out
        (
            self.slots, self.peer_slots, self.s1, self.r1, self.s2, self.r2,
            self.acc, self.s3, self.r3, self.s4, self.r4, self.res,
        ) = bufs
        self.sems = sems
        self.waits = []

    @staticmethod
    def scratch(unit):
        bf16, f32 = jnp.bfloat16, jnp.float32
        dma = pltpu.SemaphoreType.DMA
        bufs = [
            pltpu.VMEM((SIDE, SIDE, 2) + unit, bf16),
            pltpu.VMEM((SIDE, SIDE, 2) + unit, bf16),
            pltpu.VMEM((2, 2, SIDE) + unit, bf16),
            pltpu.VMEM((2, 2, SIDE) + unit, bf16),
            pltpu.VMEM((2, 2, SIDE, 2) + unit, bf16),
            pltpu.VMEM((2, 2, SIDE, 2) + unit, bf16),
            pltpu.VMEM((2, SIDE, 2) + unit, f32),
            pltpu.VMEM((2, 2) + unit, bf16),
            pltpu.VMEM((2, 2) + unit, bf16),
            pltpu.VMEM((2, 2, 2) + unit, bf16),
            pltpu.VMEM((2, 2, 2) + unit, bf16),
            pltpu.VMEM((2, 2) + unit, f32),
        ]
        sems = []
        for dims in ((2, 4), (2, 2, SIDE), (2, 2, SIDE, 2), (2, 2), (2, 2, 2), (1,)):
            sems += [dma(dims), dma(dims)]
        return bufs, sems

    def copy(self, src, dst, stage, at, device):
        send, recv = self.sems[2 * stage], self.sems[2 * stage + 1]
        return remote(src, dst, send.at[at], recv.at[at], (device, self.z))

    def go(self, copy):
        copy.start()
        self.waits.append(copy)

    def spot(self, tau, di, j):
        if tau == 0:
            return side(self.y + di), j
        return j, side(self.x + di)

    def near(self, tau, axis, d):
        s = 1 - 2 * d
        if (tau == 0) == (axis == 0):
            return device_of(self.y + s, self.x, self.core)
        return device_of(self.y, self.x + s, self.core)

    def from_peer(self, tau, di):
        if tau == 0:
            at = (side(self.y + di), slice(None), 0)
        else:
            at = (slice(None), side(self.x + di), 1)
        return self.copy(
            self.slots.at[at], self.peer_slots.at[at], 0, (tau, di + 1), self.peer
        )

    def share(self):
        for di in (2, 1, -1, 0):
            for tau in (0, 1):

                @pl.loop(0, SIDE)
                def _(j):
                    yy, xx = self.spot(tau, di, j)
                    o = (yy * SIDE + xx) * 2 + tau
                    self.slots[yy, xx, tau] = self.packed[self.index[o], 1 - self.core]

                self.go(self.from_peer(tau, di))

    def term(self, tau, di, j, e):
        yy, xx = self.spot(tau, di, j)
        o = (yy * SIDE + xx) * 2 + tau
        times = self.packed.shape[-1] // self.entry.shape[1]
        mine = jnp.concatenate([self.entry[pl.ds(o, 1), :]] * times, axis=1)
        theirs = jnp.concatenate([self.peer_entry[pl.ds(o, 1), :]] * times, axis=1)
        a = self.packed[self.index[o], self.core].astype(jnp.float32)
        b = self.peer_slots[yy, xx, tau].astype(jnp.float32)
        return jnp.where(mine == e, a, 0.0) + jnp.where(theirs == e, b, 0.0)

    def first(self, tau, d, j):
        at = (tau, d, j)
        return self.copy(self.s1.at[at], self.r1.at[at], 1, at, self.near(tau, 0, d))

    def second(self, tau, d, j, e):
        at = (tau, d, j, e)
        return self.copy(self.s2.at[at], self.r2.at[at], 2, at, self.near(tau, 0, d))

    def third(self, tau, d):
        at = (tau, d)
        return self.copy(self.s3.at[at], self.r3.at[at], 3, at, self.near(tau, 1, d))

    def fourth(self, tau, d, e):
        at = (tau, d, e)
        return self.copy(self.s4.at[at], self.r4.at[at], 4, at, self.near(tau, 1, d))

    def send_first(self):
        for tau in (0, 1):
            self.from_peer(tau, 2).wait_recv()

            @pl.loop(0, SIDE)
            def _(j):
                for d in (0, 1):
                    self.s1[tau, d, j] = self.term(tau, 2, j, d).astype(self.s1.dtype)
                    self.first(tau, d, j).start()

    def send_second_free(self):
        for tau in (0, 1):
            for d in (0, 1):
                self.from_peer(tau, 1 - 2 * d).wait_recv()

            @pl.loop(0, SIDE)
            def _(j):
                for d in (0, 1):
                    value = self.term(tau, 1 - 2 * d, j, 1 - d)
                    self.s2[tau, d, j, 1 - d] = value.astype(self.s2.dtype)
                    self.second(tau, d, j, 1 - d).start()

    def send_second(self, tau):
        @pl.loop(0, SIDE)
        def _(j):
            for d in (0, 1):
                self.first(tau, d, j).wait_recv()
                value = self.term(tau, 1 - 2 * d, j, d) + self.r1[tau, d, j].astype(jnp.float32)
                self.s2[tau, d, j, d] = value.astype(self.s2.dtype)
                self.second(tau, d, j, d).start()

    def keep(self):
        for tau in (0, 1):
            self.from_peer(tau, 0).wait_recv()

            @pl.loop(0, SIDE)
            def _(j):
                for e in (0, 1):
                    self.acc[tau, j, e] = self.term(tau, 0, j, e)

    def total(self, tau, dj, e):
        j = side((self.x if tau == 0 else self.y) + dj)
        for d in (0, 1):
            self.second(tau, d, j, e).wait_recv()
        return (
            self.acc[tau, j, e]
            + self.r2[tau, 0, j, e].astype(jnp.float32)
            + self.r2[tau, 1, j, e].astype(jnp.float32)
        )

    def send_third(self):
        for tau in (0, 1):
            for d in (0, 1):
                self.s3[tau, d] = self.total(tau, 2, d).astype(self.s3.dtype)
                self.go(self.third(tau, d))

    def send_fourth_free(self):
        for tau in (0, 1):
            for d in (0, 1):
                value = self.total(tau, 1 - 2 * d, 1 - d)
                self.s4[tau, d, 1 - d] = value.astype(self.s4.dtype)
                self.go(self.fourth(tau, d, 1 - d))

    def send_fourth(self):
        for tau in (0, 1):
            for d in (0, 1):
                value = self.total(tau, 1 - 2 * d, d)
                self.third(tau, d).wait_recv()
                value += self.r3[tau, d].astype(jnp.float32)
                self.s4[tau, d, d] = value.astype(self.s4.dtype)
                self.go(self.fourth(tau, d, d))

    def finish(self):
        for tau in (0, 1):
            for e in (0, 1):
                value = self.total(tau, 0, e)
                for d in (0, 1):
                    self.fourth(tau, d, e).wait_recv()
                    value += self.r4[tau, d, e].astype(jnp.float32)
                self.res[tau, e] = value
        self.go(self.copy(
            self.res.at[1 - self.core], self.out.at[:, self.core], 5, 0, self.peer
        ))
        self.out[:, self.core] = self.res[self.core]

    def finished(self):
        self.copy(
            self.res.at[1 - self.core], self.out.at[:, 1 - self.core], 5, 0, self.peer
        ).wait_recv()

    def sent(self):
        for copy in self.waits:
            copy.wait_send()
        for tau in (0, 1):
            for d in (0, 1):

                @pl.loop(0, SIDE)
                def _(j):
                    self.first(tau, d, j).wait_send()
                    for e in (0, 1):
                        self.second(tau, d, j, e).wait_send()


REDUCE_BUFS, REDUCE_SEMS, SUM_REFS = 12, 12, 6


def scatter_kernel(
    index, owners, packed, entry, part, cotangent, beside, out_down, out_up, beyond, *rest
):
    rest = list(rest)

    def take(n):
        taken = rest[:n]
        del rest[:n]
        return taken

    peer_entry, lowered, packed_up = take(3)
    sum_refs = take(SUM_REFS)
    down_bufs, down_sems = take(REDUCE_BUFS), take(REDUCE_SEMS)
    up_bufs, up_sems = take(REDUCE_BUFS), take(REDUCE_SEMS)
    entry_send, entry_recv, cot_send, cot_recv = rest
    greet_neighbours()
    downs = PlaneReduce(index, packed, entry, peer_entry, out_down, down_bufs, down_sems)
    ups = PlaneReduce(index, packed_up, entry, peer_entry, out_up, up_bufs, up_sems)
    sums = RingSum(part, lowered, *sum_refs)
    rows = cotangent.shape[0]
    cots = CotangentRing(
        lambda step, d: beside.at[d] if step == 1 else beyond.at[2 * (step - 2) + d],
        lambda step, d: beyond.at[4] if step == 3 else beyond.at[2 * (step - 1) + d],
        cot_send, cot_recv, rows,
    )

    def cot_from_before(q):
        for d in (0, 1):
            here = pl.ds(q * cots.quarter, cots.quarter)
            copy = remote(
                beside.at[2 + d].at[here], beyond.at[2 + d].at[here], cot_send.at[2, d, q],
                cot_recv.at[2, d, q], (cots.me, ring(cots.z + 1 - 2 * d)),
            )
            copy.start()
            cots.copies.append(copy)

    sums.begin()
    entries = remote(entry, peer_entry, entry_send, entry_recv, (downs.peer, downs.z))
    entries.start()
    downs.share()
    for q in (2, 3):
        cots.launch(1, q, first=True)
    entries.wait_recv()
    downs.send_first()
    sums.step(1)
    downs.send_second_free()
    sums.step(2)
    downs.send_second(0)
    sums.step(3)
    downs.send_second(1)
    sums.total()
    downs.keep()
    sums.onward(1)
    for q in (0, 1):
        cot_from_before(q)
    sums.onward(2)
    sums.onward(3)
    sums.end()
    for q in (2, 3):
        cots.launch(2, q)

    segments = owners.shape[0]
    seg_rows, keys = rows // segments, cotangent.shape[1]
    ranks = 2 * HALF
    values = []
    for g in range(segments):
        both = lowered[g // 2].reshape(seg_rows, 2 * ranks)
        values.append(lax.dot_general(
            both[:, (g % 2) * ranks : (g % 2 + 1) * ranks],
            cotangent[g * seg_rows : (g + 1) * seg_rows, :],
            (((0,), (0,)), ((), ())),
            preferred_element_type=jnp.float32,
        ))
    for g in range(segments):
        value = values[g]
        for h in range(segments):
            if h != g:
                value = value + jnp.where(owners[h] == owners[g], values[h], 0.0)
        scaled = (value * (ADAPTER_SCALE / seg_rows)).astype(packed_up.dtype)
        packed_up[g] = scaled.reshape(packed_up.shape[1:])

    ups.share()
    downs.send_third()
    ups.send_first()
    downs.send_fourth_free()
    ups.send_second_free()
    downs.send_fourth()
    for tau in (0, 1):
        ups.send_second(tau)
    for q in range(4):
        cots.launch(3, q)
    ups.keep()
    ups.send_third()
    downs.finish()
    ups.send_fourth_free()
    ups.send_fourth()
    ups.finish()
    downs.finished()
    ups.finished()
    for q in range(4):
        cots.arrived(3, q)
    for q in (2, 3):
        for d in (0, 1):
            if q // 2 != d:
                cots.copy(2, d, q).wait_recv()
    for q in (0, 1):
        for d in (0, 1):
            if q // 2 != d:
                cots.copy(2, d, q).wait_recv()
    entries.wait_send()
    for each in (downs, ups, sums, cots):
        each.sent()


def scatter_gradients(index, owners, packed, entry, part, cotangent, beside):
    down_unit = packed.shape[2:]
    up_unit = (HALF, cotangent.shape[1])
    bf16, f32 = jnp.bfloat16, jnp.float32
    dma = pltpu.SemaphoreType.DMA
    scalars = pl.BlockSpec(memory_space=pltpu.SMEM)
    whole = pl.BlockSpec(memory_space=pltpu.VMEM)
    anywhere = pl.BlockSpec(memory_space=pl.ANY)
    down_bufs, down_sems = PlaneReduce.scratch(down_unit)
    up_bufs, up_sems = PlaneReduce.scratch(up_unit)
    return pl.pallas_call(
        scatter_kernel,
        out_shape=(
            jax.ShapeDtypeStruct((2, 2) + down_unit, f32),
            jax.ShapeDtypeStruct((2, 2) + up_unit, f32),
            jax.ShapeDtypeStruct((5,) + beside.shape[1:], bf16),
        ),
        in_specs=[scalars, scalars, whole, whole, whole, whole, anywhere],
        out_specs=(whole, whole, anywhere),
        scratch_shapes=[
            pltpu.VMEM(entry.shape, f32),
            pltpu.VMEM(part.shape, bf16),
            pltpu.VMEM((packed.shape[0], 2) + up_unit, bf16),
        ]
        + ring_sum_scratch(part.shape)
        + down_bufs + down_sems + up_bufs + up_sems
        + [dma(()), dma(()), dma((4, 2, 4)), dma((4, 2, 4))],
        compiler_params=pltpu.CompilerParams(
            collective_id=1, has_side_effects=True, vmem_limit_bytes=30 * MIB
        ),
        name="scatter_gradients",
    )(index, owners, packed, entry, part, cotangent, beside)


def tokens_kernel(
    places, live, cotangent, beside, beyond, frozen, pulled, maps, out, tiles, sems
):
    segments = places.shape[0]
    width, keys = out.shape[1], cotangent.shape[1]
    rows = out.shape[0] // segments
    ranks = 2 * HALF
    z = lax.axis_index("tsp")
    block = tiles.shape[1]
    steps = out.shape[0] // block
    row = lax.broadcasted_iota(jnp.int32, (rows, width), 0)
    offsets = (0, -1, 1, -2, 2, -3, 3, 4)
    weights = jnp.concatenate(
        [frozen[:, pl.ds(pl.multiple_of(ring(z + r) * keys, keys), keys)] for r in offsets],
        axis=1,
    )

    def store(b):
        return pltpu.make_async_copy(
            tiles.at[lax.rem(b, 2)], out.at[pl.ds(b * block, block)], sems.at[lax.rem(b, 2)]
        )

    for half in (0, 1):
        second = (beside, 2) if half == 0 else (beyond, 0)
        third = (beside, 3) if half == 0 else (beyond, 1)
        parts = (
            (beside, 0), (beside, 1), second, third, (beyond, 2), (beyond, 3), (beyond, 4)
        )

        @pl.loop(half * steps // 2, (half + 1) * steps // 2)
        def _(b):
            @pl.when(b >= 2)
            def _():
                store(b - 2).wait()

            here = pl.ds(pl.multiple_of(b * block, block), block)
            left = jnp.concatenate(
                [cotangent[here, :]] + [ref[k, here, :] for ref, k in parts], axis=1
            )
            value = lax.dot_general(
                left, weights, (((1,), (1,)), ((), ())), preferred_element_type=jnp.float32
            )
            for k in range(2):
                g = 2 * b + k
                both = pulled[b].reshape(rows, 2 * ranks)
                extra = jnp.dot(
                    both[:, k * ranks : (k + 1) * ranks], maps[places[g]].reshape(ranks, width),
                    preferred_element_type=jnp.float32,
                )
                total = value[k * rows : (k + 1) * rows] + ADAPTER_SCALE * extra
                tiles[lax.rem(b, 2), k * rows : (k + 1) * rows] = jnp.where(
                    row < live[g], total, 0.0
                ).astype(out.dtype)
            store(b).start()

    for b in (steps - 2, steps - 1):
        store(b).wait()


def token_gradients(places, live, cotangent, beside, beyond, frozen, pulled, maps):
    segments = places.shape[0]
    rows, width = cotangent.shape[0] // segments, frozen.shape[0]
    scalars = pl.BlockSpec(memory_space=pltpu.SMEM)
    whole = pl.BlockSpec(memory_space=pltpu.VMEM)
    return pl.pallas_call(
        tokens_kernel,
        out_shape=jax.ShapeDtypeStruct((segments * rows, width), jnp.bfloat16),
        in_specs=[scalars, scalars] + [whole] * 6,
        out_specs=pl.BlockSpec(memory_space=pl.ANY),
        scratch_shapes=[
            pltpu.VMEM((2, 2 * rows, width), jnp.bfloat16),
            pltpu.SemaphoreType.DMA((2,)),
        ],
        compiler_params=pltpu.CompilerParams(vmem_limit_bytes=28 * MIB),
        name="token_gradients",
    )(places, live, cotangent, beside, beyond, frozen, pulled, maps)


def on_device(
    tokens,
    cotangent,
    frozen_key_weight,
    adapter_down_weight,
    adapter_up_weight,
    adapter_place_table,
    segment_adapter,
    segment_live_count,
):
    dp_count = lax.axis_size("dp")
    held, ranks, width = adapter_down_weight.shape
    keys = cotangent.shape[1]
    live = segment_live_count
    places = lookup(segment_adapter, adapter_place_table)
    owners = places // held
    segment = jnp.arange(places.shape[0], dtype=jnp.int32)
    same = owners[:, None] == owners[None, :]
    heads = jnp.min(jnp.where(same, segment[None, :], places.shape[0]), axis=1)
    owner_hit = owners[:, None] == jnp.arange(dp_count, dtype=jnp.int32)[None, :]
    wanted = jnp.max(jnp.where(owner_hit, (places % held)[:, None], -1), axis=0)
    index = jnp.max(jnp.where(owner_hit, heads[:, None], 0), axis=0)
    entry = jnp.broadcast_to(wanted.astype(jnp.float32)[:, None], (dp_count, 128))
    far = lambda array: pltpu.with_memory_space_constraint(array, pltpu.HBM)
    maps, pulled, tokens_here, cotangent_here, beside = gather_maps(
        places, live,
        far(adapter_down_weight.reshape(held, 2, HALF, width)),
        far(adapter_up_weight.reshape(held, 2, HALF, keys)),
        far(tokens), far(cotangent),
    )
    part, packed = between(places, live, heads, tokens_here, maps, pulled)
    down_grad, up_grad, beyond = scatter_gradients(
        index, owners, packed, entry, part, cotangent_here, beside
    )
    token_gradient = token_gradients(
        places, live, cotangent_here, beside, beyond, frozen_key_weight, pulled, maps
    )
    return (
        token_gradient,
        down_grad.reshape(held, ranks, width),
        up_grad.reshape(held, ranks, keys),
    )


def solution(mesh):
    placed = (
        P("dp", "tsp"),
        P("dp", "tsp"),
        P("tsp", None),
        P("dp", None, "tsp"),
        P("dp", None, "tsp"),
        P(),
        P("dp"),
        P("dp"),
    )
    return jax.shard_map(
        on_device,
        mesh=mesh,
        in_specs=placed,
        out_specs=(P("dp", "tsp"), P("dp", None, "tsp"), P("dp", None, "tsp")),
        check_vma=False,
    )
```

time: 472 us -> 130 us (0.28)
  waiting for transfers between devices: 364 us -> 0 us
  Pallas kernels: 0 us -> 126 us
  matrix products: 35.8 us -> 0 us
  other arithmetic: 17.2 us -> 1.15 us
  blocking collectives: 15.3 us -> 0 us
  local copies, waits for them, and re-layouts: 15.6 us -> 2.16 us
  between operations: 13.9 us -> 0.71 us
  starting transfers between devices: 9.6 us -> 0 us
    reduce_scatter x2 -> x0, waiting for transfers between devices: 208 us -> none  [the longest x1 127 us: on_device(): lax.psum_scatter(dense_down, 'dp', scatter_dimension=0, tiled=True)]
    pallas_call x0 -> x4, Pallas kernels: none -> 126 us  [the longest x1 57.6 us: scatter_gradients(): pl.pallas_call(scatter_kernel, out_shape=(jax.ShapeDtypeStruct((2, 2) + d...]
    psum x1 -> x0, waiting for transfers between devices: 71.8 us -> none  [on_device(): summed = lax.psum(partial_terms, 'tsp')]
    all_to_all x2 -> x0, waiting for transfers between devices: 54.5 us -> none  [the longest x1 49.6 us: on_device(): lax.all_to_all(reply_down, 'dp', split_axis=0, concat_axis=0, tiled=True)]
    dot_general x12 -> x0, matrix products: 35.8 us -> none  [the longest x1 6.88 us: on_device(): jnp.einsum('go,ord->grd', picker, fetched_down, preferred_element_type=jn...]
    all_gather x1 -> x0, waiting for transfers between devices: 29 us -> none  [on_device(): lax.all_gather(cotangent, 'tsp', axis=1, tiled=True)]
    all_to_all x1 -> x0, blocking collectives: 15.3 us -> none  [on_device(): lax.all_to_all(wanted[:, None], 'dp', split_axis=0, concat_axis=0, tiled=...]
    select_n x3 -> x1, other arithmetic: 14.1 us -> 0.01 us  [on_device(): owners = places // held]
  transfers between devices with their start and end apart: 6 -> 0, of which waited for: 6 -> 0; matrix products, arithmetic and copies ran while one was open for 11% -> 0% of each run, Pallas kernels for 0% -> 0%
where the time goes in v3:
time: 130 us
  Pallas kernels  126 us (97%)
  local copies, waits for them, and re-layouts  2.16 us (2%)
    pallas_call x1, Pallas kernels, scatter_gradients(): pl.pallas_call(scatter_kernel, out_shape=(jax.ShapeDtypeStruct((2, 2) + d...  57.6 us
    pallas_call x1, Pallas kernels, gather_maps(): pl.pallas_call(gather_kernel, out_shape=(jax.ShapeDtypeStruct((count,) +...  56.7 us
    pallas_call x1, Pallas kernels, token_gradients(): pl.pallas_call(tokens_kernel, out_shape=jax.ShapeDtypeStruct((segments *...  8.97 us
    pallas_call x1, Pallas kernels, between(): pl.pallas_call(between_kernel, out_shape=(jax.ShapeDtypeStruct(pulled.sha...  2.79 us

profile of v3, /device:TPU:1, one launch (start us, length us, event | category | flops | bytes accessed | tf_op | source)
XLA Modules:
  0.0 130.1 jit_solution(7034599973450230703)
XLA Ops:
  0.6 0.0 copy-start.2
  0.6 0.9 select_reduce_fusion.3.places
  1.5 0.2 select_reduce_fusion.2.heads
  1.7 0.1 select_reduce_fusion
  1.8 0.1 broadcast_in_dim.68.entry
  1.9 0.0 copy-start.1
  1.9 0.7 copy-done.1
  2.5 56.7 %gather_maps.1 = (bf16[64,2,32,1024]{3,2,1,0:T(8,128)(2,1)S(1)}, bf16[8,2,64,128]{3,2,1,0:T(8,128)(2,1)S(1)}, bf16[2048,1024]{1,0:T(8,128)(2,1)S(1)}, bf16[2048,...) custom-call(s32[16]{0:T(128)S(1)} %select_reduce_fusion.3.places, s32[16]{0:T(128)S(1)} %copy-done.1, ...), custom_call_target="tpu_custom_call" | custom-call | tf_op jit(solution)/shard_map/gather_maps/pallas_call | solution.py:391
  59.3 0.0 copy-done.2
  59.3 2.8 %between.1 = (f32[8,2,64,128]{3,2,1,0:T(8,128)S(1)}, bf16[16,2,32,1024]{3,2,1,0:T(8,128)(2,1)S(1)}) custom-call(s32[16]{0:T(128)S(1)} %select_reduce_fusion.3.places, s32[16]{0:T(128)S(1)} %copy-done.2, s32[16]{0:T(128)S(1)} %select_reduce_fusion.2.heads, bf16[2048,1024]{1,0:T(8,128)(2,1)S(1)} %get-tuple-element.15.tokens, ...), custom_call_target="tpu_custom_call" | custom-call | tf_op jit(solution)/shard_map/between/pallas_call | solution.py:448
  62.1 0.0 copy-start
  62.1 57.6 %scatter_gradients.1 = (f32[2,2,32,1024]{3,2,1,0:T(8,128)S(1)}, f32[2,2,32,128]{3,2,1,0:T(8,128)S(1)}, bf16[5,2048,128]{2,1,0:T(8,128)(2,1)S(1)}) custom-call(s32[32]{0:T(128)S(1)} %get-tuple-element.24.index, s32[16]{0:T(128)S(1)} %get-tuple-element.25.owners, bf16[16,2,32,1024]{3,2,1,0:T(8,128)(2,1)S(1)} %get-tuple-element.18.packed, ...), custom_call_target="tpu_custom_call" | custom-call | tf_op jit(solution)/shard_map/scatter_gradients/pallas_call | solution.py:795
  119.7 0.0 copy-done
  119.7 9.0 %token_gradients.1 = bf16[2048,1024]{1,0:T(8,128)(2,1)} custom-call(s32[16]{0:T(128)S(1)} %select_reduce_fusion.3.places, s32[16]{0:T(128)S(1)} %copy-done.2, bf16[2048,128]{1,0:T(8,128)(2,1)S(1)} %get-tuple-element.13.cotangent, bf16[4,2048,128]{2,1,0:T(8,128)(2,1)S(1)} %get-tuple-element.14.beside, bf16[5,2048,128]{2,1,0:T(8,128)(2,1)S(1)} %get-tuple-element.20.beyond, ...), custom_call_target="tpu_custom_call" | custom-call | tf_op jit(solution)/shard_map/token_gradients/pallas_call | solution.py:883
  128.7 0.8 copy.13
  129.5 0.6 copy.14
  (2 shorter events, 0.0 us)
Async XLA Ops:
  0.6 58.6 %copy-start.2 = (s32[16]{0:T(128)S(1)}, s32[16]{0:T(128)}, u32[]{:S(2)}) copy-start(s32[16]{0:T(128)} %live.5) | copy-start | bytes 196
  1.9 0.7 copy-start.1
  62.1 57.6 %copy-start = (bf16[1024,1024]{1,0:T(8,128)(2,1)S(1)}, bf16[1024,1024]{1,0:T(8,128)(2,1)}, u32[]{:S(2)}) copy-start(bf16[1024,1024]{1,0:T(8,128)(2,1)} %frozen.1) | copy-start | bytes 6291460

commit v4 on v3

--- a/solution.py
+++ b/solution.py
@@ -257,39 +257,50 @@
 
 
 class CotangentRing:
-    def __init__(self, source, target, send_sem, recv_sem, rows):
+    eighths = 8
+
+    def __init__(self, source, target, send_sem, recv_sem, rows, steps):
         self.me, self.z = lax.axis_index("dp"), lax.axis_index("tsp")
         self.source, self.target = source, target
         self.send_sem, self.recv_sem = send_sem, recv_sem
-        self.quarter = rows // 4
+        self.size = rows // self.eighths
         self.copies = []
+        self.origin = steps[0]
+        self.queue, self.waited = [], set()
+        for step in steps:
+            for k in range(self.eighths if step < 3 else self.eighths // 2):
+                pieces = [(step, 0, k), (step, 1, k if step < 3 else k + self.eighths // 2)]
+                self.queue.append(pieces)
 
     def copy(self, step, d, q):
-        here = pl.ds(q * self.quarter, self.quarter)
+        here = pl.ds(q * self.size, self.size)
         src, dst = self.source(step, d), self.target(step, d)
+        at = (step - self.origin, d, q)
         return remote(
-            src.at[here], dst.at[here], self.send_sem.at[step, d, q],
-            self.recv_sem.at[step, d, q], (self.me, ring(self.z + 1 - 2 * d)),
+            src.at[here], dst.at[here], self.send_sem.at[at], self.recv_sem.at[at],
+            (self.me, ring(self.z + 1 - 2 * d)),
         )
 
-    def launch(self, step, q, first=False):
-        for d in (0, 1):
-            if step == 3 and q // 2 != d:
-                continue
-            if not first:
-                self.copy(step - 1, d, q).wait_recv()
-            copy = self.copy(step, d, q)
-            copy.start()
-            self.copies.append(copy)
-
-    def arrived(self, step, q):
-        for d in (0, 1):
-            if step == 3 and q // 2 != d:
-                continue
+    def wait(self, step, d, q):
+        if step >= self.origin and (step, d, q) not in self.waited:
+            self.waited.add((step, d, q))
             self.copy(step, d, q).wait_recv()
 
+    def launch(self, count=1):
+        for pieces in self.queue[:count]:
+            for step, d, q in pieces:
+                self.wait(step - 1, d, q)
+                copy = self.copy(step, d, q)
+                copy.start()
+                self.copies.append((copy, (step, d, q)))
+        self.queue = self.queue[count:]
+
+    def arrived(self):
+        for _, piece in self.copies:
+            self.wait(*piece)
+
     def sent(self):
-        for copy in self.copies:
+        for copy, _ in self.copies:
             copy.wait_send()
 
 
@@ -304,9 +315,9 @@
     ups = PlaneGather(up, up_maps, local_sem.at[1], up_send, up_recv)
     sums = RingSum(part, pulled, held, passed, send_sem, recv_sem, out_send, out_recv)
     cots = CotangentRing(
-        lambda step, d: cotangent if step == 0 else beside.at[2 * (step - 1) + d],
+        lambda step, d: cotangent if step == 0 else beside.at[d],
         lambda step, d: beside.at[2 * step + d],
-        cot_send, cot_recv, cotangent.shape[0],
+        cot_send, cot_recv, cotangent.shape[0], (0, 1),
     )
     ups.own()
     downs.own()
@@ -314,22 +325,19 @@
     cotangent_copy.start()
     tokens_copy = pltpu.make_async_copy(tokens, tokens_here, local_sem.at[3])
     tokens_copy.start()
+    cots.launch(6)
     ups.own_arrived()
     ups.one()
     ups.two(0)
+    ups.one_arrived()
     downs.own_arrived()
     downs.one()
-    for q in range(4):
-        cots.launch(0, q, first=True)
-    ups.one_arrived()
-    downs.two(0)
     ups.onward_arrived()
-    downs.one_arrived()
     for di in NEAR:
         ups.two_arrived(di)
+    downs.two(0)
     for di in NEAR:
         ups.last_arrived(di)
-    downs.onward_arrived()
     ups.swaps_arrived()
     cotangent_copy.wait()
 
@@ -349,30 +357,35 @@
             pair.append(jnp.where(row < live[g], term, 0.0))
         part[j] = jnp.concatenate(pair, axis=1).reshape(part.shape[1:])
     sums.begin()
+    cots.launch()
+    downs.one_arrived()
     sums.step(1)
+    cots.launch()
     downs.two_arrived(0)
+    downs.onward_arrived()
     sums.step(2)
+    cots.launch()
+    sums.step(3)
+    cots.launch()
     downs.two_arrived(-1)
-    sums.step(3)
+    sums.total()
+    cots.launch()
     downs.two_arrived(1)
-    sums.total()
-    cots.launch(1, 0)
+    sums.onward(1)
+    cots.launch()
     downs.two_arrived(2)
-    sums.onward(1)
+    sums.onward(2)
+    cots.launch()
     downs.last_arrived(0)
-    cots.launch(1, 1)
     downs.last_arrived(-1)
-    sums.onward(2)
+    sums.onward(3)
+    cots.launch(3)
     downs.last_arrived(1)
     downs.last_arrived(2)
-    sums.onward(3)
     sums.end()
     downs.swaps_arrived()
     tokens_copy.wait()
-    for q in (2, 3):
-        cots.arrived(0, q)
-    for q in (0, 1):
-        cots.arrived(1, q)
+    cots.arrived()
     for each in (ups, downs, sums, cots):
         each.sent()
 
@@ -403,7 +416,7 @@
         + ring_sum_scratch(part)
         + [dma((4,))]
         + [dma((PlaneGather.copies,)) for _ in range(4)]
-        + [dma((2, 2, 4)), dma((2, 2, 4))],
+        + [dma((2, 2, CotangentRing.eighths)), dma((2, 2, CotangentRing.eighths))],
         compiler_params=pltpu.CompilerParams(
             collective_id=0, has_side_effects=True, vmem_limit_bytes=12 * MIB
         ),
@@ -689,45 +702,36 @@
     sums = RingSum(part, lowered, *sum_refs)
     rows = cotangent.shape[0]
     cots = CotangentRing(
-        lambda step, d: beside.at[d] if step == 1 else beyond.at[2 * (step - 2) + d],
-        lambda step, d: beyond.at[4] if step == 3 else beyond.at[2 * (step - 1) + d],
-        cot_send, cot_recv, rows,
+        lambda step, d: beside.at[2 + d] if step == 2 else beyond.at[d],
+        lambda step, d: beyond.at[d if step == 2 else 2],
+        cot_send, cot_recv, rows, (2, 3),
     )
-
-    def cot_from_before(q):
-        for d in (0, 1):
-            here = pl.ds(q * cots.quarter, cots.quarter)
-            copy = remote(
-                beside.at[2 + d].at[here], beyond.at[2 + d].at[here], cot_send.at[2, d, q],
-                cot_recv.at[2, d, q], (cots.me, ring(cots.z + 1 - 2 * d)),
-            )
-            copy.start()
-            cots.copies.append(copy)
-
     sums.begin()
     entries = remote(entry, peer_entry, entry_send, entry_recv, (downs.peer, downs.z))
     entries.start()
+    cots.launch()
     downs.share()
-    for q in (2, 3):
-        cots.launch(1, q, first=True)
+    sums.step(1)
+    cots.launch()
     entries.wait_recv()
     downs.send_first()
-    sums.step(1)
+    sums.step(2)
+    cots.launch()
     downs.send_second_free()
-    sums.step(2)
+    sums.step(3)
+    cots.launch()
+    sums.total()
+    cots.launch()
     downs.send_second(0)
-    sums.step(3)
+    sums.onward(1)
+    cots.launch()
     downs.send_second(1)
-    sums.total()
+    sums.onward(2)
+    cots.launch()
     downs.keep()
-    sums.onward(1)
-    for q in (0, 1):
-        cot_from_before(q)
-    sums.onward(2)
     sums.onward(3)
+    cots.launch()
     sums.end()
-    for q in (2, 3):
-        cots.launch(2, q)
 
     segments = owners.shape[0]
     seg_rows, keys = rows // segments, cotangent.shape[1]
@@ -750,33 +754,23 @@
         packed_up[g] = scaled.reshape(packed_up.shape[1:])
 
     ups.share()
-    downs.send_third()
     ups.send_first()
-    downs.send_fourth_free()
     ups.send_second_free()
-    downs.send_fourth()
+    cots.launch(4)
+    ups.keep()
     for tau in (0, 1):
         ups.send_second(tau)
-    for q in range(4):
-        cots.launch(3, q)
-    ups.keep()
+    downs.send_third()
     ups.send_third()
+    ups.send_fourth_free()
+    downs.send_fourth_free()
+    ups.send_fourth()
+    downs.send_fourth()
+    ups.finish()
     downs.finish()
-    ups.send_fourth_free()
-    ups.send_fourth()
-    ups.finish()
+    ups.finished()
     downs.finished()
-    ups.finished()
-    for q in range(4):
-        cots.arrived(3, q)
-    for q in (2, 3):
-        for d in (0, 1):
-            if q // 2 != d:
-                cots.copy(2, d, q).wait_recv()
-    for q in (0, 1):
-        for d in (0, 1):
-            if q // 2 != d:
-                cots.copy(2, d, q).wait_recv()
+    cots.arrived()
     entries.wait_send()
     for each in (downs, ups, sums, cots):
         each.sent()
@@ -797,7 +791,7 @@
         out_shape=(
             jax.ShapeDtypeStruct((2, 2) + down_unit, f32),
             jax.ShapeDtypeStruct((2, 2) + up_unit, f32),
-            jax.ShapeDtypeStruct((5,) + beside.shape[1:], bf16),
+            jax.ShapeDtypeStruct((3,) + beside.shape[1:], bf16),
         ),
         in_specs=[scalars, scalars, whole, whole, whole, whole, anywhere],
         out_specs=(whole, whole, anywhere),
@@ -808,7 +802,7 @@
         ]
         + ring_sum_scratch(part.shape)
         + down_bufs + down_sems + up_bufs + up_sems
-        + [dma(()), dma(()), dma((4, 2, 4)), dma((4, 2, 4))],
+        + [dma(()), dma(()), dma((2, 2, CotangentRing.eighths)), dma((2, 2, CotangentRing.eighths))],
         compiler_params=pltpu.CompilerParams(
             collective_id=1, has_side_effects=True, vmem_limit_bytes=30 * MIB
         ),
@@ -838,38 +832,35 @@
             tiles.at[lax.rem(b, 2)], out.at[pl.ds(b * block, block)], sems.at[lax.rem(b, 2)]
         )
 
-    for half in (0, 1):
-        second = (beside, 2) if half == 0 else (beyond, 0)
-        third = (beside, 3) if half == 0 else (beyond, 1)
-        parts = (
-            (beside, 0), (beside, 1), second, third, (beyond, 2), (beyond, 3), (beyond, 4)
+    parts = (
+        (beside, 0), (beside, 1), (beside, 2), (beside, 3), (beyond, 0), (beyond, 1), (beyond, 2)
+    )
+
+    @pl.loop(0, steps)
+    def _(b):
+        @pl.when(b >= 2)
+        def _():
+            store(b - 2).wait()
+
+        here = pl.ds(pl.multiple_of(b * block, block), block)
+        left = jnp.concatenate(
+            [cotangent[here, :]] + [ref[k, here, :] for ref, k in parts], axis=1
         )
-
-        @pl.loop(half * steps // 2, (half + 1) * steps // 2)
-        def _(b):
-            @pl.when(b >= 2)
-            def _():
-                store(b - 2).wait()
-
-            here = pl.ds(pl.multiple_of(b * block, block), block)
-            left = jnp.concatenate(
-                [cotangent[here, :]] + [ref[k, here, :] for ref, k in parts], axis=1
+        value = lax.dot_general(
+            left, weights, (((1,), (1,)), ((), ())), preferred_element_type=jnp.float32
+        )
+        for k in range(2):
+            g = 2 * b + k
+            both = pulled[b].reshape(rows, 2 * ranks)
+            extra = jnp.dot(
+                both[:, k * ranks : (k + 1) * ranks], maps[places[g]].reshape(ranks, width),
+                preferred_element_type=jnp.float32,
             )
-            value = lax.dot_general(
-                left, weights, (((1,), (1,)), ((), ())), preferred_element_type=jnp.float32
-            )
-            for k in range(2):
-                g = 2 * b + k
-                both = pulled[b].reshape(rows, 2 * ranks)
-                extra = jnp.dot(
-                    both[:, k * ranks : (k + 1) * ranks], maps[places[g]].reshape(ranks, width),
-                    preferred_element_type=jnp.float32,
-                )
-                total = value[k * rows : (k + 1) * rows] + ADAPTER_SCALE * extra
-                tiles[lax.rem(b, 2), k * rows : (k + 1) * rows] = jnp.where(
-                    row < live[g], total, 0.0
-                ).astype(out.dtype)
-            store(b).start()
+            total = value[k * rows : (k + 1) * rows] + ADAPTER_SCALE * extra
+            tiles[lax.rem(b, 2), k * rows : (k + 1) * rows] = jnp.where(
+                row < live[g], total, 0.0
+            ).astype(out.dtype)
+        store(b).start()
 
     for b in (steps - 2, steps - 1):
         store(b).wait()

time: 130 us -> 125 us (0.962)
  Pallas kernels: 126 us -> 121 us
    pallas_call x1, Pallas kernels: 57.6 us -> 52.8 us  [scatter_gradients(): pl.pallas_call(scatter_kernel, out_shape=(jax.ShapeDtypeStruct((2, 2) + d...]
where the time goes in v4:
time: 125 us
  Pallas kernels  121 us (97%)
  local copies, waits for them, and re-layouts  2.16 us (2%)
    pallas_call x1, Pallas kernels, gather_maps(): pl.pallas_call(gather_kernel, out_shape=(jax.ShapeDtypeStruct((count,) +...  55.9 us
    pallas_call x1, Pallas kernels, scatter_gradients(): pl.pallas_call(scatter_kernel, out_shape=(jax.ShapeDtypeStruct((2, 2) + d...  52.8 us
    pallas_call x1, Pallas kernels, token_gradients(): pl.pallas_call(tokens_kernel, out_shape=jax.ShapeDtypeStruct((segments *...  9.04 us
    pallas_call x1, Pallas kernels, between(): pl.pallas_call(between_kernel, out_shape=(jax.ShapeDtypeStruct(pulled.sha...  2.8 us

profile of v4, /device:TPU:1, one launch (start us, length us, event | category | flops | bytes accessed | tf_op | source)
XLA Modules:
  0.0 124.5 jit_solution(4241159643950938433)
XLA Ops:
  0.6 0.0 copy-start.2
  0.6 0.9 select_reduce_fusion.3.places
  1.5 0.0 copy-start.1
  1.5 0.7 copy-done.1
  2.2 55.9 %gather_maps.1 = (bf16[64,2,32,1024]{3,2,1,0:T(8,128)(2,1)S(1)}, bf16[8,2,64,128]{3,2,1,0:T(8,128)(2,1)S(1)}, bf16[2048,1024]{1,0:T(8,128)(2,1)S(1)}, bf16[2048,...) custom-call(s32[16]{0:T(128)S(1)} %select_reduce_fusion.3.places, s32[16]{0:T(128)S(1)} %copy-done.1, ...), custom_call_target="tpu_custom_call" | custom-call | tf_op jit(solution)/shard_map/gather_maps/pallas_call | solution.py:404
  58.1 0.2 select_reduce_fusion.2.heads
  58.3 0.0 copy-done.2
  58.3 2.8 %between.1 = (f32[8,2,64,128]{3,2,1,0:T(8,128)S(1)}, bf16[16,2,32,1024]{3,2,1,0:T(8,128)(2,1)S(1)}) custom-call(s32[16]{0:T(128)S(1)} %select_reduce_fusion.3.places, s32[16]{0:T(128)S(1)} %copy-done.2, s32[16]{0:T(128)S(1)} %select_reduce_fusion.2.heads, bf16[2048,1024]{1,0:T(8,128)(2,1)S(1)} %get-tuple-element.15.tokens, ...), custom_call_target="tpu_custom_call" | custom-call | tf_op jit(solution)/shard_map/between/pallas_call | solution.py:461
  61.1 0.0 copy-start
  61.1 0.1 select_reduce_fusion
  61.2 0.1 broadcast_in_dim.68.entry
  61.3 52.8 %scatter_gradients.1 = (f32[2,2,32,1024]{3,2,1,0:T(8,128)S(1)}, f32[2,2,32,128]{3,2,1,0:T(8,128)S(1)}, bf16[3,2048,128]{2,1,0:T(8,128)(2,1)S(1)}) custom-call(s32[32]{0:T(128)S(1)} %get-tuple-element.24.index, s32[16]{0:T(128)S(1)} %get-tuple-element.25.owners, bf16[16,2,32,1024]{3,2,1,0:T(8,128)(2,1)S(1)} %get-tuple-element.18.packed, ...), custom_call_target="tpu_custom_call" | custom-call | tf_op jit(solution)/shard_map/scatter_gradients/pallas_call | solution.py:789
  114.1 0.0 copy-done
  114.1 9.0 %token_gradients.1 = bf16[2048,1024]{1,0:T(8,128)(2,1)} custom-call(s32[16]{0:T(128)S(1)} %select_reduce_fusion.3.places, s32[16]{0:T(128)S(1)} %copy-done.2, bf16[2048,128]{1,0:T(8,128)(2,1)S(1)} %get-tuple-element.13.cotangent, bf16[4,2048,128]{2,1,0:T(8,128)(2,1)S(1)} %get-tuple-element.14.beside, bf16[3,2048,128]{2,1,0:T(8,128)(2,1)S(1)} %get-tuple-element.20.beyond, ...), custom_call_target="tpu_custom_call" | custom-call | tf_op jit(solution)/shard_map/token_gradients/pallas_call | solution.py:874
  123.1 0.8 copy.13
  123.9 0.6 copy.14
  (2 shorter events, 0.0 us)
Async XLA Ops:
  0.6 57.7 %copy-start.2 = (s32[16]{0:T(128)S(1)}, s32[16]{0:T(128)}, u32[]{:S(2)}) copy-start(s32[16]{0:T(128)} %live.5) | copy-start | bytes 196
  1.5 0.7 copy-start.1
  61.1 53.0 %copy-start = (bf16[1024,1024]{1,0:T(8,128)(2,1)S(1)}, bf16[1024,1024]{1,0:T(8,128)(2,1)}, u32[]{:S(2)}) copy-start(bf16[1024,1024]{1,0:T(8,128)(2,1)} %frozen.1) | copy-start | bytes 6291460

commit v5 on v4

--- a/solution.py
+++ b/solution.py
@@ -12,6 +12,9 @@
 HALF = 32
 MIB = 1024 * 1024
 NEAR = (0, -1, 1, 2)
+CHIPS = sorted(
+    ((dy, dx) for dy in NEAR for dx in NEAR if dy or dx), key=lambda at: -abs(at[0]) - abs(at[1])
+)
 
 
 def lookup(idents, mapping):
@@ -41,15 +44,8 @@
 def greet_neighbours():
     me, core, y, x = place_in_plane()
     z = lax.axis_index("tsp")
-    devices = [
-        (me + 1 - 2 * core, z),
-        (device_of(y, x + 1, core), z),
-        (device_of(y, x - 1, core), z),
-        (device_of(y + 1, x, core), z),
-        (device_of(y - 1, x, core), z),
-        (me, ring(z + 1)),
-        (me, ring(z - 1)),
-    ]
+    devices = [(me + 1 - 2 * core, z), (me, ring(z + 1)), (me, ring(z - 1))]
+    devices += [(device_of(y + dy, x + dx, core), z) for dy, dx in CHIPS]
     barrier = pltpu.get_barrier_semaphore()
     for device in devices:
         pl.semaphore_signal(barrier, inc=1, device_id=device, device_id_type=MESH)
@@ -166,6 +162,55 @@
                 for dj in NEAR:
                     if di or dj:
                         self.arrived(self.block(tau, di, dj, 1 - self.core), ("swap", tau, di, dj))
+
+    def sent(self):
+        for copy in self.sends:
+            copy.wait_send()
+
+
+class DirectGather:
+    copies = 2 * len(CHIPS) + 1
+
+    def __init__(self, mine, out, local_sem, send_sem, recv_sem):
+        self.me, self.core, self.y, self.x = place_in_plane()
+        self.z = lax.axis_index("tsp")
+        self.peer = self.me + 1 - 2 * self.core
+        self.mine, self.out = mine, out
+        self.local_sem, self.send_sem, self.recv_sem = local_sem, send_sem, recv_sem
+        self.sends = []
+
+    def block(self, device):
+        return self.out.at[pl.ds(2 * device, 2)]
+
+    def copy(self, src, dst, device, k):
+        return remote(src, dst, self.send_sem.at[k], self.recv_sem.at[k], (device, self.z))
+
+    def send(self, src, dst, device, k):
+        copy = self.copy(src, dst, device, k)
+        copy.start()
+        self.sends.append(copy)
+
+    def own(self):
+        here = self.block(self.me)
+        for k, (dy, dx) in enumerate(CHIPS):
+            self.send(self.mine, here, device_of(self.y + dy, self.x + dx, self.core), k)
+        self.send(self.mine, here, self.peer, 2 * len(CHIPS))
+        self.local = pltpu.make_async_copy(self.mine, here, self.local_sem)
+        self.local.start()
+
+    def pass_across(self):
+        for k, (dy, dx) in reversed(list(enumerate(CHIPS))):
+            block = self.block(device_of(self.y - dy, self.x - dx, self.core))
+            self.copy(block, block, self.peer, k).wait_recv()
+            self.send(block, block, self.peer, len(CHIPS) + k)
+
+    def arrived(self):
+        self.local.wait()
+        block = self.block(self.peer)
+        self.copy(block, block, self.peer, 2 * len(CHIPS)).wait_recv()
+        for k, (dy, dx) in reversed(list(enumerate(CHIPS))):
+            block = self.block(device_of(self.y - dy, self.x - dx, 1 - self.core))
+            self.copy(block, block, self.peer, len(CHIPS) + k).wait_recv()
 
     def sent(self):
         for copy in self.sends:
@@ -312,7 +357,7 @@
 ):
     greet_neighbours()
     downs = PlaneGather(down, down_maps, local_sem.at[0], down_send, down_recv)
-    ups = PlaneGather(up, up_maps, local_sem.at[1], up_send, up_recv)
+    ups = DirectGather(up, up_maps, local_sem.at[1], up_send, up_recv)
     sums = RingSum(part, pulled, held, passed, send_sem, recv_sem, out_send, out_recv)
     cots = CotangentRing(
         lambda step, d: cotangent if step == 0 else beside.at[d],
@@ -326,19 +371,11 @@
     tokens_copy = pltpu.make_async_copy(tokens, tokens_here, local_sem.at[3])
     tokens_copy.start()
     cots.launch(6)
-    ups.own_arrived()
-    ups.one()
-    ups.two(0)
-    ups.one_arrived()
     downs.own_arrived()
     downs.one()
-    ups.onward_arrived()
-    for di in NEAR:
-        ups.two_arrived(di)
     downs.two(0)
-    for di in NEAR:
-        ups.last_arrived(di)
-    ups.swaps_arrived()
+    ups.pass_across()
+    ups.arrived()
     cotangent_copy.wait()
 
     segments = places.shape[0]
@@ -362,9 +399,9 @@
     sums.step(1)
     cots.launch()
     downs.two_arrived(0)
+    sums.step(2)
+    cots.launch()
     downs.onward_arrived()
-    sums.step(2)
-    cots.launch()
     sums.step(3)
     cots.launch()
     downs.two_arrived(-1)
@@ -415,7 +452,8 @@
         scratch_shapes=[pltpu.VMEM((count,) + up.shape[1:], bf16), pltpu.VMEM(part, jnp.float32)]
         + ring_sum_scratch(part)
         + [dma((4,))]
-        + [dma((PlaneGather.copies,)) for _ in range(4)]
+        + [dma((PlaneGather.copies,)) for _ in range(2)]
+        + [dma((DirectGather.copies,)) for _ in range(2)]
         + [dma((2, 2, CotangentRing.eighths)), dma((2, 2, CotangentRing.eighths))],
         compiler_params=pltpu.CompilerParams(
             collective_id=0, has_side_effects=True, vmem_limit_bytes=12 * MIB
@@ -678,6 +716,93 @@
                         self.second(tau, d, j, e).wait_send()
 
 
+class DirectReduce:
+    def __init__(self, index, packed, entry, peer_entry, out, bufs, sems):
+        self.me, self.core, self.y, self.x = place_in_plane()
+        self.z = lax.axis_index("tsp")
+        self.peer = self.me + 1 - 2 * self.core
+        self.index, self.packed, self.entry, self.peer_entry = index, packed, entry, peer_entry
+        self.out = out
+        self.slots, self.peer_slots, self.terms, self.landed, self.res = bufs
+        self.send_sem, self.recv_sem = sems
+        self.waits = []
+
+    @staticmethod
+    def scratch(unit):
+        bf16 = jnp.bfloat16
+        dma = pltpu.SemaphoreType.DMA
+        chips = SIDE * SIDE
+        bufs = [
+            pltpu.VMEM((chips, 2) + unit, bf16),
+            pltpu.VMEM((chips, 2) + unit, bf16),
+            pltpu.VMEM((chips, 2, 2) + unit, bf16),
+            pltpu.VMEM((len(CHIPS), 2, 2) + unit, bf16),
+            pltpu.VMEM((2, 2) + unit, jnp.float32),
+        ]
+        return bufs, [dma((len(CHIPS) + 2,)), dma((len(CHIPS) + 2,))]
+
+    def copy(self, src, dst, device, k):
+        return remote(src, dst, self.send_sem.at[k], self.recv_sem.at[k], (device, self.z))
+
+    def go(self, copy):
+        copy.start()
+        self.waits.append(copy)
+
+    def share(self):
+        @pl.loop(0, SIDE * SIDE)
+        def _(q):
+            for tau in (0, 1):
+                self.slots[q, tau] = self.packed[self.index[2 * q + tau], 1 - self.core]
+
+        self.go(self.copy(self.slots, self.peer_slots, self.peer, len(CHIPS)))
+
+    def term(self, q, tau, e):
+        o = 2 * q + tau
+        a = self.packed[self.index[o], self.core].astype(jnp.float32)
+        b = self.peer_slots[q, tau].astype(jnp.float32)
+        return jnp.where(self.entry[pl.ds(o, 1), :] == e, a, 0.0) + jnp.where(
+            self.peer_entry[pl.ds(o, 1), :] == e, b, 0.0
+        )
+
+    def send_all(self):
+        self.copy(self.slots, self.peer_slots, self.peer, len(CHIPS)).wait_recv()
+
+        @pl.loop(0, SIDE * SIDE)
+        def _(q):
+            for tau in (0, 1):
+                for e in (0, 1):
+                    self.terms[q, tau, e] = self.term(q, tau, e).astype(self.terms.dtype)
+
+        for k, (dy, dx) in enumerate(CHIPS):
+            device = device_of(self.y + dy, self.x + dx, self.core)
+            self.go(self.copy(
+                self.terms.at[lax.div(device, 2)], self.landed.at[k], device, k
+            ))
+
+    def finish(self):
+        for k in range(len(CHIPS)):
+            self.copy(self.landed.at[k], self.landed.at[k], self.peer, k).wait_recv()
+        for tau in (0, 1):
+            for e in (0, 1):
+                value = self.term(lax.div(self.me, 2), tau, e)
+                for k in range(len(CHIPS)):
+                    value += self.landed[k, tau, e].astype(jnp.float32)
+                self.res[tau, e] = value
+        self.go(self.copy(
+            self.res.at[1 - self.core], self.out.at[:, self.core], self.peer, len(CHIPS) + 1
+        ))
+        self.out[:, self.core] = self.res[self.core]
+
+    def finished(self):
+        self.copy(
+            self.res.at[1 - self.core], self.out.at[:, 1 - self.core], self.peer, len(CHIPS) + 1
+        ).wait_recv()
+
+    def sent(self):
+        for copy in self.waits:
+            copy.wait_send()
+
+
 REDUCE_BUFS, REDUCE_SEMS, SUM_REFS = 12, 12, 6
 
 
@@ -694,11 +819,11 @@
     peer_entry, lowered, packed_up = take(3)
     sum_refs = take(SUM_REFS)
     down_bufs, down_sems = take(REDUCE_BUFS), take(REDUCE_SEMS)
-    up_bufs, up_sems = take(REDUCE_BUFS), take(REDUCE_SEMS)
+    up_bufs, up_sems = take(5), take(2)
     entry_send, entry_recv, cot_send, cot_recv = rest
     greet_neighbours()
     downs = PlaneReduce(index, packed, entry, peer_entry, out_down, down_bufs, down_sems)
-    ups = PlaneReduce(index, packed_up, entry, peer_entry, out_up, up_bufs, up_sems)
+    ups = DirectReduce(index, packed_up, entry, peer_entry, out_up, up_bufs, up_sems)
     sums = RingSum(part, lowered, *sum_refs)
     rows = cotangent.shape[0]
     cots = CotangentRing(
@@ -754,22 +879,15 @@
         packed_up[g] = scaled.reshape(packed_up.shape[1:])
 
     ups.share()
-    ups.send_first()
-    ups.send_second_free()
+    downs.send_third()
+    ups.send_all()
     cots.launch(4)
-    ups.keep()
-    for tau in (0, 1):
-        ups.send_second(tau)
-    downs.send_third()
-    ups.send_third()
-    ups.send_fourth_free()
     downs.send_fourth_free()
-    ups.send_fourth()
     downs.send_fourth()
+    downs.finish()
     ups.finish()
-    downs.finish()
+    downs.finished()
     ups.finished()
-    downs.finished()
     cots.arrived()
     entries.wait_send()
     for each in (downs, ups, sums, cots):
@@ -785,7 +903,7 @@
     whole = pl.BlockSpec(memory_space=pltpu.VMEM)
     anywhere = pl.BlockSpec(memory_space=pl.ANY)
     down_bufs, down_sems = PlaneReduce.scratch(down_unit)
-    up_bufs, up_sems = PlaneReduce.scratch(up_unit)
+    up_bufs, up_sems = DirectReduce.scratch(up_unit)
     return pl.pallas_call(
         scatter_kernel,
         out_shape=(

time: 125 us -> 118 us (0.944)
  Pallas kernels: 121 us -> 114 us
    pallas_call x1, Pallas kernels: 55.9 us -> 51.7 us  [gather_maps(): pl.pallas_call(gather_kernel, out_shape=(jax.ShapeDtypeStruct((count,) +...]
    pallas_call x1, Pallas kernels: 52.8 us -> 50.7 us  [scatter_gradients(): pl.pallas_call(scatter_kernel, out_shape=(jax.ShapeDtypeStruct((2, 2) + d...]
where the time goes in v5:
time: 118 us
  Pallas kernels  114 us (97%)
  local copies, waits for them, and re-layouts  2.16 us (2%)
    pallas_call x1, Pallas kernels, gather_maps(): pl.pallas_call(gather_kernel, out_shape=(jax.ShapeDtypeStruct((count,) +...  51.7 us
    pallas_call x1, Pallas kernels, scatter_gradients(): pl.pallas_call(scatter_kernel, out_shape=(jax.ShapeDtypeStruct((2, 2) + d...  50.7 us
    pallas_call x1, Pallas kernels, token_gradients(): pl.pallas_call(tokens_kernel, out_shape=jax.ShapeDtypeStruct((segments *...  9.04 us
    pallas_call x1, Pallas kernels, between(): pl.pallas_call(between_kernel, out_shape=(jax.ShapeDtypeStruct(pulled.sha...  2.8 us

profile of v5, /device:TPU:1, one launch (start us, length us, event | category | flops | bytes accessed | tf_op | source)
XLA Modules:
  0.0 118.2 jit_solution(1318387340199260786)
XLA Ops:
  0.6 0.0 copy-start.2
  0.6 0.9 select_reduce_fusion.3.places
  1.5 0.0 copy-start.1
  1.5 0.7 copy-done.1
  2.2 51.7 %gather_maps.1 = (bf16[64,2,32,1024]{3,2,1,0:T(8,128)(2,1)S(1)}, bf16[8,2,64,128]{3,2,1,0:T(8,128)(2,1)S(1)}, bf16[2048,1024]{1,0:T(8,128)(2,1)S(1)}, bf16[2048,...) custom-call(s32[16]{0:T(128)S(1)} %select_reduce_fusion.3.places, s32[16]{0:T(128)S(1)} %copy-done.1, ...), custom_call_target="tpu_custom_call" | custom-call | tf_op jit(solution)/shard_map/gather_maps/pallas_call | solution.py:441
  53.9 0.2 select_reduce_fusion.2.heads
  54.1 0.0 copy-done.2
  54.1 2.8 %between.1 = (f32[8,2,64,128]{3,2,1,0:T(8,128)S(1)}, bf16[16,2,32,1024]{3,2,1,0:T(8,128)(2,1)S(1)}) custom-call(s32[16]{0:T(128)S(1)} %select_reduce_fusion.3.places, s32[16]{0:T(128)S(1)} %copy-done.2, s32[16]{0:T(128)S(1)} %select_reduce_fusion.2.heads, bf16[2048,1024]{1,0:T(8,128)(2,1)S(1)} %get-tuple-element.15.tokens, ...), custom_call_target="tpu_custom_call" | custom-call | tf_op jit(solution)/shard_map/between/pallas_call | solution.py:499
  56.9 0.0 copy-start
  56.9 0.1 select_reduce_fusion
  57.0 0.1 broadcast_in_dim.68.entry
  57.1 50.7 %scatter_gradients.1 = (f32[2,2,32,1024]{3,2,1,0:T(8,128)S(1)}, f32[2,2,32,128]{3,2,1,0:T(8,128)S(1)}, bf16[3,2048,128]{2,1,0:T(8,128)(2,1)S(1)}) custom-call(s32[32]{0:T(128)S(1)} %get-tuple-element.24.index, s32[16]{0:T(128)S(1)} %get-tuple-element.25.owners, bf16[16,2,32,1024]{3,2,1,0:T(8,128)(2,1)S(1)} %get-tuple-element.18.packed, ...), custom_call_target="tpu_custom_call" | custom-call | tf_op jit(solution)/shard_map/scatter_gradients/pallas_call | solution.py:907
  107.8 0.0 copy-done
  107.8 9.0 %token_gradients.1 = bf16[2048,1024]{1,0:T(8,128)(2,1)} custom-call(s32[16]{0:T(128)S(1)} %select_reduce_fusion.3.places, s32[16]{0:T(128)S(1)} %copy-done.2, bf16[2048,128]{1,0:T(8,128)(2,1)S(1)} %get-tuple-element.13.cotangent, bf16[4,2048,128]{2,1,0:T(8,128)(2,1)S(1)} %get-tuple-element.14.beside, bf16[3,2048,128]{2,1,0:T(8,128)(2,1)S(1)} %get-tuple-element.20.beyond, ...), custom_call_target="tpu_custom_call" | custom-call | tf_op jit(solution)/shard_map/token_gradients/pallas_call | solution.py:992
  116.8 0.8 copy.13
  117.6 0.6 copy.14
  (2 shorter events, 0.0 us)
Async XLA Ops:
  0.6 53.4 %copy-start.2 = (s32[16]{0:T(128)S(1)}, s32[16]{0:T(128)}, u32[]{:S(2)}) copy-start(s32[16]{0:T(128)} %live.5) | copy-start | bytes 196
  1.5 0.7 copy-start.1
  56.9 50.9 %copy-start = (bf16[1024,1024]{1,0:T(8,128)(2,1)S(1)}, bf16[1024,1024]{1,0:T(8,128)(2,1)}, u32[]{:S(2)}) copy-start(bf16[1024,1024]{1,0:T(8,128)(2,1)} %frozen.1) | copy-start | bytes 6291460

commit v6 on v5

--- a/solution.py
+++ b/solution.py
@@ -44,7 +44,7 @@
 def greet_neighbours():
     me, core, y, x = place_in_plane()
     z = lax.axis_index("tsp")
-    devices = [(me + 1 - 2 * core, z), (me, ring(z + 1)), (me, ring(z - 1))]
+    devices = [(me + 1 - 2 * core, z)] + [(me, ring(z + k)) for k in range(1, RING)]
     devices += [(device_of(y + dy, x + dx, core), z) for dy, dx in CHIPS]
     barrier = pltpu.get_barrier_semaphore()
     for device in devices:
@@ -256,13 +256,6 @@
                 )
                 self.send(self.passed.at[d, step, u], d, step, u)
 
-    def pass_on(self, chunk, u, d, step):
-        ref = self.out.at[ring(chunk)] if u is None else self.out.at[ring(chunk), u]
-        return remote(
-            ref, ref, self.out_send.at[d, step], self.out_recv.at[d, step],
-            (self.me, ring(self.i + 1 - 2 * d)),
-        )
-
     def total(self):
         for u in (0, 1):
             for d in (0, 1):
@@ -270,22 +263,20 @@
             self.out[self.i, u] = (
                 self.part[self.i, u] + self.held[0, 3, u] + self.held[1, 3, u]
             ).astype(self.out.dtype)
-        for d in (0, 1):
-            copy = self.pass_on(self.i, None, d, 0)
+        for k in (4, 3, 5, 2, 6, 1, 7):
+            copy = self.across(self.i, k)
             copy.start()
             self.copies.append(copy)
 
-    def onward(self, step):
-        for d in (0, 1):
-            s = 1 - 2 * d
-            self.pass_on(self.i - step * s, None, d, step - 1).wait_recv()
-            copy = self.pass_on(self.i - step * s, d if step == 3 else None, d, step)
-            copy.start()
-            self.copies.append(copy)
+    def across(self, chunk, k):
+        ref = self.out.at[ring(chunk)]
+        return remote(
+            ref, ref, self.out_send.at[k], self.out_recv.at[k], (self.me, ring(self.i + k))
+        )
 
     def end(self):
-        for d in (0, 1):
-            self.pass_on(self.i + 4, d, d, 3).wait_recv()
+        for k in range(1, RING):
+            self.across(self.i - k, k).wait_recv()
 
     def sent(self):
         for copy in self.copies:
@@ -297,7 +288,7 @@
     shape = (2, 4, 2) + part[2:]
     return [
         pltpu.VMEM(shape, jnp.float32), pltpu.VMEM(shape, jnp.float32),
-        dma((2, 4, 2)), dma((2, 4, 2)), dma((2, 4)), dma((2, 4)),
+        dma((2, 4, 2)), dma((2, 4, 2)), dma((RING,)), dma((RING,)),
     ]
 
 
@@ -406,17 +397,13 @@
     cots.launch()
     downs.two_arrived(-1)
     sums.total()
-    cots.launch()
+    cots.launch(2)
     downs.two_arrived(1)
-    sums.onward(1)
-    cots.launch()
+    cots.launch(2)
     downs.two_arrived(2)
-    sums.onward(2)
-    cots.launch()
     downs.last_arrived(0)
+    cots.launch(2)
     downs.last_arrived(-1)
-    sums.onward(3)
-    cots.launch(3)
     downs.last_arrived(1)
     downs.last_arrived(2)
     sums.end()
@@ -807,7 +794,8 @@
 
 
 def scatter_kernel(
-    index, owners, packed, entry, part, cotangent, beside, out_down, out_up, beyond, *rest
+    index, owners, places, live, packed, entry, part, cotangent, beside, frozen, pulled, maps,
+    out_down, out_up, out_tokens, *rest
 ):
     rest = list(rest)
 
@@ -816,7 +804,7 @@
         del rest[:n]
         return taken
 
-    peer_entry, lowered, packed_up = take(3)
+    peer_entry, lowered, packed_up, beyond, weights = take(5)
     sum_refs = take(SUM_REFS)
     down_bufs, down_sems = take(REDUCE_BUFS), take(REDUCE_SEMS)
     up_bufs, up_sems = take(5), take(2)
@@ -846,16 +834,15 @@
     sums.step(3)
     cots.launch()
     sums.total()
-    cots.launch()
+    cots.launch(2)
     downs.send_second(0)
-    sums.onward(1)
-    cots.launch()
+    cots.launch(2)
     downs.send_second(1)
-    sums.onward(2)
-    cots.launch()
+    z, keys = lax.axis_index("tsp"), cotangent.shape[1]
+    for k, r in enumerate((0, -1, 1, -2, 2, -3, 3, 4)):
+        first = pl.multiple_of(ring(z + r) * keys, keys)
+        weights[:, k * keys : (k + 1) * keys] = frozen[:, pl.ds(first, keys)]
     downs.keep()
-    sums.onward(3)
-    cots.launch()
     sums.end()
 
     segments = owners.shape[0]
@@ -884,17 +871,47 @@
     cots.launch(4)
     downs.send_fourth_free()
     downs.send_fourth()
+    cots.arrived()
+
+    block, width = 2 * seg_rows, out_tokens.shape[1]
+    row = lax.broadcasted_iota(jnp.int32, (seg_rows, width), 0)
+    parts = [(beside, k) for k in range(4)] + [(beyond, k) for k in range(3)]
+
+    def token_block(b):
+        here = pl.ds(pl.multiple_of(b * block, block), block)
+        left = jnp.concatenate(
+            [cotangent[here, :]] + [ref[k, here, :] for ref, k in parts], axis=1
+        )
+        value = lax.dot_general(
+            left, weights[...], (((1,), (1,)), ((), ())), preferred_element_type=jnp.float32
+        )
+        both = pulled[b].reshape(seg_rows, 2 * ranks)
+        for k in (0, 1):
+            g = 2 * b + k
+            extra = jnp.dot(
+                both[:, k * ranks : (k + 1) * ranks], maps[places[g]].reshape(ranks, width),
+                preferred_element_type=jnp.float32,
+            )
+            total = value[k * seg_rows : (k + 1) * seg_rows] + ADAPTER_SCALE * extra
+            rows_here = pl.ds(pl.multiple_of(g * seg_rows, seg_rows), seg_rows)
+            out_tokens[rows_here, :] = jnp.where(row < live[g], total, 0.0).astype(
+                out_tokens.dtype
+            )
+
+    pl.loop(0, 5)(token_block)
     downs.finish()
     ups.finish()
+    pl.loop(5, segments // 2)(token_block)
     downs.finished()
     ups.finished()
-    cots.arrived()
     entries.wait_send()
     for each in (downs, ups, sums, cots):
         each.sent()
 
 
-def scatter_gradients(index, owners, packed, entry, part, cotangent, beside):
+def scatter_gradients(
+    index, owners, places, live, packed, entry, part, cotangent, beside, frozen, pulled, maps
+):
     down_unit = packed.shape[2:]
     up_unit = (HALF, cotangent.shape[1])
     bf16, f32 = jnp.bfloat16, jnp.float32
@@ -909,14 +926,16 @@
         out_shape=(
             jax.ShapeDtypeStruct((2, 2) + down_unit, f32),
             jax.ShapeDtypeStruct((2, 2) + up_unit, f32),
-            jax.ShapeDtypeStruct((3,) + beside.shape[1:], bf16),
+            jax.ShapeDtypeStruct((cotangent.shape[0], frozen.shape[0]), bf16),
         ),
-        in_specs=[scalars, scalars, whole, whole, whole, whole, anywhere],
-        out_specs=(whole, whole, anywhere),
+        in_specs=[scalars] * 4 + [whole] * 8,
+        out_specs=(whole, whole, whole),
         scratch_shapes=[
             pltpu.VMEM(entry.shape, f32),
             pltpu.VMEM(part.shape, bf16),
             pltpu.VMEM((packed.shape[0], 2) + up_unit, bf16),
+            pltpu.VMEM((3,) + beside.shape[1:], bf16),
+            pltpu.VMEM(frozen.shape, bf16),
         ]
         + ring_sum_scratch(part.shape)
         + down_bufs + down_sems + up_bufs + up_sems
@@ -925,82 +944,35 @@
             collective_id=1, has_side_effects=True, vmem_limit_bytes=30 * MIB
         ),
         name="scatter_gradients",
-    )(index, owners, packed, entry, part, cotangent, beside)
-
-
-def tokens_kernel(
-    places, live, cotangent, beside, beyond, frozen, pulled, maps, out, tiles, sems
-):
-    segments = places.shape[0]
-    width, keys = out.shape[1], cotangent.shape[1]
-    rows = out.shape[0] // segments
-    ranks = 2 * HALF
-    z = lax.axis_index("tsp")
-    block = tiles.shape[1]
-    steps = out.shape[0] // block
-    row = lax.broadcasted_iota(jnp.int32, (rows, width), 0)
-    offsets = (0, -1, 1, -2, 2, -3, 3, 4)
-    weights = jnp.concatenate(
-        [frozen[:, pl.ds(pl.multiple_of(ring(z + r) * keys, keys), keys)] for r in offsets],
-        axis=1,
-    )
-
-    def store(b):
-        return pltpu.make_async_copy(
-            tiles.at[lax.rem(b, 2)], out.at[pl.ds(b * block, block)], sems.at[lax.rem(b, 2)]
-        )
-
-    parts = (
-        (beside, 0), (beside, 1), (beside, 2), (beside, 3), (beyond, 0), (beyond, 1), (beyond, 2)
-    )
-
-    @pl.loop(0, steps)
-    def _(b):
-        @pl.when(b >= 2)
-        def _():
-            store(b - 2).wait()
-
-        here = pl.ds(pl.multiple_of(b * block, block), block)
-        left = jnp.concatenate(
-            [cotangent[here, :]] + [ref[k, here, :] for ref, k in parts], axis=1
-        )
-        value = lax.dot_general(
-            left, weights, (((1,), (1,)), ((), ())), preferred_element_type=jnp.float32
-        )
-        for k in range(2):
-            g = 2 * b + k
-            both = pulled[b].reshape(rows, 2 * ranks)
-            extra = jnp.dot(
-                both[:, k * ranks : (k + 1) * ranks], maps[places[g]].reshape(ranks, width),
-                preferred_element_type=jnp.float32,
-            )
-            total = value[k * rows : (k + 1) * rows] + ADAPTER_SCALE * extra
-            tiles[lax.rem(b, 2), k * rows : (k + 1) * rows] = jnp.where(
-                row < live[g], total, 0.0
-            ).astype(out.dtype)
-        store(b).start()
-
-    for b in (steps - 2, steps - 1):
-        store(b).wait()
-
-
-def token_gradients(places, live, cotangent, beside, beyond, frozen, pulled, maps):
-    segments = places.shape[0]
-    rows, width = cotangent.shape[0] // segments, frozen.shape[0]
-    scalars = pl.BlockSpec(memory_space=pltpu.SMEM)
-    whole = pl.BlockSpec(memory_space=pltpu.VMEM)
+    )(index, owners, places, live, packed, entry, part, cotangent, beside, frozen, pulled, maps)
+
+
+def store_kernel(a, b, c, out_a, out_b, out_c, sems):
+    pieces = 8
+    copies = [
+        pltpu.make_async_copy(b, out_b, sems.at[pieces]),
+        pltpu.make_async_copy(c, out_c, sems.at[pieces + 1]),
+    ]
+    rows = a.shape[0] // pieces
+    for k in range(pieces):
+        here = pl.ds(k * rows, rows)
+        copies.append(pltpu.make_async_copy(a.at[here], out_a.at[here], sems.at[k]))
+    for copy in copies:
+        copy.start()
+    for copy in copies:
+        copy.wait()
+
+
+def store(*arrays):
     return pl.pallas_call(
-        tokens_kernel,
-        out_shape=jax.ShapeDtypeStruct((segments * rows, width), jnp.bfloat16),
-        in_specs=[scalars, scalars] + [whole] * 6,
-        out_specs=pl.BlockSpec(memory_space=pl.ANY),
-        scratch_shapes=[
-            pltpu.VMEM((2, 2 * rows, width), jnp.bfloat16),
-            pltpu.SemaphoreType.DMA((2,)),
-        ],
-        compiler_params=pltpu.CompilerParams(vmem_limit_bytes=28 * MIB),
-        name="token_gradients",
-    )(places, live, cotangent, beside, beyond, frozen, pulled, maps)
+        store_kernel,
+        out_shape=tuple(jax.ShapeDtypeStruct(array.shape, array.dtype) for array in arrays),
+        in_specs=[pl.BlockSpec(memory_space=pltpu.VMEM)] * 3,
+        out_specs=(pl.BlockSpec(memory_space=pltpu.HBM),) * 3,
+        scratch_shapes=[pltpu.SemaphoreType.DMA((10,))],
+        compiler_params=pltpu.CompilerParams(vmem_limit_bytes=8 * MIB),
+        name="store",
+    )(*arrays)
 
 
 def on_device(
@@ -1034,17 +1006,16 @@
         far(tokens), far(cotangent),
     )
     part, packed = between(places, live, heads, tokens_here, maps, pulled)
-    down_grad, up_grad, beyond = scatter_gradients(
-        index, owners, packed, entry, part, cotangent_here, beside
+    down_grad, up_grad, token_gradient = scatter_gradients(
+        index, owners, places, live, packed, entry, part, cotangent_here, beside,
+        frozen_key_weight, pulled, maps,
     )
-    token_gradient = token_gradients(
-        places, live, cotangent_here, beside, beyond, frozen_key_weight, pulled, maps
-    )
-    return (
+    token_gradient, down_grad, up_grad = store(
         token_gradient,
         down_grad.reshape(held, ranks, width),
         up_grad.reshape(held, ranks, keys),
     )
+    return token_gradient, down_grad, up_grad
 
 
 def solution(mesh):

time: 118 us -> 108 us (0.915)
  Pallas kernels: 114 us -> 106 us
  local copies, waits for them, and re-layouts: 2.16 us -> 0.74 us
    pallas_call x1, Pallas kernels: 9.04 us -> 2.28 us  [store(): pl.pallas_call(store_kernel, out_shape=tuple((jax.ShapeDtypeStruct(array....]
    pallas_call x1, Pallas kernels: 50.7 us -> 47 us  [scatter_gradients(): pl.pallas_call(scatter_kernel, out_shape=(jax.ShapeDtypeStruct((2, 2) + d...]
    pallas_call x1, Pallas kernels: 51.7 us -> 53.6 us  [gather_maps(): pl.pallas_call(gather_kernel, out_shape=(jax.ShapeDtypeStruct((count,) +...]
    unnamed x8 -> x6, local copies, waits for them, and re-layouts: 2.09 us -> 0.67 us
where the time goes in v6:
time: 108 us
  Pallas kernels  106 us (98%)
  other arithmetic  1.15 us (1%)
    pallas_call x1, Pallas kernels, gather_maps(): pl.pallas_call(gather_kernel, out_shape=(jax.ShapeDtypeStruct((count,) +...  53.6 us
    pallas_call x1, Pallas kernels, scatter_gradients(): pl.pallas_call(scatter_kernel, out_shape=(jax.ShapeDtypeStruct((2, 2) + d...  47 us
    pallas_call x1, Pallas kernels, between(): pl.pallas_call(between_kernel, out_shape=(jax.ShapeDtypeStruct(pulled.sha...  2.76 us
    pallas_call x1, Pallas kernels, store(): pl.pallas_call(store_kernel, out_shape=tuple((jax.ShapeDtypeStruct(array....  2.28 us

profile of v6, /device:TPU:1, one launch (start us, length us, event | category | flops | bytes accessed | tf_op | source)
XLA Modules:
  0.0 108.2 jit_solution(5076652484803111761)
XLA Ops:
  0.6 0.0 copy-start.2
  0.6 0.9 select_reduce_fusion.3.places
  1.5 0.2 select_reduce_fusion.2.heads
  1.7 0.1 select_reduce_fusion
  1.8 0.1 broadcast_in_dim.68.entry
  1.9 0.0 copy-start.1
  1.9 0.7 copy-done.1
  2.5 53.6 %gather_maps.1 = (bf16[64,2,32,1024]{3,2,1,0:T(8,128)(2,1)S(1)}, bf16[8,2,64,128]{3,2,1,0:T(8,128)(2,1)S(1)}, bf16[2048,1024]{1,0:T(8,128)(2,1)S(1)}, bf16[2048,...) custom-call(s32[16]{0:T(128)S(1)} %select_reduce_fusion.3.places, s32[16]{0:T(128)S(1)} %copy-done.1, ...), custom_call_target="tpu_custom_call" | custom-call | tf_op jit(solution)/shard_map/gather_maps/pallas_call | solution.py:428
  56.1 0.0 copy-done.2
  56.1 0.0 copy-start
  56.1 2.8 %between.1 = (f32[8,2,64,128]{3,2,1,0:T(8,128)S(1)}, bf16[16,2,32,1024]{3,2,1,0:T(8,128)(2,1)S(1)}) custom-call(s32[16]{0:T(128)S(1)} %select_reduce_fusion.3.places, s32[16]{0:T(128)S(1)} %copy-done.2, s32[16]{0:T(128)S(1)} %select_reduce_fusion.2.heads, bf16[2048,1024]{1,0:T(8,128)(2,1)S(1)} %get-tuple-element.13.tokens, ...), custom_call_target="tpu_custom_call" | custom-call | tf_op jit(solution)/shard_map/between/pallas_call | solution.py:486
  58.9 0.0 copy-done
  58.9 47.0 %scatter_gradients.1 = (f32[2,2,32,1024]{3,2,1,0:T(8,128)S(1)}, f32[2,2,32,128]{3,2,1,0:T(8,128)S(1)}, bf16[2048,1024]{1,0:T(8,128)(2,1)S(1)}) custom-call(s32[32]{0:T(128)S(1)} %get-tuple-element.24.index, s32[16]{0:T(128)S(1)} %get-tuple-element.25.owners, s32[16]{0:T(128)S(1)} %select_reduce_fusion.3.places, s32[16]{0:T(128)S(1)} %copy-done.2, ...), custom_call_target="tpu_custom_call" | custom-call | tf_op jit(solution)/shard_map/scatter_gradients/pallas_call | solution.py:924
  105.9 2.3 %store.1 = (bf16[2048,1024]{1,0:T(8,128)(2,1)}, f32[2,64,1024]{2,1,0:T(8,128)}, f32[2,64,128]{2,1,0:T(8,128)}) custom-call(bf16[2048,1024]{1,0:T(8,128)(2,1)S(1)} %get-tuple-element.20.a, f32[2,64,1024]{2,1,0:T(8,128)S(1)} %bitcast.4, f32[2,64,128]{2,1,0:T(8,128)S(1)} %bitcast.5), custom_call_target="tpu_custom_call" | custom-call | tf_op jit(solution)/shard_map/store/pallas_call | solution.py:967
  (2 shorter events, 0.0 us)
Async XLA Ops:
  0.6 55.5 %copy-start.2 = (s32[16]{0:T(128)S(1)}, s32[16]{0:T(128)}, u32[]{:S(2)}) copy-start(s32[16]{0:T(128)} %live.5) | copy-start | bytes 196
  1.9 0.7 copy-start.1
  56.1 2.8 %copy-start = (bf16[1024,1024]{1,0:T(8,128)(2,1)S(1)}, bf16[1024,1024]{1,0:T(8,128)(2,1)}, u32[]{:S(2)}) copy-start(bf16[1024,1024]{1,0:T(8,128)(2,1)} %frozen.1) | copy-start | bytes 6291460

commit v7 on v6

--- a/solution.py
+++ b/solution.py
@@ -17,11 +17,6 @@
 )
 
 
-def lookup(idents, mapping):
-    matches = idents[:, None] == jnp.arange(mapping.shape[0], dtype=jnp.int32)[None, :]
-    return jnp.sum(jnp.where(matches, mapping[None, :], 0), axis=1)
-
-
 def place_in_plane():
     me = lax.axis_index("dp")
     core = lax.rem(me, 2)
@@ -236,19 +231,26 @@
         copy.start()
         self.copies.append(copy)
 
+    def halves(self, d):
+        return ((0, 1), (2, 3)) if d == 0 else ((2, 3), (0, 1))
+
     def begin(self):
-        for d in (0, 1):
-            self.send(self.part.at[ring(self.i + 4), d], d, 0, d)
-        for d in (0, 1):
-            s = 1 - 2 * d
-            self.send(self.part.at[ring(self.i + 3 * s), 1 - d], d, 1, 1 - d)
+        for k in (0, 1):
+            for d in (0, 1):
+                u = self.halves(d)[0][k]
+                self.send(self.part.at[ring(self.i + 4), u], d, 0, u)
+        for k in (0, 1):
+            for d in (0, 1):
+                u = self.halves(d)[1][k]
+                self.send(self.part.at[ring(self.i + 3 * (1 - 2 * d)), u], d, 1, u)
 
     def step(self, step):
-        for v in (0, 1):
+        for k in range(4):
             for d in (0, 1):
-                u = v if d == 0 else 1 - v
-                if step == 1 and v == 1:
+                own, other = self.halves(d)
+                if step == 1 and k >= 2:
                     continue
+                u = own[k] if step == 1 else (other + own)[k]
                 s = 1 - 2 * d
                 self.copy(self.held.at[d, step - 1, u], d, step - 1, u).wait_recv()
                 self.passed[d, step, u] = (
@@ -257,7 +259,7 @@
                 self.send(self.passed.at[d, step, u], d, step, u)
 
     def total(self):
-        for u in (0, 1):
+        for u in range(4):
             for d in (0, 1):
                 self.copy(self.held.at[d, 3, u], d, 3, u).wait_recv()
             self.out[self.i, u] = (
@@ -285,10 +287,10 @@
 
 def ring_sum_scratch(part):
     dma = pltpu.SemaphoreType.DMA
-    shape = (2, 4, 2) + part[2:]
+    shape = (2, 4, 4) + part[2:]
     return [
         pltpu.VMEM(shape, jnp.float32), pltpu.VMEM(shape, jnp.float32),
-        dma((2, 4, 2)), dma((2, 4, 2)), dma((RING,)), dma((RING,)),
+        dma((2, 4, 4)), dma((2, 4, 4)), dma((RING,)), dma((RING,)),
     ]
 
 
@@ -341,7 +343,7 @@
 
 
 def gather_kernel(
-    places, live, down, up, tokens, cotangent,
+    table, idents, live, down, up, tokens, cotangent,
     down_maps, pulled, tokens_here, cotangent_here, beside,
     up_maps, part, held, passed, send_sem, recv_sem, out_send, out_recv,
     local_sem, down_send, down_recv, up_send, up_recv, cot_send, cot_recv,
@@ -369,7 +371,7 @@
     ups.arrived()
     cotangent_copy.wait()
 
-    segments = places.shape[0]
+    segments = idents.shape[0]
     rows = cotangent.shape[0] // segments
     ranks, keys = 2 * HALF, cotangent.shape[1]
     row = lax.broadcasted_iota(jnp.int32, (rows, ranks), 0)
@@ -378,7 +380,7 @@
         for g in (2 * j, 2 * j + 1):
             term = lax.dot_general(
                 cotangent_here[g * rows : (g + 1) * rows, :],
-                up_maps[places[g]].reshape(ranks, keys),
+                up_maps[table[idents[g]]].reshape(ranks, keys),
                 (((1,), (1,)), ((), ())),
                 preferred_element_type=jnp.float32,
             )
@@ -414,11 +416,11 @@
         each.sent()
 
 
-def gather_maps(places, live, down, up, tokens, cotangent):
+def gather_maps(table, idents, live, down, up, tokens, cotangent):
     count = 2 * lax.axis_size("dp")
-    rows = cotangent.shape[0] // places.shape[0]
+    rows = cotangent.shape[0] // idents.shape[0]
     ranks = 2 * HALF
-    part = (places.shape[0] // 2, 2, rows // 2, 2 * ranks)
+    part = (idents.shape[0] // 2, 4, rows // 4, 2 * ranks)
     bf16 = jnp.bfloat16
     dma = pltpu.SemaphoreType.DMA
     scalars = pl.BlockSpec(memory_space=pltpu.SMEM)
@@ -434,7 +436,7 @@
             jax.ShapeDtypeStruct(cotangent.shape, bf16),
             jax.ShapeDtypeStruct((4,) + cotangent.shape, bf16),
         ),
-        in_specs=[scalars, scalars, far, far, far, far],
+        in_specs=[scalars, scalars, scalars, far, far, far, far],
         out_specs=(anywhere, whole, whole, whole, anywhere),
         scratch_shapes=[pltpu.VMEM((count,) + up.shape[1:], bf16), pltpu.VMEM(part, jnp.float32)]
         + ring_sum_scratch(part)
@@ -446,13 +448,35 @@
             collective_id=0, has_side_effects=True, vmem_limit_bytes=12 * MIB
         ),
         name="gather_maps",
-    )(places, live, down, up, tokens, cotangent)
-
-
-def between_kernel(places, live, heads, tokens, maps, pulled, part, packed, total):
-    segments = places.shape[0]
+    )(table, idents, live, down, up, tokens, cotangent)
+
+
+def between_kernel(
+    table, idents, live, tokens, maps, pulled, part, packed, places, before, index, entry, total
+):
+    segments = idents.shape[0]
     rows, width = tokens.shape[0] // segments, tokens.shape[1]
     ranks = 2 * HALF
+    @pl.loop(0, index.shape[0])
+    def _(o):
+        index[o] = -1
+
+    entry[...] = jnp.full_like(entry, -1.0)
+
+    @pl.loop(0, segments)
+    def _(g):
+        place = table[idents[g]]
+        owner = lax.div(place, 2)
+        places[g] = place
+        before[g] = index[owner]
+        index[owner] = g
+        held = lax.rem(place, 2).astype(jnp.float32)
+        entry[pl.ds(owner, 1), :] = jnp.full((1, entry.shape[1]), held, jnp.float32)
+
+    @pl.loop(0, index.shape[0])
+    def _(o):
+        index[o] = jnp.maximum(index[o], 0)
+
     row = lax.broadcasted_iota(jnp.int32, (rows, ranks), 0)
     for j in range(segments // 2):
         both = pulled[j].reshape(rows, 2 * ranks)
@@ -469,8 +493,10 @@
                 both[:, k * ranks : (k + 1) * ranks], tokens[here, :],
                 (((0,), (0,)), ((), ())), preferred_element_type=jnp.float32,
             )
-            h = heads[g]
-            total[h] = jnp.where(h == g, value, total[h] + value)
+            if g:
+                earlier = total[jnp.maximum(before[g], 0)]
+                value = value + jnp.where(before[g] >= 0, earlier, 0.0)
+            total[g] = value
         part[j] = jnp.concatenate(pair, axis=1).reshape(part.shape[1:])
 
     @pl.loop(0, segments)
@@ -479,8 +505,9 @@
         packed[g] = scaled.reshape(packed.shape[1:])
 
 
-def between(places, live, heads, tokens, maps, pulled):
-    segments, width = places.shape[0], tokens.shape[1]
+def between(table, idents, live, tokens, maps, pulled):
+    segments, width = idents.shape[0], tokens.shape[1]
+    owners = lax.axis_size("dp")
     scalars = pl.BlockSpec(memory_space=pltpu.SMEM)
     whole = pl.BlockSpec(memory_space=pltpu.VMEM)
     return pl.pallas_call(
@@ -488,13 +515,17 @@
         out_shape=(
             jax.ShapeDtypeStruct(pulled.shape, jnp.float32),
             jax.ShapeDtypeStruct((segments, 2, HALF, width), jnp.bfloat16),
+            jax.ShapeDtypeStruct((segments,), jnp.int32),
+            jax.ShapeDtypeStruct((segments,), jnp.int32),
+            jax.ShapeDtypeStruct((owners,), jnp.int32),
+            jax.ShapeDtypeStruct((owners, 128), jnp.float32),
         ),
         in_specs=[scalars] * 3 + [whole] * 3,
-        out_specs=(whole, whole),
+        out_specs=(whole, whole, scalars, scalars, scalars, whole),
         scratch_shapes=[pltpu.VMEM((segments, 2 * HALF, width), jnp.float32)],
         compiler_params=pltpu.CompilerParams(vmem_limit_bytes=24 * MIB),
         name="between",
-    )(places, live, heads, tokens, maps, pulled)
+    )(table, idents, live, tokens, maps, pulled)
 
 
 class PlaneReduce:
@@ -794,7 +825,7 @@
 
 
 def scatter_kernel(
-    index, owners, places, live, packed, entry, part, cotangent, beside, frozen, pulled, maps,
+    index, before, places, live, packed, entry, part, cotangent, beside, frozen, pulled, maps,
     out_down, out_up, out_tokens, *rest
 ):
     rest = list(rest)
@@ -804,7 +835,7 @@
         del rest[:n]
         return taken
 
-    peer_entry, lowered, packed_up, beyond, weights = take(5)
+    peer_entry, lowered, packed_up, beyond, weights, up_total = take(6)
     sum_refs = take(SUM_REFS)
     down_bufs, down_sems = take(REDUCE_BUFS), take(REDUCE_SEMS)
     up_bufs, up_sems = take(5), take(2)
@@ -845,24 +876,27 @@
     downs.keep()
     sums.end()
 
-    segments = owners.shape[0]
+    segments = before.shape[0]
     seg_rows, keys = rows // segments, cotangent.shape[1]
     ranks = 2 * HALF
-    values = []
     for g in range(segments):
         both = lowered[g // 2].reshape(seg_rows, 2 * ranks)
-        values.append(lax.dot_general(
+        value = lax.dot_general(
             both[:, (g % 2) * ranks : (g % 2 + 1) * ranks],
             cotangent[g * seg_rows : (g + 1) * seg_rows, :],
             (((0,), (0,)), ((), ())),
             preferred_element_type=jnp.float32,
-        ))
-    for g in range(segments):
-        value = values[g]
-        for h in range(segments):
-            if h != g:
-                value = value + jnp.where(owners[h] == owners[g], values[h], 0.0)
-        scaled = (value * (ADAPTER_SCALE / seg_rows)).astype(packed_up.dtype)
+        )
+        up_total[g] = value
+
+    @pl.loop(1, segments)
+    def _(g):
+        earlier = up_total[jnp.maximum(before[g], 0)]
+        up_total[g] = up_total[g] + jnp.where(before[g] >= 0, earlier, 0.0)
+
+    @pl.loop(0, segments)
+    def _(g):
+        scaled = (up_total[g] * (ADAPTER_SCALE / seg_rows)).astype(packed_up.dtype)
         packed_up[g] = scaled.reshape(packed_up.shape[1:])
 
     ups.share()
@@ -910,7 +944,7 @@
 
 
 def scatter_gradients(
-    index, owners, places, live, packed, entry, part, cotangent, beside, frozen, pulled, maps
+    index, before, places, live, packed, entry, part, cotangent, beside, frozen, pulled, maps
 ):
     down_unit = packed.shape[2:]
     up_unit = (HALF, cotangent.shape[1])
@@ -936,6 +970,7 @@
             pltpu.VMEM((packed.shape[0], 2) + up_unit, bf16),
             pltpu.VMEM((3,) + beside.shape[1:], bf16),
             pltpu.VMEM(frozen.shape, bf16),
+            pltpu.VMEM((packed.shape[0], 2 * HALF, cotangent.shape[1]), f32),
         ]
         + ring_sum_scratch(part.shape)
         + down_bufs + down_sems + up_bufs + up_sems
@@ -944,7 +979,7 @@
             collective_id=1, has_side_effects=True, vmem_limit_bytes=30 * MIB
         ),
         name="scatter_gradients",
-    )(index, owners, places, live, packed, entry, part, cotangent, beside, frozen, pulled, maps)
+    )(index, before, places, live, packed, entry, part, cotangent, beside, frozen, pulled, maps)
 
 
 def store_kernel(a, b, c, out_a, out_b, out_c, sems):
@@ -985,29 +1020,22 @@
     segment_adapter,
     segment_live_count,
 ):
-    dp_count = lax.axis_size("dp")
     held, ranks, width = adapter_down_weight.shape
     keys = cotangent.shape[1]
     live = segment_live_count
-    places = lookup(segment_adapter, adapter_place_table)
-    owners = places // held
-    segment = jnp.arange(places.shape[0], dtype=jnp.int32)
-    same = owners[:, None] == owners[None, :]
-    heads = jnp.min(jnp.where(same, segment[None, :], places.shape[0]), axis=1)
-    owner_hit = owners[:, None] == jnp.arange(dp_count, dtype=jnp.int32)[None, :]
-    wanted = jnp.max(jnp.where(owner_hit, (places % held)[:, None], -1), axis=0)
-    index = jnp.max(jnp.where(owner_hit, heads[:, None], 0), axis=0)
-    entry = jnp.broadcast_to(wanted.astype(jnp.float32)[:, None], (dp_count, 128))
     far = lambda array: pltpu.with_memory_space_constraint(array, pltpu.HBM)
+    small = [far(adapter_place_table), far(segment_adapter), far(live)]
     maps, pulled, tokens_here, cotangent_here, beside = gather_maps(
-        places, live,
+        *small,
         far(adapter_down_weight.reshape(held, 2, HALF, width)),
         far(adapter_up_weight.reshape(held, 2, HALF, keys)),
         far(tokens), far(cotangent),
     )
-    part, packed = between(places, live, heads, tokens_here, maps, pulled)
+    part, packed, places, before, index, entry = between(
+        adapter_place_table, segment_adapter, live, tokens_here, maps, pulled
+    )
     down_grad, up_grad, token_gradient = scatter_gradients(
-        index, owners, places, live, packed, entry, part, cotangent_here, beside,
+        index, before, places, live, packed, entry, part, cotangent_here, beside,
         frozen_key_weight, pulled, maps,
     )
     token_gradient, down_grad, up_grad = store(

time: 108 us -> 107 us (level)
  other arithmetic: 1.15 us -> 0 us
    pallas_call x1, Pallas kernels: 2.76 us -> 5.14 us  [between(): pl.pallas_call(between_kernel, out_shape=(jax.ShapeDtypeStruct(pulled.sha...]
where the time goes in v7:
time: 107 us
  Pallas kernels  107 us (100%)
    pallas_call x1, Pallas kernels, gather_maps(): pl.pallas_call(gather_kernel, out_shape=(jax.ShapeDtypeStruct((count,) +...  53.2 us
    pallas_call x1, Pallas kernels, scatter_gradients(): pl.pallas_call(scatter_kernel, out_shape=(jax.ShapeDtypeStruct((2, 2) + d...  46 us
    pallas_call x1, Pallas kernels, between(): pl.pallas_call(between_kernel, out_shape=(jax.ShapeDtypeStruct(pulled.sha...  5.14 us
    pallas_call x1, Pallas kernels, store(): pl.pallas_call(store_kernel, out_shape=tuple((jax.ShapeDtypeStruct(array....  2.28 us

profile of v7, /device:TPU:1, one launch (start us, length us, event | category | flops | bytes accessed | tf_op | source)
XLA Modules:
  0.0 107.4 jit_solution(17444408798821952020)
XLA Ops:
  0.6 0.0 copy-start.1
  0.6 0.0 copy-start.3
  0.7 0.0 copy-start.2
  0.7 53.2 %gather_maps.1 = (bf16[64,2,32,1024]{3,2,1,0:T(8,128)(2,1)S(1)}, bf16[8,4,32,128]{3,2,1,0:T(8,128)(2,1)S(1)}, bf16[2048,1024]{1,0:T(8,128)(2,1)S(1)}, bf16[2048,...) custom-call(s32[64]{0:T(128)} %table.3, s32[16]{0:T(128)} %idents.3, s32[16]{0:T(128)} %live.5, ...), custom_call_target="tpu_custom_call" | custom-call | tf_op jit(solution)/shard_map/gather_maps/pallas_call | solution.py:430
  53.9 0.0 copy-done.1
  53.9 0.0 copy-done.3
  53.9 0.0 copy-done.2
  53.9 0.0 copy-start
  53.9 5.1 %between.1 = (f32[8,4,32,128]{3,2,1,0:T(8,128)S(1)}, bf16[16,2,32,1024]{3,2,1,0:T(8,128)(2,1)S(1)}, s32[16]{0:T(128)S(1)}, s32[16]{0:T(128)S(1)}, s32[32]{0:T(128)S(1)}, /*index=5*/f32[32,128]{1,0:T(8,128)S(1)}) custom-call(s32[64]{0:T(128)S(1)} %copy-done.2, s32[16]{0:T(128)S(1)} %copy-done.3, s32[16]{0:T(128)S(1)} %copy-done.1, ...), custom_call_target="tpu_custom_call" | custom-call | tf_op jit(solution)/shard_map/between/pallas_call | solution.py:513
  59.1 0.0 copy-done
  59.1 46.0 %scatter_gradients.1 = (f32[2,2,32,1024]{3,2,1,0:T(8,128)S(1)}, f32[2,2,32,128]{3,2,1,0:T(8,128)S(1)}, bf16[2048,1024]{1,0:T(8,128)(2,1)S(1)}) custom-call(s32[32]{0:T(128)S(1)} %get-tuple-element.20.index, s32[16]{0:T(128)S(1)} %get-tuple-element.21.before, s32[16]{0:T(128)S(1)} %get-tuple-element.22.places, s32[16]{0:T(128)S(1)} %copy-done.1, ...), custom_call_target="tpu_custom_call" | custom-call | tf_op jit(solution)/shard_map/scatter_gradients/pallas_call | solution.py:958
  105.1 2.3 %store.1 = (bf16[2048,1024]{1,0:T(8,128)(2,1)}, f32[2,64,1024]{2,1,0:T(8,128)}, f32[2,64,128]{2,1,0:T(8,128)}) custom-call(bf16[2048,1024]{1,0:T(8,128)(2,1)S(1)} %get-tuple-element.28.a, f32[2,64,1024]{2,1,0:T(8,128)S(1)} %bitcast.4, f32[2,64,128]{2,1,0:T(8,128)S(1)} %bitcast.5), custom_call_target="tpu_custom_call" | custom-call | tf_op jit(solution)/shard_map/store/pallas_call | solution.py:1002
Async XLA Ops:
  0.6 53.2 %copy-start.1 = (s32[16]{0:T(128)S(1)}, s32[16]{0:T(128)}, u32[]{:S(2)}) copy-start(s32[16]{0:T(128)} %live.5) | copy-start | bytes 196
  0.6 53.2 %copy-start.3 = (s32[16]{0:T(128)S(1)}, s32[16]{0:T(128)}, u32[]{:S(2)}) copy-start(s32[16]{0:T(128)} %idents.3) | copy-start | bytes 196
  0.7 53.2 %copy-start.2 = (s32[64]{0:T(128)S(1)}, s32[64]{0:T(128)}, u32[]{:S(2)}) copy-start(s32[64]{0:T(128)} %table.3) | copy-start | bytes 772
  53.9 5.2 %copy-start = (bf16[1024,1024]{1,0:T(8,128)(2,1)S(1)}, bf16[1024,1024]{1,0:T(8,128)(2,1)}, u32[]{:S(2)}) copy-start(bf16[1024,1024]{1,0:T(8,128)(2,1)} %frozen.1) | copy-start | bytes 6291460
